TPU v7x, 128 devices: a whole 4x4x4 slice. The times are simulated.
128 devices in a mesh: dp: 8 (over y, core), seq: 16 (over z, x).
Axes of the slice: x: 4, y: 4, z: 4, core: 2. Of those that a mesh axis runs over, the one named last changes fastest.
Arguments:
- loader_rows: bfloat16 [8, 8192, 1152], P('dp', 'seq'), may hold values from -6 to 6
- lengths: int32 [8, 128], P('dp'), may hold values from 1 to 128, 8192 in all within a row
- block_order: int32 [8, 64], P('dp'), may hold values from 0 to 63, as said below
- norm_gain: float32 [1152], replicated, may hold values from 0.1 to 1.9
- qkv_weight: bfloat16 [1152, 3456], replicated, may hold values from -0.1875 to 0.1875
- upstream_grad: bfloat16 [8, 8192, 1152], P('dp', 'seq'), may hold values from -6 to 6
Outputs:
- attention: bfloat16 [8, 8192, 1152], P('dp', 'seq')
- loader_grad: bfloat16 [8, 8192, 1152], P('dp', 'seq')
- weight_grad: float32 [1152, 3456], P('seq')
- gain_grad: float32 [1152], P('seq')
Inputs may be any that keep to these rules, and one draw needn't show every extreme that they name: Images lie back to back in pack order; each pack's lengths sum to 8192. Each row of block_order is a permutation of the pack's 64 blocks. Of the blocks that one index of seq holds in pack order (blocks k * 4 onwards), no two come from the loader rows of the same index of seq, and no two loader blocks of one index of seq go to the same index.
All inputs are finite; a program needn't handle non-finite values.
Results may differ from a plain program's by a relative error of at most 0.015.
Values may be sent and summed in bfloat16 or wider, within the bound.
No kernel may reach another device: no remote copies, remote signals or barrier semaphores. Data moves between devices by JAX's collectives and lax.ppermute only.
A program may use at most 192 MiB of HBM per device.

v0:
```python
import jax
import jax.numpy as jnp
from jax import lax
from jax.sharding import PartitionSpec as P

HEADS = 16
BLK = 128
L_MAX = 128


epsilon = 1e-06
group_heads = 4


def padded(x, sides, width):
    for axis, dim in sides:
        peers, length = (lax.axis_size(axis), x.shape[dim])
        up = [(i, (i + 1) % peers) for i in range(peers - 1)]
        down = [(j, i) for i, j in up]
        last = lax.slice_in_dim(x, length - width, length, axis=dim)
        leading = lax.slice_in_dim(x, 0, width, axis=dim)
        before = lax.ppermute(last, axis, up)
        after = lax.ppermute(leading, axis, down)
        x = jnp.concatenate([before, x, after], axis=dim)
    return x


def passed_along(value, axis, steps):
    count = lax.axis_size(axis)
    leading, last = (max(0, -steps), min(count, count - steps))
    return lax.ppermute(value, axis, [(source, source + steps) for source in range(leading, last)])


def pick_rows(selector, blocks):
    return jnp.einsum("ab,brc->arc", selector, blocks, preferred_element_type=jnp.float32).astype(
        jnp.bfloat16
    )


def attend(operands, visible, score_scale):
    queries, key_cols, value_cols, upstream = operands
    scores = (
        jnp.einsum("hdi,hdj->hij", queries, key_cols, preferred_element_type=jnp.float32)
        * score_scale
    )
    weights = jnp.where(visible[None], jnp.exp(scores), 0.0)
    probabilities = weights / jnp.sum(weights, axis=2, keepdims=True)
    rounded = probabilities.astype(jnp.bfloat16)
    attended = jnp.einsum("hij,hdj->hdi", rounded, value_cols, preferred_element_type=jnp.float32)
    grad_probs = jnp.einsum(
        "hdi,hdj->hij", upstream, value_cols, preferred_element_type=jnp.float32
    )
    centred = jnp.sum(probabilities * grad_probs, axis=2, keepdims=True)
    grad_scores = (probabilities * (grad_probs - centred) * score_scale).astype(jnp.bfloat16)
    query_grad = jnp.einsum(
        "hij,hdj->hdi", grad_scores, key_cols, preferred_element_type=jnp.float32
    )
    key_grad = jnp.einsum("hij,hdi->hdj", grad_scores, queries, preferred_element_type=jnp.float32)
    value_grad = jnp.einsum("hij,hdi->hdj", rounded, upstream, preferred_element_type=jnp.float32)
    return (attended.astype(jnp.bfloat16), query_grad, key_grad, value_grad)


def project_columns(weight_cols, row_block):
    return lax.dot_general(
        weight_cols, row_block, (((0,), (1,)), ((), ())), preferred_element_type=jnp.float32
    ).astype(jnp.bfloat16)


def local(loader_rows, lengths, block_order, norm_gain, qkv_weight, upstream_grad):
    seq_count = lax.axis_size("seq")
    pack_count = lax.axis_size("dp")
    my_index = lax.axis_index("seq")
    row_count = loader_rows.shape[1]
    model_width = loader_rows.shape[2]
    head_dim = model_width // HEADS
    score_scale = head_dim ** (-0.5)
    per_device = row_count // BLK
    block_total = block_order.shape[1]
    order_row = block_order[0]
    inverse_order = (
        jnp.zeros((block_total,), jnp.int32)
        .at[order_row]
        .set(jnp.arange(block_total, dtype=jnp.int32))
    )
    own_blocks = my_index * per_device + jnp.arange(per_device, dtype=jnp.int32)
    target_device = inverse_order[own_blocks] // per_device
    source_device = order_row[own_blocks] // per_device
    devices = jnp.arange(seq_count, dtype=jnp.int32)
    send_select = (devices[:, None] == target_device[None, :]).astype(jnp.bfloat16)
    take_select = (source_device[:, None] == devices[None, :]).astype(jnp.bfloat16)
    outgoing = pick_rows(send_select, loader_rows[0].reshape(per_device, BLK, model_width))
    incoming = lax.all_to_all(outgoing, "seq", split_axis=0, concat_axis=0, tiled=True)
    pack_rows = pick_rows(take_select, incoming).reshape(row_count, model_width)
    values = pack_rows.astype(jnp.float32)
    centre = jnp.mean(values, axis=1, keepdims=True)
    spread = jnp.mean((values - centre) ** 2, axis=1, keepdims=True)
    inverse_std = lax.rsqrt(spread + epsilon)
    normed = (values - centre) * inverse_std
    scaled = (normed * norm_gain).astype(jnp.bfloat16)
    projected = project_columns(qkv_weight, scaled)
    keys_values = padded(projected[model_width:], (("seq", 1),), L_MAX)
    key_span = row_count + 2 * L_MAX
    image_ends = jnp.cumsum(lengths[0])
    positions = my_index * row_count - L_MAX + jnp.arange(key_span, dtype=jnp.int32)
    counted = jnp.sum((image_ends[None, :] <= positions[:, None]).astype(jnp.int32), axis=1)
    inside = (positions >= 0) & (positions < block_total * BLK)
    key_ids = jnp.where(inside, counted, -1)
    query_ids = key_ids[L_MAX : L_MAX + row_count]
    visible = query_ids[:, None] == key_ids[None, :]
    group_count = HEADS // group_heads
    query_part = projected[:model_width].reshape(group_count, group_heads, head_dim, row_count)
    key_part = keys_values[:model_width].reshape(group_count, group_heads, head_dim, key_span)
    value_part = keys_values[model_width:].reshape(group_count, group_heads, head_dim, key_span)
    upstream_part = upstream_grad[0].T.reshape(group_count, group_heads, head_dim, row_count)

    def per_group(operands):
        return attend(operands, visible, score_scale)

    attended, query_grad, key_grad, value_grad = lax.map(
        per_group, (query_part, key_part, value_part, upstream_part)
    )
    attention = attended.reshape(model_width, row_count).T.reshape(1, row_count, model_width)
    rim_grads = jnp.concatenate(
        [key_grad.reshape(model_width, key_span), value_grad.reshape(model_width, key_span)], axis=0
    )
    from_above = passed_along(rim_grads[:, :L_MAX].astype(jnp.bfloat16), "seq", -1).astype(
        jnp.float32
    )
    from_below = passed_along(
        rim_grads[:, L_MAX + row_count :].astype(jnp.bfloat16), "seq", 1
    ).astype(jnp.float32)
    own_grads = rim_grads[:, L_MAX : L_MAX + row_count]
    own_grads = own_grads.at[:, row_count - L_MAX :].add(from_above)
    own_grads = own_grads.at[:, :L_MAX].add(from_below)
    grad_cols = jnp.concatenate(
        [query_grad.reshape(model_width, row_count), own_grads], axis=0
    ).astype(jnp.bfloat16)
    weight_local = lax.dot_general(
        scaled, grad_cols, (((0,), (1,)), ((), ())), preferred_element_type=jnp.float32
    )
    input_grad = lax.dot_general(
        grad_cols, qkv_weight, (((0,), (1,)), ((), ())), preferred_element_type=jnp.float32
    )
    gain_local = jnp.sum(input_grad * normed, axis=0)
    pushed = input_grad * norm_gain
    row_grad = inverse_std * (
        pushed
        - jnp.mean(pushed, axis=1, keepdims=True)
        - normed * jnp.mean(pushed * normed, axis=1, keepdims=True)
    )
    returning = pick_rows(
        take_select.T, row_grad.astype(jnp.bfloat16).reshape(per_device, BLK, model_width)
    )
    returned = lax.all_to_all(returning, "seq", split_axis=0, concat_axis=0, tiled=True)
    loader_grad = pick_rows(send_select.T, returned).reshape(1, row_count, model_width)
    weight_share, gain_share = (
        lax.psum_scatter(
            weight_local.astype(jnp.bfloat16), "seq", scatter_dimension=0, tiled=True
        ).astype(jnp.float32),
        lax.psum_scatter(
            gain_local.astype(jnp.bfloat16), "seq", scatter_dimension=0, tiled=True
        ).astype(jnp.float32),
    )
    weight_share, gain_share = (
        lax.psum(weight_share.astype(jnp.bfloat16), "dp").astype(jnp.float32),
        lax.psum(gain_share.astype(jnp.bfloat16), "dp").astype(jnp.float32),
    )
    return (attention, loader_grad, weight_share / pack_count, gain_share / pack_count)


def solution(mesh):
    placed = (P("dp", "seq", None), P("dp", None), P("dp", None), P(), P(), P("dp", "seq", None))
    return jax.shard_map(
        local,
        mesh=mesh,
        in_specs=placed,
        out_specs=(P("dp", "seq", None), P("dp", "seq", None), P("seq", None), P("seq")),
        check_vma=False,
    )
```

profile of v0, /device:TPU:1, one launch (start us, length us, event | category | flops | bytes accessed | tf_op | source)
XLA Modules:
  0.0 610.9 jit_solution(7131820990850081415)
XLA Ops:
  9.9 2.2 convolution_convert_fusion.3
  12.2 3.3 copy.58
  15.4 8.6 %all-to-all-start = ((bf16[16,128,1152]{2,1,0:T(8,128)(2,1)}), bf16[16,128,1152]{2,1,0:T(8,128)(2,1)}, u32[]{:S(2)}, u32[]{:S(2)}) async-start(bf16[16,128,1152]{2,1,0:T(8,128)(2,1)} %copy.58), calls=%async_computation | async-start | bytes 9437184 | tf_op jit(solution)/shard_map/all_to_all | solution.py:92
  24.7 69.3 %all-to-all-done = bf16[16,128,1152]{2,1,0:T(8,128)(2,1)} async-done(((bf16[16,128,1152]{2,1,0:T(8,128)(2,1)}), bf16[16,128,1152]{2,1,0:T(8,128)(2,1)}, u32[]{:S(2)}, u32[]{:S(2)}) %all-to-all-start) | async-done | bytes 4718624 | tf_op jit(solution)/shard_map/all_to_all | solution.py:92
  94.0 5.3 fusion.124
  101.4 8.9 %fusion.82 = bf16[3456,512]{0,1:T(8,128)(2,1)S(1)} fusion(bf16[512,1152]{1,0:T(8,128)(2,1)S(1)} %multiply_convert_fusion.2, bf16[1152,3456]{1,0:T(8,128)(2,1)} %param.16), kind=kOutput, calls=%fused_computation.65 | convolution fusion | flops 4078632960 | bytes 12681216 | tf_op jit(solution)/shard_map/dot_general | solution.py:64
  112.4 2.1 collective-permute-start
  120.9 4.3 collective-permute-done
  125.2 4.6 collective-permute-done.1
  133.2 2.6 copy.64
  135.9 3.9 copy.66
  139.7 219.4 %while.19 = (s32[]{:T(128)}, bf16[4,4,72,512]{3,2,1,0:T(8,128)(2,1)}, bf16[4,4,72,512]{3,2,1,0:T(8,128)(2,1)}, f32[4,4,72,768]{3,2,1,0:T(8,128)}, f32[4,4,72,768...) while((s32[]{:T(128)}, ...), condition=%wide.region_8.9_spmd.clone, body=%wide.region_5.8_spmd.clone.sunk | while | flops 1411403264 | bytes 84315256 | solution.py:119
  140.2 5.4 fusion.155
  145.6 4.7 fusion.157
  150.3 17.1 %fusion.159 = f32[4,4,72,768]{3,2,1,0:T(8,128)} fusion(f32[4,4,72,768]{3,2,1,0:T(8,128)} %get-tuple-element.264, s32[]{:T(128)} %get-tuple-element.261, f32[4,512,768]{2,1,0:T(8,128)} %fusion.157, bf16[4,4,72,512]{3,2,1,0:T(8,128)(2,1)} %get-tuple-element.279, f32[4,512,768]{2,1,0:T(8,128)} %get-tuple-element.247, ...), kind=kOutput, calls=%fused_computation.22.clone.1 | convolution fusion | flops 243796736 | bytes 27149312 | tf_op jit(solution)/shard_map/while/body/eval_jaxpr/hij,hdi->hdj/dot_general | solution.py:58
  167.4 5.6 fusion.160
  173.0 16.5 %fusion.158 = bf16[4,4,72,512]{3,2,1,0:T(8,128)(2,1)} fusion(bf16[4,4,72,512]{3,2,1,0:T(8,128)(2,1)} %get-tuple-element.263, s32[]{:T(128)} %get-tuple-element.261, f32[4,512,768]{2,1,0:T(8,128)} %fusion.157, bf16[4,4,72,768]{3,2,1,0:T(8,128)(2,1)} %get-tuple-element.280, f32[4,512,768]{2,1,0:T(8,128)} %get-tuple-element.247, ...), kind=kOutput, calls=%fused_computation.24.clone.1 | convolution fusion | flops 243796736 | bytes 27001856 | tf_op jit(solution)/shard_map/while/body/eval_jaxpr/hij,hdj->hdi/dot_general | solution.py:55
  189.5 5.2 fusion.156
  195.0 5.4 fusion.155
  200.4 4.7 fusion.157
  205.1 17.1 %fusion.159 = f32[4,4,72,768]{3,2,1,0:T(8,128)} fusion(f32[4,4,72,768]{3,2,1,0:T(8,128)} %get-tuple-element.264, s32[]{:T(128)} %get-tuple-element.261, f32[4,512,768]{2,1,0:T(8,128)} %fusion.157, bf16[4,4,72,512]{3,2,1,0:T(8,128)(2,1)} %get-tuple-element.279, f32[4,512,768]{2,1,0:T(8,128)} %get-tuple-element.247, ...), kind=kOutput, calls=%fused_computation.22.clone.1 | convolution fusion | flops 243796736 | bytes 27149312 | tf_op jit(solution)/shard_map/while/body/eval_jaxpr/hij,hdi->hdj/dot_general | solution.py:58
  222.1 5.6 fusion.160
  227.7 16.5 %fusion.158 = bf16[4,4,72,512]{3,2,1,0:T(8,128)(2,1)} fusion(bf16[4,4,72,512]{3,2,1,0:T(8,128)(2,1)} %get-tuple-element.263, s32[]{:T(128)} %get-tuple-element.261, f32[4,512,768]{2,1,0:T(8,128)} %fusion.157, bf16[4,4,72,768]{3,2,1,0:T(8,128)(2,1)} %get-tuple-element.280, f32[4,512,768]{2,1,0:T(8,128)} %get-tuple-element.247, ...), kind=kOutput, calls=%fused_computation.24.clone.1 | convolution fusion | flops 243796736 | bytes 27001856 | tf_op jit(solution)/shard_map/while/body/eval_jaxpr/hij,hdj->hdi/dot_general | solution.py:55
  244.2 5.2 fusion.156
  249.7 5.4 fusion.155
  255.1 4.7 fusion.157
  259.8 17.1 %fusion.159 = f32[4,4,72,768]{3,2,1,0:T(8,128)} fusion(f32[4,4,72,768]{3,2,1,0:T(8,128)} %get-tuple-element.264, s32[]{:T(128)} %get-tuple-element.261, f32[4,512,768]{2,1,0:T(8,128)} %fusion.157, bf16[4,4,72,512]{3,2,1,0:T(8,128)(2,1)} %get-tuple-element.279, f32[4,512,768]{2,1,0:T(8,128)} %get-tuple-element.247, ...), kind=kOutput, calls=%fused_computation.22.clone.1 | convolution fusion | flops 243796736 | bytes 27149312 | tf_op jit(solution)/shard_map/while/body/eval_jaxpr/hij,hdi->hdj/dot_general | solution.py:58
  276.9 5.7 fusion.160
  282.5 16.5 %fusion.158 = bf16[4,4,72,512]{3,2,1,0:T(8,128)(2,1)} fusion(bf16[4,4,72,512]{3,2,1,0:T(8,128)(2,1)} %get-tuple-element.263, s32[]{:T(128)} %get-tuple-element.261, f32[4,512,768]{2,1,0:T(8,128)} %fusion.157, bf16[4,4,72,768]{3,2,1,0:T(8,128)(2,1)} %get-tuple-element.280, f32[4,512,768]{2,1,0:T(8,128)} %get-tuple-element.247, ...), kind=kOutput, calls=%fused_computation.24.clone.1 | convolution fusion | flops 243796736 | bytes 27001856 | tf_op jit(solution)/shard_map/while/body/eval_jaxpr/hij,hdj->hdi/dot_general | solution.py:55
  299.0 5.2 fusion.156
  304.5 5.4 fusion.155
  309.9 4.7 fusion.157
  314.6 17.1 %fusion.159 = f32[4,4,72,768]{3,2,1,0:T(8,128)} fusion(f32[4,4,72,768]{3,2,1,0:T(8,128)} %get-tuple-element.264, s32[]{:T(128)} %get-tuple-element.261, f32[4,512,768]{2,1,0:T(8,128)} %fusion.157, bf16[4,4,72,512]{3,2,1,0:T(8,128)(2,1)} %get-tuple-element.279, f32[4,512,768]{2,1,0:T(8,128)} %get-tuple-element.247, ...), kind=kOutput, calls=%fused_computation.22.clone.1 | convolution fusion | flops 243796736 | bytes 27149312 | tf_op jit(solution)/shard_map/while/body/eval_jaxpr/hij,hdi->hdj/dot_general | solution.py:58
  331.7 5.6 fusion.160
  337.3 16.5 %fusion.158 = bf16[4,4,72,512]{3,2,1,0:T(8,128)(2,1)} fusion(bf16[4,4,72,512]{3,2,1,0:T(8,128)(2,1)} %get-tuple-element.263, s32[]{:T(128)} %get-tuple-element.261, f32[4,512,768]{2,1,0:T(8,128)} %fusion.157, bf16[4,4,72,768]{3,2,1,0:T(8,128)(2,1)} %get-tuple-element.280, f32[4,512,768]{2,1,0:T(8,128)} %get-tuple-element.247, ...), kind=kOutput, calls=%fused_computation.24.clone.1 | convolution fusion | flops 243796736 | bytes 27001856 | tf_op jit(solution)/shard_map/while/body/eval_jaxpr/hij,hdj->hdi/dot_general | solution.py:55
  353.8 5.2 fusion.156
  359.2 3.6 fusion.81
  364.9 4.0 collective-permute-start.3
  369.6 7.6 %collective-permute-done.2 = bf16[2304,128]{1,0:T(8,128)(2,1)S(1)} collective-permute-done((bf16[2304,128]{1,0:T(8,128)(2,1)S(1)}, bf16[2304,128]{1,0:T(8,128)(2,1)S(1)}, u32[]{:S(2)}, u32[]{:S(2)}) %collective-permute-start.2) | collective-permute-done | bytes 589856 | tf_op jit(solution)/shard_map/ppermute | solution.py:31
  382.2 7.7 %convolution_convert_fusion = bf16[1152,3456]{1,0:T(8,128)(2,1)} fusion(bf16[512,1152]{1,0:T(8,128)(2,1)S(1)} %copy-done.12, bf16[2304,512]{1,0:T(8,128)(2,1)S(1)} %convert.14, bf16[1152,512]{1,0:T(8,128)(2,1)S(1)} %bitcast.145), kind=kOutput, calls=%fused_computation.57 | convolution fusion | flops 4087922688 | bytes 12681216 | tf_op jit(solution)/shard_map/dot_general | solution.py:138
  391.6 10.2 %multiply_reduce_fusion.1 = (bf16[1152]{0:T(1024)(128)(2,1)}, f32[512]{0:T(512)S(1)}, f32[512]{0:T(512)S(1)}, f32[512,1152]{1,0:T(8,128)S(1)}) fusion(f32[4,128,1152]{2,1,0:T(8,128)S(1)} %copy-done.6, f32[512]{0:T(512)S(1)} %bitcast.141, f32[512]{0:T(512)S(1)} %bitcast.138, f32[1152]{0:T(1024)S(1)} %copy-done.14, bf16[1152,3456]{1,0:T(8,128)(2,1)} %param.16, ...), kind=kOutput, calls=%fused_computation.80 | convolution fusion | flops 4088657920 | bytes 16235264 | tf_op jit(solution)/shard_map/dot_general | solution.py:141
  402.5 2.2 convolution_convert_fusion.2
  404.8 3.2 copy.70
  408.0 11.1 %all-to-all-start.1 = ((bf16[16,128,1152]{2,1,0:T(8,128)(2,1)}), bf16[16,128,1152]{2,1,0:T(8,128)(2,1)}, u32[]{:S(2)}, u32[]{:S(2)}) async-start(bf16[16,128,1152]{2,1,0:T(8,128)(2,1)} %copy.70), calls=%async_computation.1 | async-start | bytes 9437184 | tf_op jit(solution)/shard_map/all_to_all | solution.py:154
  421.8 95.7 %all-reduce.1 = bf16[1152]{0:T(1024)(128)(2,1)S(1)} all-reduce(bf16[1152]{0:T(1024)(128)(2,1)S(1)} %copy-done.19), channel_id=3, replica_groups=mesh['dp'=8,'seq'=16] {'seq'}, use_global_device_ids=true, to_apply=%region_15.16.clone | all-reduce | flops 1152 | bytes 4608
  517.6 24.7 %psum.15 = bf16[72]{0:T(256)(128)(2,1)S(1)} all-reduce(bf16[72]{0:T(256)(128)(2,1)S(1)} %dynamic-slice.19), channel_id=1, replica_groups=mesh['dp'=8,'seq'=16] {'dp'}, use_global_device_ids=true, to_apply=%region_16.17 | all-reduce | flops 72 | bytes 288 | tf_op jit(solution)/shard_map/psum | solution.py:166
  542.9 5.3 fusion.91
  549.3 52.3 %all-reduce.4.cloned.1.call-done = bf16[72,3456]{1,0:T(8,128)(2,1)} async-done(((bf16[72,3456]{1,0:T(8,128)(2,1)}), bf16[72,3456]{1,0:T(8,128)(2,1)}) %all-reduce.4.cloned.1.call-update) | async-done | bytes 497680 | tf_op jit(solution)/shard_map/psum | solution.py:165
  (117 shorter events, 34.3 us)
Async XLA Ops:
  7.2 2.2 copy-start
  9.4 0.5 copy-start.20
  15.4 8.7 %copy-start.2 = (s32[1,64]{1,0:T(1,128)S(1)}, s32[1,64]{1,0:T(1,128)}, u32[]{:S(2)}) copy-start(s32[1,64]{1,0:T(1,128)} %param.14) | copy-start | bytes 772
  15.4 78.6 %all-to-all-start = ((bf16[16,128,1152]{2,1,0:T(8,128)(2,1)}), bf16[16,128,1152]{2,1,0:T(8,128)(2,1)}, u32[]{:S(2)}, u32[]{:S(2)}) async-start(bf16[16,128,1152]{2,1,0:T(8,128)(2,1)} %copy.58), calls=%async_computation | async-start | bytes 9437184 | tf_op jit(solution)/shard_map/all_to_all | solution.py:92
  24.0 518.8 %reduce-scatter.4.cloned.1.call-start = ((), (), s32[]{:S(2)}) async-start(), calls=%async_computation.4 | async-start | bytes 8460288
  24.7 74.6 %copy-start.22 = (s32[4]{0:T(128)}, s32[4]{0:T(128)S(1)}, u32[]{:S(2)}) copy-start(s32[4]{0:T(128)S(1)} %and_select_fusion.2) | copy-start | bytes 52
  99.4 1.7 copy-start.13
  99.5 10.8 %copy-start.5 = (f32[4,128,1152]{2,1,0:T(8,128)}, f32[4,128,1152]{2,1,0:T(8,128)S(1)}, u32[]{:S(2)}) copy-start(f32[4,128,1152]{2,1,0:T(8,128)S(1)} %copy.60) | copy-start | bytes 7077892
  100.3 0.6 copy-start.15
  100.5 0.5 copy-start.17
  101.4 8.9 %copy-start.11 = (bf16[512,1152]{1,0:T(8,128)(2,1)}, bf16[512,1152]{1,0:T(8,128)(2,1)S(1)}, u32[]{:S(2)}) copy-start(bf16[512,1152]{1,0:T(8,128)(2,1)S(1)} %multiply_convert_fusion.2) | copy-start | bytes 3538948
  101.4 14.5 %copy-start.24 = (s32[1,128]{1,0:T(1,128)S(1)}, s32[1,128]{1,0:T(1,128)}, u32[]{:S(2)}) copy-start(s32[1,128]{1,0:T(1,128)} %param.13) | copy-start | bytes 1540
  101.4 15.2 %copy-start.9 = (bf16[1,512,1152]{2,1,0:T(8,128)(2,1)S(1)}, bf16[1,512,1152]{2,1,0:T(8,128)(2,1)}, u32[]{:S(2)}) copy-start(bf16[1,512,1152]{2,1,0:T(8,128)(2,1)} %param.17) | copy-start | bytes 3538948
  110.3 2.1 copy-start.7
  112.4 12.8 %collective-permute-start = (bf16[2304,128]{0,1:T(8,128)(2,1)}, bf16[2304,128]{0,1:T(8,128)(2,1)}, u32[]{:S(2)}, u32[]{:S(2)}) collective-permute-start(bf16[2304,128]{0,1:T(8,128)(2,1)} %get-tuple-element.171), channel_id=1, source_target_pairs={{0,1},{1,2},{2,3},{3,4},{4,5},{5,6},{6,7},{7,8},{8,9},{9,10},{10,1... | collective-permute-start | bytes 1769480 | tf_op jit(solution)/shard_map/ppermute | solution.py:22
  114.5 15.3 %collective-permute-start.1 = (bf16[2304,128]{0,1:T(8,128)(2,1)}, bf16[2304,128]{0,1:T(8,128)(2,1)}, u32[]{:S(2)}, u32[]{:S(2)}) collective-permute-start(bf16[2304,128]{0,1:T(8,128)(2,1)} %get-tuple-element.172), channel_id=1, source_target_pairs={{1,0},{2,1},{3,2},{4,3},{5,4},{6,5},{7,6},{8,7},{9,8},{10,9},{11,1... | collective-permute-start | bytes 1769480 | tf_op jit(solution)/shard_map/ppermute | solution.py:23
  118.1 1.3 slice-start.1
  118.1 11.8 %slice-start = ((bf16[3456,512]{0,1:T(8,128)(2,1)}), bf16[2304,512]{0,1:T(8,128)(2,1)S(1)}, s32[]{:S(2)}) async-start(bf16[3456,512]{0,1:T(8,128)(2,1)} %copy-done.7), calls=%async_computation.5 | async-start | bytes 4718592 | tf_op jit(solution)/shard_map/slice | solution.py:101
  359.2 9.8 %copy-start.3 = (f32[4,4,72,768]{3,2,1,0:T(8,128)S(1)}, f32[4,4,72,768]{3,2,1,0:T(8,128)}, u32[]{:S(2)}) copy-start(f32[4,4,72,768]{3,2,1,0:T(8,128)} %get-tuple-element.85) | copy-start | bytes 10616836
  359.2 9.8 %copy-start.4 = (f32[4,4,72,768]{3,2,1,0:T(8,128)S(1)}, f32[4,4,72,768]{3,2,1,0:T(8,128)}, u32[]{:S(2)}) copy-start(f32[4,4,72,768]{3,2,1,0:T(8,128)} %get-tuple-element.86) | copy-start | bytes 10616836
  362.9 14.3 %collective-permute-start.2 = (bf16[2304,128]{1,0:T(8,128)(2,1)S(1)}, bf16[2304,128]{1,0:T(8,128)(2,1)S(1)}, u32[]{:S(2)}, u32[]{:S(2)}) collective-permute-start(bf16[2304,128]{1,0:T(8,128)(2,1)S(1)} %get-tuple-element.168), channel_id=1, source_target_pairs={{1,0},{2,1},{3,2},{4,3},{5,4},{6,5},{7,6},{8,7},{9,8},{10,9},{11,1... | collective-permute-start | bytes 1769480 | tf_op jit(solution)/shard_map/ppermute | solution.py:31
  364.9 13.7 %collective-permute-start.3 = (bf16[2304,128]{1,0:T(8,128)(2,1)S(1)}, bf16[2304,128]{1,0:T(8,128)(2,1)S(1)}, u32[]{:S(2)}, u32[]{:S(2)}) collective-permute-start(bf16[2304,128]{1,0:T(8,128)(2,1)S(1)} %get-tuple-element.167), channel_id=1, source_target_pairs={{0,1},{1,2},{2,3},{3,4},{4,5},{5,6},{6,7},{7,8},{8,9},{9,10},{10,1... | collective-permute-start | bytes 1769480 | tf_op jit(solution)/shard_map/ppermute | solution.py:31
  379.7 1.8 copy-start.12
  379.7 2.5 copy-start.25
  380.0 1.5 copy-start.8
  389.9 1.7 copy-start.6
  389.9 1.7 copy-start.14
  389.9 1.7 copy-start.16
  389.9 1.7 copy-start.18
  401.8 0.7 copy-start.23
  407.9 11.2 %copy-start.26 = (u32[128]{0:T(128)S(1)}, u32[128]{0:T(128)}, u32[]{:S(2)}) copy-start(u32[128]{0:T(128)} %constant.148) | copy-start | bytes 1540
  408.0 12.4 %copy-start.10 = (bf16[4,4,72,512]{3,2,1,0:T(8,128)(2,1)S(1)}, bf16[4,4,72,512]{3,2,1,0:T(8,128)(2,1)}, u32[]{:S(2)}) copy-start(bf16[4,4,72,512]{3,2,1,0:T(8,128)(2,1)} %get-tuple-element.83) | copy-start | bytes 3538948
  408.0 13.8 %copy-start.19 = (bf16[1152]{0:T(1024)(128)(2,1)S(1)}, bf16[1152]{0:T(1024)(128)(2,1)}, u32[]{:S(2)}) copy-start(bf16[1152]{0:T(1024)(128)(2,1)} %get-tuple-element.140) | copy-start | bytes 6916
  408.0 134.9 %copy-start.21 = (s32[4]{0:T(128)S(1)}, s32[4]{0:T(128)}, u32[]{:S(2)}) copy-start(s32[4]{0:T(128)} %copy-done.20) | copy-start | bytes 52
  408.0 134.9 %all-to-all-start.1 = ((bf16[16,128,1152]{2,1,0:T(8,128)(2,1)}), bf16[16,128,1152]{2,1,0:T(8,128)(2,1)}, u32[]{:S(2)}, u32[]{:S(2)}) async-start(bf16[16,128,1152]{2,1,0:T(8,128)(2,1)} %copy.70), calls=%async_computation.1 | async-start | bytes 9437184 | tf_op jit(solution)/shard_map/all_to_all | solution.py:154
  419.1 182.5 %all-reduce.4.cloned.1.call-start = ((), (), s32[]{:S(2)}) async-start(), calls=%async_computation.3 | async-start | bytes 995328 | tf_op jit(solution)/shard_map/psum | solution.py:165
  542.9 60.8 %copy-start.1 = (bf16[1,512,1152]{2,1,0:T(8,128)(2,1)S(1)}, bf16[1,512,1152]{2,1,0:T(8,128)(2,1)}, u32[]{:S(2)}) copy-start(bf16[1,512,1152]{2,1,0:T(8,128)(2,1)} %param.12) | copy-start | bytes 3538948
Sparse Core Ops, SparseCore 0:
  390.1 150.2 reduce-scatter.3
  543.0 58.5 all-reduce.3
where the time goes:
time: 621 us; the launch traced here: 611 us
  matrix products  260 us (42%)
  waiting for transfers between devices  139 us (22%)
  blocking collectives  120 us (19%)
  local copies, waits for them, and re-layouts  32 us (5%)
  starting transfers between devices  28.6 us (5%)
  between operations  15.6 us (3%)
  other arithmetic  14.6 us (2%)
    unnamed x1, blocking collectives  95.7 us
    all_to_all x1, waiting for transfers between devices, local(): lax.all_to_all(outgoing, 'seq', split_axis=0, concat_axis=0, tiled=True)  69.3 us
    dot_general x4, matrix products, attend(): jnp.einsum('hij,hdi->hdj', grad_scores, queries, preferred_element_type=j...  68.3 us
    dot_general x4, matrix products, attend(): jnp.einsum('hij,hdj->hdi', grad_scores, key_cols, preferred_element_type=...  65.9 us
    psum x1, waiting for transfers between devices, local(): lax.psum(weight_share.astype(jnp.bfloat16), 'dp').astype(jnp.float32)  52.3 us
    psum x1, blocking collectives, local(): lax.psum(gain_share.astype(jnp.bfloat16), 'dp').astype(jnp.float32)  24.7 us
    dot_general x4, matrix products, attend(): jnp.einsum('hij,hdi->hdj', rounded, upstream, preferred_element_type=jnp....  22.5 us
    dot_general x4, matrix products, attend(): jnp.einsum('hdi,hdj->hij', queries, key_cols, preferred_element_type=jnp....  21.7 us
  transfers between devices with their start and end apart: 8, of which 6 were waited for; matrix products, arithmetic and copies ran while one was open for 5% of the time, Pallas kernels for 0%

commit v1 on v0

v1 whole, which is shorter than its diff:
```python
import functools

import jax
import jax.numpy as jnp
from jax import lax
from jax.experimental import pallas as pl
from jax.experimental.pallas import tpu as pltpu
from jax.sharding import Mesh
from jax.sharding import PartitionSpec as P

HEADS = 16
HD = 72
BLK = 128
PAIR = 2 * HD
BF16 = jnp.bfloat16
F32 = jnp.float32
EPSILON = 1e-06
SCORE_SCALE = HD ** (-0.5)
HIDDEN_BIAS = -1e30
DP = ("y", "core")
SEQ = ("z", "x")


def nn(a, b):
    return lax.dot_general(a, b, (((1,), (0,)), ((), ())), preferred_element_type=F32)


def nt(a, b):
    return lax.dot_general(a, b, (((1,), (1,)), ((), ())), preferred_element_type=F32)


def attention_kernel(
    col_ref, row_ref, q_ref, k_ref, v_ref, qh_ref, kh_ref, vh_ref, g_ref, gh_ref,
    o_ref, dq_ref, dk_ref, dv_ref, bias_ref, o_s, dq_s, dk_s, dv_s,
):
    blocks = q_ref.shape[1] // BLK
    rows = q_ref.shape[1]

    @pl.when(pl.program_id(0) == 0)
    def _():
        for b in range(blocks + 2):
            first, last = max(b - 1, 0), min(b + 1, blocks + 1)
            same = col_ref[b * BLK : (b + 1) * BLK, :] == row_ref[:, first * BLK : (last + 1) * BLK]
            bias_ref[b, :, : (last + 1 - first) * BLK] = jnp.where(same, 0.0, HIDDEN_BIAS)

    for head in range(2):
        lo, hi = head * HD, (head + 1) * HD

        def whole(own, halo):
            mid, rim = own[...].astype(F32)[lo:hi], halo[...].astype(F32)[lo:hi]
            return jnp.concatenate([rim[:, :BLK], mid, rim[:, BLK:]], axis=1)

        q32, g32 = whole(q_ref, qh_ref), whole(g_ref, gh_ref)
        q, g = q32.astype(BF16), g32.astype(BF16)
        k, v = whole(k_ref, kh_ref).astype(BF16), whole(v_ref, vh_ref).astype(BF16)
        dk_s[lo:hi, :] = jnp.zeros((HD, rows), F32)
        dv_s[lo:hi, :] = jnp.zeros((HD, rows), F32)
        for b in range(blocks + 2):
            first, last = max(b - 1, 0), min(b + 1, blocks + 1)
            width = (last + 1 - first) * BLK
            k_win = k[:, first * BLK : (last + 1) * BLK]
            v_win = v[:, first * BLK : (last + 1) * BLK]
            here = slice(b * BLK, (b + 1) * BLK)
            scores = nn(q32[:, here].T.astype(BF16), k_win)
            grad_probs = nn(g32[:, here].T.astype(BF16), v_win)
            weights = jnp.exp(scores * SCORE_SCALE + bias_ref[b, :, :width])
            probs = weights * (1.0 / jnp.sum(weights, axis=1, keepdims=True))
            rounded = probs.astype(BF16)
            centred = jnp.sum(probs * grad_probs, axis=1, keepdims=True)
            grad_scores = (probs * (grad_probs - centred) * SCORE_SCALE).astype(BF16)
            if 1 <= b <= blocks:
                own = slice((b - 1) * BLK, b * BLK)
                o_s[lo:hi, own] = nt(v_win, rounded)
                dq_s[lo:hi, own] = nt(k_win, grad_scores)
            k0, k1 = max(first, 1), min(last, blocks)
            seen = slice((k0 - first) * BLK, (k1 + 1 - first) * BLK)
            into = slice((k0 - 1) * BLK, k1 * BLK)
            dk_s[lo:hi, into] += nn(q[:, here], grad_scores[:, seen])
            dv_s[lo:hi, into] += nn(g[:, here], rounded[:, seen])
    o_ref[...] = o_s[...].astype(BF16)
    dq_ref[...] = dq_s[...].astype(BF16)
    dk_ref[...] = dk_s[...].astype(BF16)
    dv_ref[...] = dv_s[...].astype(BF16)


def attention_call(ids, own, halo, g_own, g_halo, first_pair=0, pairs=HEADS // 2):
    rows, rim = own.shape[1], halo.shape[1]
    total, blocks = rows + rim, rows // BLK
    per_part = HEADS // 2

    def spec(width, part):
        return pl.BlockSpec((PAIR, width), lambda i: (part * per_part + first_pair + i, 0))

    out = pl.BlockSpec((PAIR, rows), lambda i: (i, 0))
    shape = jax.ShapeDtypeStruct((pairs * PAIR, rows), BF16)
    return pl.pallas_call(
        attention_kernel,
        grid=(pairs,),
        in_specs=[
            pl.BlockSpec((total, 1), lambda i: (0, 0)),
            pl.BlockSpec((1, total), lambda i: (0, 0)),
            spec(rows, 0), spec(rows, 1), spec(rows, 2),
            spec(rim, 0), spec(rim, 1), spec(rim, 2),
            spec(rows, 0), spec(rim, 0),
        ],
        out_specs=[out] * 4,
        out_shape=[shape] * 4,
        scratch_shapes=[pltpu.VMEM((blocks + 2, BLK, 3 * BLK), F32)]
        + [pltpu.VMEM((PAIR, rows), F32)] * 4,
        cost_estimate=pl.CostEstimate(
            flops=pairs * 2 * 16 * 12 * BLK * BLK * HD,
            bytes_accessed=pairs * PAIR * (rows * 8 + rim * 4) * 2,
            transcendentals=pairs * 2 * 16 * BLK * BLK,
        ),
        name="packed_attention",
    )(ids[:, None], ids[None, :], own, own, own, halo, halo, halo, g_own, g_halo)


def pick_kernel(index_ref, source_ref, out_ref):
    out_ref[...] = source_ref[...]


def pick(index, source):
    count, (_, rows, width) = index.shape[0], source.shape
    return pl.pallas_call(
        pick_kernel,
        grid_spec=pltpu.PrefetchScalarGridSpec(
            num_scalar_prefetch=1,
            grid=(count,),
            in_specs=[pl.BlockSpec((1, rows, width), lambda i, index: (index[i], 0, 0))],
            out_specs=pl.BlockSpec((1, rows, width), lambda i, index: (i, 0, 0)),
        ),
        out_shape=jax.ShapeDtypeStruct((count, rows, width), source.dtype),
        cost_estimate=pl.CostEstimate(
            flops=0, bytes_accessed=4 * count * rows * width, transcendentals=0
        ),
        name="pick_blocks",
    )(index, source)


def local(loader_rows, lengths, block_order, norm_gain, qkv_weight, upstream_grad):
    seq_count = lax.axis_size(SEQ)
    pack_count = lax.axis_size(DP)
    my_index = lax.axis_index(SEQ)
    _, row_count, model_width = loader_rows.shape
    per_device = row_count // BLK
    order_row = block_order[0]
    block_total = order_row.shape[0]
    devices = jnp.arange(seq_count, dtype=jnp.int32)
    slots = jnp.arange(per_device, dtype=jnp.int32)
    places = jnp.arange(block_total, dtype=jnp.int32)
    own_blocks = my_index * per_device + slots
    found = order_row[None, :] == own_blocks[:, None]
    target_device = jnp.sum(jnp.where(found, places[None, :], 0), axis=1) // per_device
    source_device = lax.dynamic_slice_in_dim(order_row, my_index * per_device, per_device) // per_device
    send_index = jnp.sum(jnp.where(devices[:, None] == target_device[None, :], slots[None, :], 0), axis=1)
    return_index = jnp.sum(jnp.where(devices[:, None] == source_device[None, :], slots[None, :], 0), axis=1)

    upstream = upstream_grad[0]
    up = [(i, i + 1) for i in range(seq_count - 1)]
    down = [(i + 1, i) for i in range(seq_count - 1)]

    def halo(x):
        before = lax.ppermute(x[row_count - BLK :], SEQ, up)
        after = lax.ppermute(x[:BLK], SEQ, down)
        return jnp.concatenate([before, after], axis=0)

    upstream_own = upstream.T
    upstream_halo = halo(upstream).T

    values = loader_rows[0].astype(F32)
    centre = jnp.mean(values, axis=1, keepdims=True)
    spread = jnp.mean((values - centre) ** 2, axis=1, keepdims=True)
    inverse_std = lax.rsqrt(spread + EPSILON)
    normed = (values - centre) * inverse_std
    scaled_loader = (normed * norm_gain).astype(BF16)

    outgoing = pick(send_index, scaled_loader.reshape(per_device, BLK, model_width))
    incoming = lax.all_to_all(outgoing, SEQ, split_axis=0, concat_axis=0, tiled=True)
    scaled = pick(source_device, incoming).reshape(row_count, model_width)
    scaled_halo = halo(scaled)

    def project(rows):
        return lax.dot_general(
            qkv_weight, rows, (((0,), (1,)), ((), ())), preferred_element_type=F32
        ).astype(BF16)

    qkv_own = project(scaled)
    qkv_halo = project(scaled_halo)
    image_ends = jnp.cumsum(lengths[0])
    positions = my_index * row_count - BLK + jnp.arange(row_count + 2 * BLK, dtype=jnp.int32)
    counted = jnp.sum((image_ends[None, :] <= positions[:, None]).astype(jnp.int32), axis=1)
    inside = (positions >= 0) & (positions < block_total * BLK)
    ids = jnp.where(inside, counted, -1)

    attended, query_grad, key_grad, value_grad = attention_call(
        ids, qkv_own, qkv_halo, upstream_own, upstream_halo
    )
    attention = attended.T[None]
    grad_cols = jnp.concatenate([query_grad, key_grad, value_grad], axis=0)
    weight_local = lax.dot_general(
        scaled, grad_cols, (((0,), (1,)), ((), ())), preferred_element_type=F32
    ).astype(BF16)
    input_grad = lax.dot_general(
        grad_cols, qkv_weight, (((0,), (1,)), ((), ())), preferred_element_type=F32
    ).astype(BF16)
    returning = pick(return_index, input_grad.reshape(per_device, BLK, model_width))
    returned = lax.all_to_all(returning, SEQ, split_axis=0, concat_axis=0, tiled=True)
    grads = pick(target_device, returned).reshape(row_count, model_width).astype(F32)
    pushed = grads * norm_gain
    row_grad = inverse_std * (
        pushed
        - jnp.mean(pushed, axis=1, keepdims=True)
        - normed * jnp.mean(pushed * normed, axis=1, keepdims=True)
    )
    loader_grad = row_grad.astype(BF16)[None]
    weight_share = lax.psum_scatter(weight_local, SEQ, scatter_dimension=0, tiled=True)
    weight_grad = lax.psum(weight_share, DP).astype(F32) / pack_count
    share = weight_grad.shape[0]
    weight_rows = lax.dynamic_slice_in_dim(qkv_weight, my_index * share, share, 0).astype(F32)
    gain_rows = lax.dynamic_slice_in_dim(norm_gain, my_index * share, share, 0)
    gain_grad = jnp.sum(weight_rows * weight_grad, axis=1) / gain_rows
    return (attention, loader_grad, weight_grad, gain_grad)


def solution(mesh):
    fine = Mesh(mesh.devices.reshape(4, 2, 4, 4), DP + SEQ)
    rows = P(DP, SEQ, None)
    return jax.shard_map(
        local,
        mesh=fine,
        in_specs=(rows, P(DP, None), P(DP, None), P(), P(), rows),
        out_specs=(rows, rows, P(SEQ, None), P(SEQ)),
        check_vma=False,
    )
```

time: 621 us -> 409 us (0.66); the launches traced: 611 us -> 406 us
  matrix products: 260 us -> 32 us
  blocking collectives: 120 us -> 0 us
  waiting for transfers between devices: 139 us -> 221 us
  Pallas kernels: 0 us -> 68.8 us
  local copies, waits for them, and re-layouts: 32 us -> 13.2 us
  other arithmetic: 14.6 us -> 27 us
    dot_general x29 -> x2, matrix products: 242 us -> 15.1 us  [project(): lax.dot_general(qkv_weight, rows, (((0,), (1,)), ((), ())), preferred_ele...]
    unnamed x1 -> x0, blocking collectives: 95.7 us -> none
    pallas_call x0 -> x5, Pallas kernels: none -> 68.8 us  [the longest x1 42 us: attention_call(): pl.pallas_call(attention_kernel, grid=(pairs,), in_specs=[pl.BlockSpec((t...]
    ppermute x4, waiting for transfers between devices: 17.9 us -> 57.5 us  [the longest x2 50.4 us: halo(): before = lax.ppermute(x[row_count - BLK:], SEQ, up)]
    psum x1 -> x0, blocking collectives: 24.7 us -> none  [local(): lax.psum(gain_share.astype(jnp.bfloat16), 'dp').astype(jnp.float32)]
    unnamed x3, waiting for transfers between devices: 0.04 us -> 24.2 us
    all_to_all x2, waiting for transfers between devices: 69.3 us -> 81.6 us  [the longest x1 81.6 us: local(): lax.all_to_all(returning, SEQ, split_axis=0, concat_axis=0, tiled=True)]
    slice x11 -> x2, local copies, waits for them, and re-layouts: 12.6 us -> 3.16 us  [halo(): before = lax.ppermute(x[row_count - BLK:], SEQ, up)]
  transfers between devices with their start and end apart: 8 -> 8, of which waited for: 6 -> 5; matrix products, arithmetic and copies ran while one was open for 5% -> 11% of each run, Pallas kernels for 0% -> 3%
where the time goes in v1:
time: 409 us; the launch traced here: 406 us
  waiting for transfers between devices  221 us (54%)
  Pallas kernels  68.8 us (17%)
  matrix products  32 us (8%)
  starting transfers between devices  29.7 us (7%)
  other arithmetic  27 us (7%)
  between operations  14.2 us (3%)
  local copies, waits for them, and re-layouts  13.2 us (3%)
    all_to_all x1, waiting for transfers between devices, local(): lax.all_to_all(returning, SEQ, split_axis=0, concat_axis=0, tiled=True)  81.6 us
    psum x1, waiting for transfers between devices, local(): weight_grad = lax.psum(weight_share, DP).astype(F32) / pack_count  57.9 us
    ppermute x2, waiting for transfers between devices, halo(): before = lax.ppermute(x[row_count - BLK:], SEQ, up)  50.4 us
    pallas_call x1, Pallas kernels, attention_call(): pl.pallas_call(attention_kernel, grid=(pairs,), in_specs=[pl.BlockSpec((t...  42 us
    pallas_call x4, Pallas kernels, pick(): pl.pallas_call(pick_kernel, grid_spec=pltpu.PrefetchScalarGridSpec(num_sc...  26.8 us
    unnamed x3, waiting for transfers between devices  24.2 us
    dot_general x2, matrix products, project(): lax.dot_general(qkv_weight, rows, (((0,), (1,)), ((), ())), preferred_ele...  15.1 us
    all_to_all x1, starting transfers between devices, local(): lax.all_to_all(returning, SEQ, split_axis=0, concat_axis=0, tiled=True)  12.7 us
  transfers between devices with their start and end apart: 8, of which 5 were waited for; matrix products, arithmetic and copies ran while one was open for 11% of the time, Pallas kernels for 3%

profile of v1, /device:TPU:1, one launch (start us, length us, event | category | flops | bytes accessed | tf_op | source)
XLA Modules:
  0.0 406.0 jit_solution(2501050117702516957)
XLA Ops:
  7.2 0.9 select_reduce_fusion.2
  8.2 0.6 select_reduce_fusion.1.index_ref
  8.7 1.5 convert_reduce_fusion
  10.3 1.7 fusion.7
  12.0 0.6 add_rsqrt_fusion
  12.6 1.5 multiply_convert_fusion
  14.0 9.5 %pick_blocks.4 = bf16[16,128,1152]{2,1,0:T(8,128)(2,1)} custom-call(s32[16]{0:T(128)} %select_reduce_fusion.1.index_ref, bf16[4,128,1152]{2,1,0:T(8,128)(2,1)} %get-tuple-element.32.source_ref), custom_call_target="tpu_custom_call" | custom-call | bytes 9437184 | tf_op jit(solution)/shard_map/pick_blocks/pallas_call | solution.py:125
  23.6 9.0 %all-to-all-start = ((bf16[16,128,1152]{2,1,0:T(8,128)(2,1)}), bf16[16,128,1152]{2,1,0:T(8,128)(2,1)}, u32[]{:S(2)}, u32[]{:S(2)}) async-start(bf16[16,128,1152]{2,1,0:T(8,128)(2,1)} %pick_blocks.4), calls=%async_computation | async-start | bytes 9437184 | tf_op jit(solution)/shard_map/all_to_all | solution.py:179
  32.6 2.4 copy.37
  35.0 1.9 slice_bitcast_fusion.1
  36.9 3.9 collective-permute-start.2
  40.8 1.3 collective-permute-start.3
  42.1 1.4 copy.33
  43.5 1.6 reduce-window.8
  45.1 1.5 reduce.3
  46.6 0.9 convert_reduce_fusion.1
  47.5 1.2 and_select_fusion.3.index_ref
  48.8 0.6 and_select_fusion.row_ref
  49.3 0.9 reshape_select_fusion.col_ref
  50.3 50.4 %collective-permute-done.2 = bf16[128,1152]{0,1:T(8,128)(2,1)} collective-permute-done((bf16[128,1152]{0,1:T(8,128)(2,1)}, bf16[128,1152]{0,1:T(8,128)(2,1)}, u32[]{:S(2)}, u32[]{:S(2)}) %collective-permute-start.2) | collective-permute-done | bytes 294944 | tf_op jit(solution)/shard_map/ppermute | solution.py:164
  100.6 7.1 %collective-permute-done.3 = bf16[128,1152]{0,1:T(8,128)(2,1)} collective-permute-done((bf16[128,1152]{0,1:T(8,128)(2,1)}, bf16[128,1152]{0,1:T(8,128)(2,1)}, u32[]{:S(2)}, u32[]{:S(2)}) %collective-permute-start.3) | collective-permute-done | bytes 294944 | tf_op jit(solution)/shard_map/ppermute | solution.py:165
  107.7 1.9 maximum_bitcast_fusion.gh_ref
  109.6 4.1 %pick_blocks.5 = bf16[4,128,1152]{2,1,0:T(8,128)(2,1)} custom-call(s32[4]{0:T(128)} %and_select_fusion.3.index_ref, bf16[16,128,1152]{2,1,0:T(8,128)(2,1)} %all-to-all-done.source_ref), custom_call_target="tpu_custom_call" | custom-call | bytes 2359296 | tf_op jit(solution)/shard_map/pick_blocks/pallas_call | solution.py:125
  113.7 1.2 slice_bitcast_fusion.3
  115.0 1.4 collective-permute-start
  116.4 1.3 collective-permute-start.1
  117.8 10.3 %fusion.q_ref.k_ref.v_ref = bf16[3456,512]{1,0:T(8,128)(2,1)} fusion(bf16[512,1152]{1,0:T(8,128)(2,1)} %bitcast.72, bf16[1152,3456]{1,0:T(8,128)(2,1)} %param.10), kind=kOutput, calls=%fused_computation.2 | convolution fusion | flops 4078632960 | bytes 12681216 | tf_op jit(solution)/shard_map/dot_general | solution.py:184
  128.1 4.8 %fusion.1.qh_ref.kh_ref.vh_ref = bf16[3456,256]{1,0:T(8,128)(2,1)} fusion(bf16[1152,3456]{1,0:T(8,128)(2,1)S(1)} %bitcast.77, bf16[128,1152]{1,0:T(8,128)(2,1)S(1)} %collective-permute-done.1, bf16[128,1152]{1,0:T(8,128)(2,1)S(1)} %collective-permute-done), kind=kOutput, calls=%fused_computation.4 | convolution fusion | flops 2040496128 | bytes 10321920 | tf_op jit(solution)/shard_map/dot_general | solution.py:184
  132.9 42.0 %packed_attention.1 = (bf16[1152,512]{1,0:T(8,128)(2,1)}, bf16[1152,512]{1,0:T(8,128)(2,1)}, bf16[1152,512]{1,0:T(8,128)(2,1)}, bf16[1152,512]{1,0:T(8,128)(2,1)}) custom-call(s32[768,1]{1,0:T(8,128)} %reshape_select_fusion.col_ref, s32[1,768]{1,0:T(1,128)} %and_select_fusion.row_ref, bf16[3456,512]{1,0:T(8,128)(2,1)} %fusion.q_ref.k_ref.v_ref, ...), custom_call_target="tpu_custom_call" | custom-call | flops 3623878656 | bytes 11796480 | tf_op jit(solution)/shard_map/packed_attention/pallas_call | solution.py:96
  174.9 1.5 constant_dynamic-update-slice_fusion.2
  176.6 0.3 copy-done.3
  176.9 1.9 copy-done.5
  178.8 6.6 %convolution_convert_fusion = bf16[1152,3456]{1,0:T(8,128)(2,1)} fusion(bf16[512,1152]{1,0:T(8,128)(2,1)S(1)} %bitcast.73, bf16[3456,512]{1,0:T(8,128)(2,1)S(1)} %constant_dynamic-update-slice_fusion), kind=kOutput, calls=%fused_computation | convolution fusion | flops 4080844800 | bytes 12681216 | tf_op jit(solution)/shard_map/dot_general | solution.py:201
  185.5 0.7 fusion.14
  186.2 0.6 select_reduce_fusion.index_ref
  186.8 10.3 %convolution_convert_fusion.3 = bf16[512,1152]{1,0:T(8,128)(2,1)} fusion(bf16[3456,512]{1,0:T(8,128)(2,1)} %copy-done.5, bf16[1152,3456]{1,0:T(8,128)(2,1)} %param.10), kind=kOutput, calls=%fused_computation.5 | convolution fusion | flops 4077453312 | bytes 12681216 | tf_op jit(solution)/shard_map/dot_general | solution.py:204
  197.1 9.1 %pick_blocks.6 = bf16[16,128,1152]{2,1,0:T(8,128)(2,1)} custom-call(s32[16]{0:T(128)} %select_reduce_fusion.index_ref, bf16[4,128,1152]{2,1,0:T(8,128)(2,1)} %bitcast.75), custom_call_target="tpu_custom_call" | custom-call | bytes 9437184 | tf_op jit(solution)/shard_map/pick_blocks/pallas_call | solution.py:125
  206.1 12.7 %all-to-all-start.1 = ((bf16[16,128,1152]{2,1,0:T(8,128)(2,1)}), bf16[16,128,1152]{2,1,0:T(8,128)(2,1)}, u32[]{:S(2)}, u32[]{:S(2)}) async-start(bf16[16,128,1152]{2,1,0:T(8,128)(2,1)} %pick_blocks.6), calls=%async_computation.1 | async-start | bytes 9437184 | tf_op jit(solution)/shard_map/all_to_all | solution.py:208
  218.9 2.4 copy.40
  221.2 81.6 %all-to-all-done.1.source_ref = bf16[16,128,1152]{2,1,0:T(8,128)(2,1)} async-done(((bf16[16,128,1152]{2,1,0:T(8,128)(2,1)}), bf16[16,128,1152]{2,1,0:T(8,128)(2,1)}, u32[]{:S(2)}, u32[]{:S(2)}) %all-to-all-start.1) | async-done | bytes 4718624 | tf_op jit(solution)/shard_map/all_to_all | solution.py:208
  302.9 4.1 %pick_blocks.7 = bf16[4,128,1152]{2,1,0:T(8,128)(2,1)} custom-call(s32[4]{0:T(128)} %copy-done.8, bf16[16,128,1152]{2,1,0:T(8,128)(2,1)} %all-to-all-done.1.source_ref), custom_call_target="tpu_custom_call" | custom-call | bytes 2359296 | tf_op jit(solution)/shard_map/pick_blocks/pallas_call | solution.py:125
  307.0 3.0 convert_element_type.83
  310.0 0.7 multiply_reduce_fusion.1
  310.7 24.2 %reduce-scatter.4.cloned.1.call-done = bf16[72,3456]{1,0:T(8,128)(2,1)} async-done(((bf16[1152,3456]{1,0:T(8,128)(2,1)}), bf16[72,3456]{1,0:T(8,128)(2,1)}) %reduce-scatter.4.cloned.1.call-update) | async-done | bytes 497680
  334.9 3.4 fusion.5
  338.3 57.9 %all-reduce.3.cloned.1.call-done = bf16[72,3456]{1,0:T(8,128)(2,1)} async-done(((bf16[72,3456]{1,0:T(8,128)(2,1)}), bf16[72,3456]{1,0:T(8,128)(2,1)}) %all-reduce.3.cloned.1.call-update) | async-done | bytes 497680 | tf_op jit(solution)/shard_map/psum | solution.py:218
  396.2 2.4 multiply_reduce_fusion.2
  398.6 0.6 dynamic-slice_divide_fusion
  (35 shorter events, 0.5 us)
Async XLA Ops:
  7.2 5.4 %copy-start = (bf16[1,512,1152]{2,1,0:T(8,128)(2,1)S(1)}, bf16[1,512,1152]{2,1,0:T(8,128)(2,1)}, u32[]{:S(2)}) copy-start(bf16[1,512,1152]{2,1,0:T(8,128)(2,1)} %param.6) | copy-start | bytes 3538948
  7.2 5.4 %copy-start.6 = (f32[1152]{0:T(1024)S(1)}, f32[1152]{0:T(1024)}, u32[]{:S(2)}) copy-start(f32[1152]{0:T(1024)} %param.9) | copy-start | bytes 13828
  8.1 0.6 copy-start.8
  10.3 2.3 copy-start.7
  23.6 86.1 %all-to-all-start = ((bf16[16,128,1152]{2,1,0:T(8,128)(2,1)}), bf16[16,128,1152]{2,1,0:T(8,128)(2,1)}, u32[]{:S(2)}, u32[]{:S(2)}) async-start(bf16[16,128,1152]{2,1,0:T(8,128)(2,1)} %pick_blocks.4), calls=%async_computation | async-start | bytes 9437184 | tf_op jit(solution)/shard_map/all_to_all | solution.py:179
  32.6 302.3 %reduce-scatter.4.cloned.1.call-start = ((), (), s32[]{:S(2)}) async-start(), calls=%async_computation.4 | async-start | bytes 8460288
  36.9 63.7 %collective-permute-start.2 = (bf16[128,1152]{0,1:T(8,128)(2,1)}, bf16[128,1152]{0,1:T(8,128)(2,1)}, u32[]{:S(2)}, u32[]{:S(2)}) collective-permute-start(bf16[128,1152]{0,1:T(8,128)(2,1)} %get-tuple-element.34), channel_id=1, source_target_pairs={{0,1},{1,2},{2,3},{3,4},{4,5},{5,6},{6,7},{7,8},{8,9},{9,10},{10,1... | collective-permute-start | bytes 884744 | tf_op jit(solution)/shard_map/ppermute | solution.py:164
  40.8 66.9 %collective-permute-start.3 = (bf16[128,1152]{0,1:T(8,128)(2,1)}, bf16[128,1152]{0,1:T(8,128)(2,1)}, u32[]{:S(2)}, u32[]{:S(2)}) collective-permute-start(bf16[128,1152]{0,1:T(8,128)(2,1)} %get-tuple-element.35), channel_id=1, source_target_pairs={{1,0},{2,1},{3,2},{4,3},{5,4},{6,5},{7,6},{8,7},{9,8},{10,9},{11,1... | collective-permute-start | bytes 884744 | tf_op jit(solution)/shard_map/ppermute | solution.py:165
  113.7 14.3 %slice-start = ((s8[7962624]{0:T(1024)(128)(4,1)}), s8[4194304]{0:T(1024)(128)(4,1)S(1)}, s32[]{:S(2)}) async-start(s8[7962624]{0:T(1024)(128)(4,1)} %bitcast.76), calls=%async_computation.5 | async-start | bytes 8388608
  115.0 13.1 %collective-permute-start = (bf16[128,1152]{1,0:T(8,128)(2,1)S(1)}, bf16[128,1152]{1,0:T(8,128)(2,1)S(1)}, u32[]{:S(2)}, u32[]{:S(2)}) collective-permute-start(bf16[128,1152]{1,0:T(8,128)(2,1)S(1)} %get-tuple-element.36), channel_id=1, source_target_pairs={{0,1},{1,2},{2,3},{3,4},{4,5},{5,6},{6,7},{7,8},{8,9},{9,10},{10,1... | collective-permute-start | bytes 884744 | tf_op jit(solution)/shard_map/ppermute | solution.py:164
  116.4 11.6 %collective-permute-start.1 = (bf16[128,1152]{1,0:T(8,128)(2,1)S(1)}, bf16[128,1152]{1,0:T(8,128)(2,1)S(1)}, u32[]{:S(2)}, u32[]{:S(2)}) collective-permute-start(bf16[128,1152]{1,0:T(8,128)(2,1)S(1)} %get-tuple-element.37), channel_id=1, source_target_pairs={{1,0},{2,1},{3,2},{4,3},{5,4},{6,5},{7,6},{8,7},{9,8},{10,9},{11,1... | collective-permute-start | bytes 884744 | tf_op jit(solution)/shard_map/ppermute | solution.py:165
  117.7 10.3 %slice-start.1 = ((s8[7962624]{0:T(1024)(128)(4,1)}), s8[3768320]{0:T(1024)(128)(4,1)S(1)}, s32[]{:S(2)}) async-start(s8[7962624]{0:T(1024)(128)(4,1)} %bitcast.76), calls=%async_computation.6 | async-start | bytes 7536640
  174.9 1.6 copy-start.4
  174.9 2.0 copy-start.3
  176.5 2.3 copy-start.2
  176.9 1.9 copy-start.5
  206.1 96.7 %all-to-all-start.1 = ((bf16[16,128,1152]{2,1,0:T(8,128)(2,1)}), bf16[16,128,1152]{2,1,0:T(8,128)(2,1)}, u32[]{:S(2)}, u32[]{:S(2)}) async-start(bf16[16,128,1152]{2,1,0:T(8,128)(2,1)} %pick_blocks.6), calls=%async_computation.1 | async-start | bytes 9437184 | tf_op jit(solution)/shard_map/all_to_all | solution.py:208
  218.8 177.4 %all-reduce.3.cloned.1.call-start = ((), (), s32[]{:S(2)}) async-start(), calls=%async_computation.3 | async-start | bytes 995328 | tf_op jit(solution)/shard_map/psum | solution.py:218
  307.0 3.0 copy-start.1
Sparse Core Ops, SparseCore 0:
  185.6 149.2 reduce-scatter.3
  337.2 58.9 all-reduce.2

commit v2 on v1

v2 whole, which is shorter than its diff:
```python
import functools

import jax
import jax.numpy as jnp
from jax import lax
from jax.experimental import pallas as pl
from jax.experimental.pallas import tpu as pltpu
from jax.sharding import Mesh
from jax.sharding import PartitionSpec as P

HEADS = 16
HD = 72
BLK = 128
PAIR = 2 * HD
BF16 = jnp.bfloat16
F32 = jnp.float32
EPSILON = 1e-06
SCORE_SCALE = HD ** (-0.5)
HIDDEN_BIAS = -1e30
DP = ("y", "core")
SEQ = ("z", "x")


def nn(a, b):
    return lax.dot_general(a, b, (((1,), (0,)), ((), ())), preferred_element_type=F32)


def nt(a, b):
    return lax.dot_general(a, b, (((1,), (1,)), ((), ())), preferred_element_type=F32)


def attention_kernel(
    col_ref, row_ref, q_ref, k_ref, v_ref, qh_ref, kh_ref, vh_ref, g_ref, gh_ref,
    o_ref, d_ref, bias_ref, o_s, d_s,
):
    blocks = q_ref.shape[1] // BLK
    rows = q_ref.shape[1]

    @pl.when(pl.program_id(0) == 0)
    def _():
        for b in range(blocks + 2):
            first, last = max(b - 1, 0), min(b + 1, blocks + 1)
            same = col_ref[b * BLK : (b + 1) * BLK, :] == row_ref[:, first * BLK : (last + 1) * BLK]
            bias_ref[b, :, : (last + 1 - first) * BLK] = jnp.where(same, 0.0, HIDDEN_BIAS)

    for head in range(2):
        lo, hi = head * HD, (head + 1) * HD

        def whole(own, halo):
            mid, rim = own[...].astype(F32)[lo:hi], halo[...].astype(F32)[lo:hi]
            return jnp.concatenate([rim[:, :BLK], mid, rim[:, BLK:]], axis=1)

        q32, g32 = whole(q_ref, qh_ref), whole(g_ref, gh_ref)
        q, g = q32.astype(BF16), g32.astype(BF16)
        k, v = whole(k_ref, kh_ref).astype(BF16), whole(v_ref, vh_ref).astype(BF16)
        q_at, k_at, v_at = (slice((3 * head + part) * HD, (3 * head + part + 1) * HD) for part in range(3))
        d_s[k_at, :] = jnp.zeros((HD, rows), F32)
        d_s[v_at, :] = jnp.zeros((HD, rows), F32)
        for b in range(blocks + 2):
            first, last = max(b - 1, 0), min(b + 1, blocks + 1)
            width = (last + 1 - first) * BLK
            k_win = k[:, first * BLK : (last + 1) * BLK]
            v_win = v[:, first * BLK : (last + 1) * BLK]
            here = slice(b * BLK, (b + 1) * BLK)
            scores = nn(q32[:, here].T.astype(BF16), k_win)
            grad_probs = nn(g32[:, here].T.astype(BF16), v_win)
            weights = jnp.exp(scores * SCORE_SCALE + bias_ref[b, :, :width])
            probs = weights * (1.0 / jnp.sum(weights, axis=1, keepdims=True))
            rounded = probs.astype(BF16)
            centred = jnp.sum(probs * grad_probs, axis=1, keepdims=True)
            grad_scores = (probs * (grad_probs - centred) * SCORE_SCALE).astype(BF16)
            if 1 <= b <= blocks:
                own = slice((b - 1) * BLK, b * BLK)
                o_s[lo:hi, own] = nt(v_win, rounded)
                d_s[q_at, own] = nt(k_win, grad_scores)
            k0, k1 = max(first, 1), min(last, blocks)
            seen = slice((k0 - first) * BLK, (k1 + 1 - first) * BLK)
            into = slice((k0 - 1) * BLK, k1 * BLK)
            d_s[k_at, into] += nn(q[:, here], grad_scores[:, seen])
            d_s[v_at, into] += nn(g[:, here], rounded[:, seen])
    o_ref[...] = o_s[...].astype(BF16)
    d_ref[...] = d_s[...].astype(BF16)


def attention_call(ids, own, halo, g_own, g_halo, first_pair=0, pairs=HEADS // 2):
    rows, rim = own.shape[1], halo.shape[1]
    total, blocks = rows + rim, rows // BLK
    per_part = HEADS // 2

    def spec(width, part):
        return pl.BlockSpec((PAIR, width), lambda i: (part * per_part + first_pair + i, 0))

    return pl.pallas_call(
        attention_kernel,
        grid=(pairs,),
        in_specs=[
            pl.BlockSpec((total, 1), lambda i: (0, 0)),
            pl.BlockSpec((1, total), lambda i: (0, 0)),
            spec(rows, 0), spec(rows, 1), spec(rows, 2),
            spec(rim, 0), spec(rim, 1), spec(rim, 2),
            spec(rows, 0), spec(rim, 0),
        ],
        out_specs=[
            pl.BlockSpec((PAIR, rows), lambda i: (i, 0)),
            pl.BlockSpec((3 * PAIR, rows), lambda i: (i, 0)),
        ],
        out_shape=[
            jax.ShapeDtypeStruct((pairs * PAIR, rows), BF16),
            jax.ShapeDtypeStruct((pairs * 3 * PAIR, rows), BF16),
        ],
        scratch_shapes=[
            pltpu.VMEM((blocks + 2, BLK, 3 * BLK), F32),
            pltpu.VMEM((PAIR, rows), F32),
            pltpu.VMEM((3 * PAIR, rows), F32),
        ],
        cost_estimate=pl.CostEstimate(
            flops=pairs * 2 * 16 * 12 * BLK * BLK * HD,
            bytes_accessed=pairs * PAIR * (rows * 8 + rim * 4) * 2,
            transcendentals=pairs * 2 * 16 * BLK * BLK,
        ),
        name="packed_attention",
    )(ids[:, None], ids[None, :], own, own, own, halo, halo, halo, g_own, g_halo)


def route_kernel(me_ref, order_ref, first_ref, cross_ref, last_ref, back_first_ref, back_cross_ref, back_last_ref, place, half, hue):
    me = me_ref[0]
    count = order_ref.shape[0]

    def clear(p, _):
        place[order_ref[p]] = p
        half[p] = -1
        hue[p] = -1
        return 0

    lax.fori_loop(0, count, clear, 0)

    def split(bits, partner, mate, seed):
        def start(i, _):
            def step(state):
                at, _ = state
                other = partner(at)
                bits[at] = 0
                bits[other] = 1
                following = mate(other)
                return following, bits[following] < 0

            at = seed(i)
            lax.while_loop(lambda state: state[1], step, (at, bits[at] < 0))
            return 0

        lax.fori_loop(0, count // 2, start, 0)

    split(half, lambda p: p ^ 1, lambda p: place[order_ref[p] ^ 1], lambda i: 2 * i)

    def same_half(p):
        return jnp.where(half[p ^ 2] == half[p], p ^ 2, p ^ 3)

    def same_half_loader(p):
        block = order_ref[p]
        near, far = place[block ^ 2], place[block ^ 3]
        return jnp.where(half[near] == half[p], near, far)

    split(hue, same_half, same_half_loader, lambda i: 4 * (i // 2) + i % 2)

    for slot in range(4):
        at = place[4 * me + slot]
        colour = 2 * half[at] + hue[at]
        first_ref[colour] = slot
        back_last_ref[slot] = colour
        at = 4 * me + slot
        colour = 2 * half[at] + hue[at]
        back_first_ref[colour] = slot
        last_ref[slot] = colour

    mine = me // 4

    def cross(p, _):
        @pl.when(2 * half[p] + hue[p] == mine)
        def _():
            source = order_ref[p] // 4
            cross_ref[p // 4] = source
            back_cross_ref[source] = p // 4

        return 0

    lax.fori_loop(0, count, cross, 0)


def route(me, order):
    smem = pl.BlockSpec(memory_space=pltpu.SMEM)
    sizes = (4, 16, 4, 4, 16, 4)
    return pl.pallas_call(
        route_kernel,
        in_specs=[smem, smem],
        out_specs=[smem] * len(sizes),
        out_shape=[jax.ShapeDtypeStruct((n,), jnp.int32) for n in sizes],
        scratch_shapes=[pltpu.SMEM(order.shape, jnp.int32)] * 3,
        name="route_blocks",
    )(me[None], order)


def pick_kernel(index_ref, source_ref, out_ref):
    for i in range(out_ref.shape[0]):
        out_ref[i] = source_ref[index_ref[i]]


def pick(index, source):
    shape = (index.shape[0],) + source.shape[1:]
    size = 2 * shape[0] * shape[1] * shape[2]
    return pl.pallas_call(
        pick_kernel,
        in_specs=[pl.BlockSpec(memory_space=pltpu.SMEM), pl.BlockSpec(memory_space=pltpu.VMEM)],
        out_specs=pl.BlockSpec(memory_space=pltpu.VMEM),
        out_shape=jax.ShapeDtypeStruct(shape, source.dtype),
        cost_estimate=pl.CostEstimate(flops=0, bytes_accessed=2 * size, transcendentals=0),
        name="pick_blocks",
    )(index, source)


def statistics(values):
    centre = jnp.mean(values, axis=1, keepdims=True)
    spread = jnp.mean((values - centre) ** 2, axis=1, keepdims=True)
    inverse_std = lax.rsqrt(spread + EPSILON)
    return (values - centre) * inverse_std, inverse_std


def norm_kernel(index_ref, rows_ref, gain_ref, out_ref):
    normed, _ = statistics(rows_ref[0].astype(F32))
    out_ref[0] = (normed * gain_ref[...]).astype(BF16)


def norm_blocks(index, blocks, gain):
    count, rows, width = blocks.shape
    return pl.pallas_call(
        norm_kernel,
        grid_spec=pltpu.PrefetchScalarGridSpec(
            num_scalar_prefetch=1,
            grid=(count,),
            in_specs=[
                pl.BlockSpec((1, rows, width), lambda i, index: (index[i], 0, 0)),
                pl.BlockSpec((1, width), lambda i, index: (0, 0)),
            ],
            out_specs=pl.BlockSpec((1, rows, width), lambda i, index: (i, 0, 0)),
        ),
        out_shape=jax.ShapeDtypeStruct(blocks.shape, BF16),
        name="norm_blocks",
    )(index, blocks, gain[None])


def norm_back_kernel(index_ref, grads_ref, rows_ref, gain_ref, out_ref):
    normed, inverse_std = statistics(rows_ref[0].astype(F32))
    pushed = grads_ref[0].astype(F32) * gain_ref[...]
    along = jnp.mean(pushed * normed, axis=1, keepdims=True)
    out_ref[0] = (
        inverse_std * (pushed - jnp.mean(pushed, axis=1, keepdims=True) - normed * along)
    ).astype(BF16)


def norm_back(index, grads, blocks, gain):
    count, rows, width = blocks.shape
    return pl.pallas_call(
        norm_back_kernel,
        grid_spec=pltpu.PrefetchScalarGridSpec(
            num_scalar_prefetch=1,
            grid=(count,),
            in_specs=[
                pl.BlockSpec((1, rows, width), lambda i, index: (index[i], 0, 0)),
                pl.BlockSpec((1, rows, width), lambda i, index: (i, 0, 0)),
                pl.BlockSpec((1, width), lambda i, index: (0, 0)),
            ],
            out_specs=pl.BlockSpec((1, rows, width), lambda i, index: (i, 0, 0)),
        ),
        out_shape=jax.ShapeDtypeStruct(blocks.shape, BF16),
        name="norm_back",
    )(index, grads, blocks, gain[None])


GROUPS = 2


def local(loader_rows, lengths, block_order, norm_gain, qkv_weight, upstream_grad):
    seq_count = lax.axis_size(SEQ)
    pack_count = lax.axis_size(DP)
    my_index = lax.axis_index(SEQ)
    _, row_count, model_width = loader_rows.shape
    per_device = row_count // BLK
    order_row = block_order[0]
    block_total = order_row.shape[0]
    piece = BLK * per_device // seq_count
    first, cross, last, back_first, back_cross, back_last = route(my_index, order_row)

    def exchange(x):
        x = x.reshape(seq_count, piece, model_width)
        return lax.all_to_all(x, SEQ, split_axis=0, concat_axis=0, tiled=True)

    up = [(i, i + 1) for i in range(seq_count - 1)]
    down = [(i + 1, i) for i in range(seq_count - 1)]

    def halo(x):
        before = lax.ppermute(x[row_count - BLK :], SEQ, up)
        after = lax.ppermute(x[:BLK], SEQ, down)
        return jnp.concatenate([before, after], axis=0)

    upstream = upstream_grad[0]
    upstream_own = upstream.T
    upstream_halo = halo(upstream).T

    loader_blocks = loader_rows[0].reshape(per_device, BLK, model_width)
    outgoing = norm_blocks(first, loader_blocks, norm_gain)
    spread = exchange(pick(cross, exchange(outgoing)))
    scaled = pick(last, spread.reshape(per_device, BLK, model_width)).reshape(row_count, model_width)
    scaled_halo = halo(scaled)

    def project(rows):
        return lax.dot_general(
            qkv_weight, rows, (((0,), (1,)), ((), ())), preferred_element_type=F32
        ).astype(BF16)

    qkv_own = project(scaled)
    qkv_halo = project(scaled_halo)
    image_ends = jnp.cumsum(lengths[0])
    positions = my_index * row_count - BLK + jnp.arange(row_count + 2 * BLK, dtype=jnp.int32)
    counted = jnp.sum((image_ends[None, :] <= positions[:, None]).astype(jnp.int32), axis=1)
    inside = (positions >= 0) & (positions < block_total * BLK)
    ids = jnp.where(inside, counted, -1)

    pairs = HEADS // 2 // GROUPS
    attended, grads, shares = [], [], []
    for group in range(GROUPS):
        out, grad = attention_call(
            ids, qkv_own, qkv_halo, upstream_own, upstream_halo, group * pairs, pairs
        )
        weight_local = nn(grad, scaled).astype(BF16)
        shares.append(lax.psum_scatter(weight_local, DP, scatter_dimension=0, tiled=True))
        attended.append(out)
        grads.append(grad)
    attention = jnp.concatenate(attended, axis=0).T[None]
    grad_cols = jnp.concatenate(grads, axis=0).reshape(HEADS, 3, HD, row_count)
    grad_cols = grad_cols.transpose(1, 0, 2, 3).reshape(3 * model_width, row_count)
    input_grad = lax.dot_general(
        grad_cols, qkv_weight, (((0,), (1,)), ((), ())), preferred_element_type=F32
    ).astype(BF16)
    returning = pick(back_first, input_grad.reshape(per_device, BLK, model_width))
    returned = exchange(pick(back_cross, exchange(returning)))
    loader_grad = norm_back(
        back_last, returned.reshape(per_device, BLK, model_width), loader_blocks, norm_gain
    ).reshape(1, row_count, model_width)

    share = model_width // seq_count
    per_pack = 3 * model_width // pack_count
    partial = jnp.concatenate(shares, axis=0).T.reshape(seq_count, share, per_pack)
    partial = lax.all_to_all(partial, SEQ, split_axis=0, concat_axis=0, tiled=True)
    summed = jnp.sum(partial.astype(F32), axis=0).astype(BF16)
    weight_cols = lax.all_gather(summed, DP, axis=0)
    heads = HEADS // GROUPS // pack_count
    weight_cols = weight_cols.reshape(pack_count, share, GROUPS, heads, 3, HD)
    weight_grad = weight_cols.transpose(1, 4, 2, 0, 3, 5).reshape(share, 3 * model_width)
    weight_grad = weight_grad.astype(F32) / pack_count
    weight_rows = lax.dynamic_slice_in_dim(qkv_weight, my_index * share, share, 0).astype(F32)
    gain_rows = lax.dynamic_slice_in_dim(norm_gain, my_index * share, share, 0)
    gain_grad = jnp.sum(weight_rows * weight_grad, axis=1) / gain_rows
    return (attention, loader_grad, weight_grad, gain_grad)


def solution(mesh):
    fine = Mesh(mesh.devices.reshape(4, 2, 4, 4), DP + SEQ)
    rows = P(DP, SEQ, None)
    return jax.shard_map(
        local,
        mesh=fine,
        in_specs=(rows, P(DP, None), P(DP, None), P(), P(), rows),
        out_specs=(rows, rows, P(SEQ, None), P(SEQ)),
        check_vma=False,
    )
```

time: 409 us -> 270 us (0.66)
  waiting for transfers between devices: 221 us -> 50.2 us
  blocking collectives: 0 us -> 43.3 us
  other arithmetic: 27 us -> 9.15 us
    psum x1 -> x0, waiting for transfers between devices: 57.9 us -> none  [local(): weight_grad = lax.psum(weight_share, DP).astype(F32) / pack_count]
    all_to_all x2 -> x4, waiting for transfers between devices: 81.6 us -> 30.5 us  [the longest x3 22.3 us: exchange(): return lax.all_to_all(x, SEQ, split_axis=0, concat_axis=0, tiled=True)]
    ppermute x2, waiting for transfers between devices: 50.4 us -> 11.1 us  [halo(): before = lax.ppermute(x[row_count - BLK:], SEQ, up)]
    all_to_all x0 -> x1, blocking collectives: none -> 25.8 us  [exchange(): return lax.all_to_all(x, SEQ, split_axis=0, concat_axis=0, tiled=True)]
    unnamed x3 -> x4, waiting for transfers between devices: 24.2 us -> 6.58 us
    all_gather x0 -> x1, blocking collectives: none -> 17.5 us  [local(): weight_cols = lax.all_gather(summed, DP, axis=0)]
    convert_element_type x3 -> x0, other arithmetic: 7.86 us -> none  [the longest x1 3.41 us: local(): loader_grad = row_grad.astype(BF16)[None]]
    reduce_sum x6 -> x1, other arithmetic: 6.06 us -> 0.18 us  [local(): summed = jnp.sum(partial.astype(F32), axis=0).astype(BF16)]
  transfers between devices with their start and end apart: 8 -> 10, of which waited for: 5 -> 6; matrix products, arithmetic and copies ran while one was open for 11% -> 13% of each run, Pallas kernels for 3% -> 12%
where the time goes in v2:
time: 270 us; the launch traced here: 269 us
  Pallas kernels  69.2 us (26%)
  waiting for transfers between devices  50.2 us (19%)
  blocking collectives  43.3 us (16%)
  matrix products  35.5 us (13%)
  starting transfers between devices  32.6 us (12%)
  local copies, waits for them, and re-layouts  14.6 us (5%)
  between operations  14.3 us (5%)
  other arithmetic  9.15 us (3%)
    pallas_call x2, Pallas kernels, attention_call(): pl.pallas_call(attention_kernel, grid=(pairs,), in_specs=[pl.BlockSpec((t...  44.6 us
    all_to_all x1, blocking collectives, exchange(): return lax.all_to_all(x, SEQ, split_axis=0, concat_axis=0, tiled=True)  25.8 us
    all_to_all x3, waiting for transfers between devices, exchange(): return lax.all_to_all(x, SEQ, split_axis=0, concat_axis=0, tiled=True)  22.3 us
    all_gather x1, blocking collectives, local(): weight_cols = lax.all_gather(summed, DP, axis=0)  17.5 us
    all_to_all x3, starting transfers between devices, exchange(): return lax.all_to_all(x, SEQ, split_axis=0, concat_axis=0, tiled=True)  17.4 us
    dot_general x2, matrix products, project(): lax.dot_general(qkv_weight, rows, (((0,), (1,)), ((), ())), preferred_ele...  15.1 us
    dot_general x2, matrix products, nn(): lax.dot_general(a, b, (((1,), (0,)), ((), ())), preferred_element_type=F32)  11.8 us
    ppermute x2, waiting for transfers between devices, halo(): before = lax.ppermute(x[row_count - BLK:], SEQ, up)  11.1 us
  transfers between devices with their start and end apart: 10, of which 6 were waited for; matrix products, arithmetic and copies ran while one was open for 13% of the time, Pallas kernels for 12%

profile of v2, /device:TPU:1, one launch (start us, length us, event | category | flops | bytes accessed | tf_op | source)
XLA Modules:
  0.0 269.0 jit_solution(5064945722224180700)
XLA Ops:
  7.2 1.3 broadcast_in_dim.25.gain_ref
  8.5 5.4 %route_blocks.1 = (s32[4]{0:T(128)}, s32[16]{0:T(128)}, s32[4]{0:T(128)}, s32[4]{0:T(128)}, s32[16]{0:T(128)}, /*index=5*/s32[4]{0:T(128)}) custom-call(s32[1]{0:T(128)} %bitcast.1.me_ref, s32[64]{0:T(128)} %bitcast.75), custom_call_target="tpu_custom_call" | custom-call | tf_op jit(solution)/shard_map/route_blocks/pallas_call | solution.py:192
  13.9 4.6 %norm_blocks.1 = bf16[4,128,1152]{2,1,0:T(8,128)(2,1)} custom-call(s32[4]{0:T(128)} %get-tuple-element.16.index_ref, bf16[4,128,1152]{2,1,0:T(8,128)(2,1)} %bitcast.60, f32[1,1152]{1,0:T(1,128)} %broadcast_in_dim.25.gain_ref), custom_call_target="tpu_custom_call" | custom-call | tf_op jit(solution)/shard_map/norm_blocks/pallas_call | solution.py:234
  18.5 8.5 %all-to-all-start = ((bf16[16,32,1152]{2,1,0:T(8,128)(2,1)}), bf16[16,32,1152]{2,1,0:T(8,128)(2,1)S(1)}, u32[]{:S(2)}, u32[]{:S(2)}) async-start(bf16[16,32,1152]{2,1,0:T(8,128)(2,1)} %bitcast.65), calls=%async_computation | async-start | bytes 2359296 | tf_op jit(solution)/shard_map/all_to_all | solution.py:294
  27.1 0.6 copy.68
  27.7 16.8 %all-to-all-done.source_ref = bf16[16,32,1152]{2,1,0:T(8,128)(2,1)S(1)} async-done(((bf16[16,32,1152]{2,1,0:T(8,128)(2,1)}), bf16[16,32,1152]{2,1,0:T(8,128)(2,1)S(1)}, u32[]{:S(2)}, u32[]{:S(2)}) %all-to-all-start) | async-done | bytes 1179680 | tf_op jit(solution)/shard_map/all_to_all | solution.py:294
  44.5 1.0 copy-done.3
  45.5 2.4 pick_blocks.4
  47.9 5.1 %all-to-all-start.1 = ((bf16[16,32,1152]{2,1,0:T(8,128)(2,1)}), bf16[16,32,1152]{2,1,0:T(8,128)(2,1)S(1)}, u32[]{:S(2)}, u32[]{:S(2)}) async-start(bf16[16,32,1152]{2,1,0:T(8,128)(2,1)} %pick_blocks.4), calls=%async_computation.1 | async-start | bytes 2359296 | tf_op jit(solution)/shard_map/all_to_all | solution.py:294
  53.2 3.3 %collective-permute-start.2 = (bf16[128,1152]{0,1:T(8,128)(2,1)S(1)}, bf16[128,1152]{0,1:T(8,128)(2,1)S(1)}, u32[]{:S(2)}, u32[]{:S(2)}) collective-permute-start(bf16[128,1152]{0,1:T(8,128)(2,1)S(1)} %get-tuple-element.48), channel_id=1, source_target_pairs={{0,1},{1,2},{2,3},{3,4},{4,5},{5,6},{6,7},{7,8},{8,9},{9,10},{10,1... | collective-permute-start | bytes 884744 | tf_op jit(solution)/shard_map/ppermute | solution.py:300
  56.5 1.3 collective-permute-start.3
  59.1 0.9 reshape_select_fusion.col_ref
  60.0 11.1 %collective-permute-done.2 = bf16[128,1152]{0,1:T(8,128)(2,1)S(1)} collective-permute-done((bf16[128,1152]{0,1:T(8,128)(2,1)S(1)}, bf16[128,1152]{0,1:T(8,128)(2,1)S(1)}, u32[]{:S(2)}, u32[]{:S(2)}) %collective-permute-start.2) | collective-permute-done | bytes 294944 | tf_op jit(solution)/shard_map/ppermute | solution.py:300
  71.1 2.1 collective-permute-done.3
  73.1 0.9 maximum_bitcast_fusion.1.gh_ref
  74.0 1.0 copy-done.1
  75.0 2.4 pick_blocks.5
  77.4 1.2 slice_bitcast_fusion.3
  78.7 4.2 %collective-permute-start = (bf16[128,1152]{1,0:T(8,128)(2,1)S(1)}, bf16[128,1152]{1,0:T(8,128)(2,1)S(1)}, u32[]{:S(2)}, u32[]{:S(2)}) collective-permute-start(bf16[128,1152]{1,0:T(8,128)(2,1)S(1)} %get-tuple-element.50), channel_id=1, source_target_pairs={{0,1},{1,2},{2,3},{3,4},{4,5},{5,6},{6,7},{7,8},{8,9},{9,10},{10,1... | collective-permute-start | bytes 884744 | tf_op jit(solution)/shard_map/ppermute | solution.py:300
  82.9 1.3 collective-permute-start.1
  84.2 10.3 %fusion.q_ref.k_ref.v_ref = bf16[3456,512]{1,0:T(8,128)(2,1)} fusion(bf16[512,1152]{1,0:T(8,128)(2,1)} %bitcast.67, bf16[1152,3456]{1,0:T(8,128)(2,1)} %param.10), kind=kOutput, calls=%fused_computation.3 | convolution fusion | flops 4078632960 | bytes 12681216 | tf_op jit(solution)/shard_map/dot_general | solution.py:315
  94.6 4.8 %fusion.1.qh_ref.kh_ref.vh_ref = bf16[3456,256]{1,0:T(8,128)(2,1)} fusion(bf16[1152,3456]{1,0:T(8,128)(2,1)S(1)} %bitcast.73, bf16[128,1152]{1,0:T(8,128)(2,1)S(1)} %collective-permute-done.1, bf16[128,1152]{1,0:T(8,128)(2,1)S(1)} %collective-permute-done), kind=kOutput, calls=%fused_computation.5 | convolution fusion | flops 2040496128 | bytes 10321920 | tf_op jit(solution)/shard_map/dot_general | solution.py:315
  99.4 22.4 %packed_attention.2 = (bf16[576,512]{1,0:T(8,128)(2,1)}, bf16[1728,512]{1,0:T(8,128)(2,1)}) custom-call(s32[768,1]{1,0:T(8,128)} %reshape_select_fusion.col_ref, s32[1,768]{1,0:T(1,128)} %and_select_fusion.row_ref, bf16[3456,512]{1,0:T(8,128)(2,1)} %fusion.q_ref.k_ref.v_ref, bf16[3456,512]{1,0:T(8,128)(2,1)} %fusion.q_ref.k_ref.v_ref, ...), custom_call_target="tpu_custom_call" | custom-call | flops 1811939328 | bytes 5898240 | tf_op jit(solution)/shard_map/packed_attention/pallas_call | solution.py:93
  121.8 5.9 %convolution_convert_fusion.1 = bf16[1728,1152]{1,0:T(8,128)(2,1)} fusion(bf16[1728,512]{1,0:T(8,128)(2,1)} %get-tuple-element.22, bf16[512,1152]{1,0:T(8,128)(2,1)S(1)} %bitcast.68), kind=kOutput, calls=%fused_computation.1 | convolution fusion | flops 2040422400 | bytes 6930432 | tf_op jit(solution)/shard_map/dot_general | solution.py:25
  127.7 22.2 %packed_attention.3 = (bf16[576,512]{1,0:T(8,128)(2,1)}, bf16[1728,512]{1,0:T(8,128)(2,1)}) custom-call(s32[768,1]{1,0:T(8,128)} %reshape_select_fusion.col_ref, s32[1,768]{1,0:T(1,128)} %and_select_fusion.row_ref, bf16[3456,512]{1,0:T(8,128)(2,1)} %fusion.q_ref.k_ref.v_ref, bf16[3456,512]{1,0:T(8,128)(2,1)} %fusion.q_ref.k_ref.v_ref, ...), custom_call_target="tpu_custom_call" | custom-call | flops 1811939328 | bytes 5898240 | tf_op jit(solution)/shard_map/packed_attention/pallas_call | solution.py:93
  150.0 5.9 %convolution_convert_fusion = bf16[1728,1152]{1,0:T(8,128)(2,1)} fusion(bf16[1728,512]{1,0:T(8,128)(2,1)} %get-tuple-element.23, bf16[512,1152]{1,0:T(8,128)(2,1)S(1)} %bitcast.69), kind=kOutput, calls=%fused_computation | convolution fusion | flops 2040422400 | bytes 6930432 | tf_op jit(solution)/shard_map/dot_general | solution.py:25
  155.9 1.5 copy-done.6
  158.5 8.6 %convolution_convert_fusion.4 = bf16[512,1152]{1,0:T(8,128)(2,1)} fusion(bf16[3456,512]{1,0:T(8,128)(2,1)S(1)} %bitcast.66, bf16[1152,3456]{1,0:T(8,128)(2,1)} %param.10), kind=kOutput, calls=%fused_computation.7 | convolution fusion | flops 4077453312 | bytes 12681216 | tf_op jit(solution)/shard_map/dot_general | solution.py:340
  167.1 2.4 pick_blocks.6
  169.5 25.8 %all_to_all.25.source_ref = bf16[16,32,1152]{2,1,0:T(8,128)(2,1)} all-to-all(bf16[16,32,1152]{2,1,0:T(8,128)(2,1)} %bitcast.64), channel_id=1, replica_groups=mesh['y'=4,'core'=2,'z'=4,'x'=4] {'z','x'}, dimensions={0} | all-to-all | bytes 2359296 | tf_op jit(solution)/shard_map/all_to_all | solution.py:294
  195.3 2.4 pick_blocks.7
  197.6 3.7 %all-to-all-start.3 = ((bf16[16,32,1152]{2,1,0:T(8,128)(2,1)}), bf16[16,32,1152]{2,1,0:T(8,128)(2,1)S(1)}, u32[]{:S(2)}, u32[]{:S(2)}) async-start(bf16[16,32,1152]{2,1,0:T(8,128)(2,1)} %pick_blocks.7), calls=%async_computation.3 | async-start | bytes 2359296 | tf_op jit(solution)/shard_map/all_to_all | solution.py:294
  201.4 1.3 copy.72
  202.7 6.5 %reduce-scatter.9.cloned.1.call-done = bf16[216,1152]{1,0:T(8,128)(2,1)} async-done(((bf16[1728,1152]{1,0:T(8,128)(2,1)}), bf16[216,1152]{1,0:T(8,128)(2,1)}) %reduce-scatter.9.cloned.1.call-update) | async-done | bytes 497680
  209.2 1.3 copy.73
  210.5 1.5 pad_maximum_fusion.1
  211.9 5.5 %all-to-all-done.3 = bf16[16,32,1152]{2,1,0:T(8,128)(2,1)S(1)} async-done(((bf16[16,32,1152]{2,1,0:T(8,128)(2,1)}), bf16[16,32,1152]{2,1,0:T(8,128)(2,1)S(1)}, u32[]{:S(2)}, u32[]{:S(2)}) %all-to-all-start.3) | async-done | bytes 1179680 | tf_op jit(solution)/shard_map/all_to_all | solution.py:294
  217.4 5.1 %all-to-all-start.4 = ((bf16[16,72,432]{2,1,0:T(8,128)(2,1)}), bf16[16,72,432]{2,1,0:T(8,128)(2,1)S(1)}, u32[]{:S(2)}, u32[]{:S(2)}) async-start(bf16[16,72,432]{2,1,0:T(8,128)(2,1)} %bitcast.27), calls=%async_computation.4 | async-start | bytes 2359296 | tf_op jit(solution)/shard_map/all_to_all | solution.py:352
  222.5 1.3 maximum_bitcast_fusion
  223.8 1.4 copy.76
  225.2 5.0 %norm_back.1 = bf16[4,128,1152]{2,1,0:T(8,128)(2,1)} custom-call(s32[4]{0:T(128)} %get-tuple-element.19.index_ref, bf16[4,128,1152]{2,1,0:T(8,128)(2,1)} %bitcast.63, bf16[4,128,1152]{2,1,0:T(8,128)(2,1)} %bitcast.61, f32[1,1152]{1,0:T(1,128)} %broadcast_in_dim.25.gain_ref), custom_call_target="tpu_custom_call" | custom-call | tf_op jit(solution)/shard_map/norm_back/pallas_call | solution.py:261
  230.2 8.3 %all-to-all-done.4 = bf16[16,72,432]{2,1,0:T(8,128)(2,1)S(1)} async-done(((bf16[16,72,432]{2,1,0:T(8,128)(2,1)}), bf16[16,72,432]{2,1,0:T(8,128)(2,1)S(1)}, u32[]{:S(2)}, u32[]{:S(2)}) %all-to-all-start.4) | async-done | bytes 995360 | tf_op jit(solution)/shard_map/all_to_all | solution.py:352
  238.7 17.5 %all-gather = bf16[576,432]{1,0:T(8,128)(2,1)S(1)} all-gather(bf16[72,432]{1,0:T(8,128)(2,1)S(1)} %reduce_sum.37), channel_id=2, replica_groups=mesh['y'=4,'core'=2,'z'=4,'x'=4] {'y','core'}, dimensions={0}, use_global_device_ids=true | all-gather | bytes 559872 | tf_op jit(solution)/shard_map/all_gather | solution.py:354
  256.6 0.8 div.17
  257.4 0.9 copy.75
  258.3 1.0 div.19
  259.2 1.6 multiply_reduce_fusion
  260.8 1.3 dynamic-slice_divide_fusion
  (42 shorter events, 3.1 us)
Async XLA Ops:
  18.5 8.6 %copy-start.8 = (bf16[1,512,1152]{2,1,0:T(8,128)(2,1)S(1)}, bf16[1,512,1152]{2,1,0:T(8,128)(2,1)}, u32[]{:S(2)}) copy-start(bf16[1,512,1152]{2,1,0:T(8,128)(2,1)} %param.11) | copy-start | bytes 3538948
  18.5 26.0 %all-to-all-start = ((bf16[16,32,1152]{2,1,0:T(8,128)(2,1)}), bf16[16,32,1152]{2,1,0:T(8,128)(2,1)S(1)}, u32[]{:S(2)}, u32[]{:S(2)}) async-start(bf16[16,32,1152]{2,1,0:T(8,128)(2,1)} %bitcast.65), calls=%async_computation | async-start | bytes 2359296 | tf_op jit(solution)/shard_map/all_to_all | solution.py:294
  27.7 25.4 %copy-start = (bf16[1,512,1152]{1,2,0:T(8,128)(2,1)}, bf16[1,512,1152]{1,2,0:T(8,128)(2,1)S(1)}, u32[]{:S(2)}) copy-start(bf16[1,512,1152]{1,2,0:T(8,128)(2,1)S(1)} %copy.68) | copy-start | bytes 3538948
  44.5 1.0 copy-start.3
  47.9 9.8 %copy-start.9 = (s32[1,128]{1,0:T(1,128)S(1)}, s32[1,128]{1,0:T(1,128)}, u32[]{:S(2)}) copy-start(s32[1,128]{1,0:T(1,128)} %param.7) | copy-start | bytes 1540
  47.9 26.1 %all-to-all-start.1 = ((bf16[16,32,1152]{2,1,0:T(8,128)(2,1)}), bf16[16,32,1152]{2,1,0:T(8,128)(2,1)S(1)}, u32[]{:S(2)}, u32[]{:S(2)}) async-start(bf16[16,32,1152]{2,1,0:T(8,128)(2,1)} %pick_blocks.4), calls=%async_computation.1 | async-start | bytes 2359296 | tf_op jit(solution)/shard_map/all_to_all | solution.py:294
  53.1 148.3 %reduce-scatter.7.cloned.1.call-start = ((), (), s32[]{:S(2)}) async-start(), calls=%async_computation.7 | async-start | bytes 4478976
  53.2 17.9 %collective-permute-start.2 = (bf16[128,1152]{0,1:T(8,128)(2,1)S(1)}, bf16[128,1152]{0,1:T(8,128)(2,1)S(1)}, u32[]{:S(2)}, u32[]{:S(2)}) collective-permute-start(bf16[128,1152]{0,1:T(8,128)(2,1)S(1)} %get-tuple-element.48), channel_id=1, source_target_pairs={{0,1},{1,2},{2,3},{3,4},{4,5},{5,6},{6,7},{7,8},{8,9},{9,10},{10,1... | collective-permute-start | bytes 884744 | tf_op jit(solution)/shard_map/ppermute | solution.py:300
  56.5 16.7 %collective-permute-start.3 = (bf16[128,1152]{0,1:T(8,128)(2,1)S(1)}, bf16[128,1152]{0,1:T(8,128)(2,1)S(1)}, u32[]{:S(2)}, u32[]{:S(2)}) collective-permute-start(bf16[128,1152]{0,1:T(8,128)(2,1)S(1)} %get-tuple-element.49), channel_id=1, source_target_pairs={{1,0},{2,1},{3,2},{4,3},{5,4},{6,5},{7,6},{8,7},{9,8},{10,9},{11,1... | collective-permute-start | bytes 884744 | tf_op jit(solution)/shard_map/ppermute | solution.py:301
  74.0 1.0 copy-start.1
  77.4 17.1 %slice-start = ((s8[7962624]{0:T(1024)(128)(4,1)}), s8[4194304]{0:T(1024)(128)(4,1)S(1)}, s32[]{:S(2)}) async-start(s8[7962624]{0:T(1024)(128)(4,1)} %bitcast.72), calls=%async_computation.9 | async-start | bytes 8388608
  78.7 15.9 %collective-permute-start = (bf16[128,1152]{1,0:T(8,128)(2,1)S(1)}, bf16[128,1152]{1,0:T(8,128)(2,1)S(1)}, u32[]{:S(2)}, u32[]{:S(2)}) collective-permute-start(bf16[128,1152]{1,0:T(8,128)(2,1)S(1)} %get-tuple-element.50), channel_id=1, source_target_pairs={{0,1},{1,2},{2,3},{3,4},{4,5},{5,6},{6,7},{7,8},{8,9},{9,10},{10,1... | collective-permute-start | bytes 884744 | tf_op jit(solution)/shard_map/ppermute | solution.py:300
  82.9 11.7 %collective-permute-start.1 = (bf16[128,1152]{1,0:T(8,128)(2,1)S(1)}, bf16[128,1152]{1,0:T(8,128)(2,1)S(1)}, u32[]{:S(2)}, u32[]{:S(2)}) collective-permute-start(bf16[128,1152]{1,0:T(8,128)(2,1)S(1)} %get-tuple-element.51), channel_id=1, source_target_pairs={{1,0},{2,1},{3,2},{4,3},{5,4},{6,5},{7,6},{8,7},{9,8},{10,9},{11,1... | collective-permute-start | bytes 884744 | tf_op jit(solution)/shard_map/ppermute | solution.py:301
  84.2 10.4 %slice-start.1 = ((s8[7962624]{0:T(1024)(128)(4,1)}), s8[3768320]{0:T(1024)(128)(4,1)S(1)}, s32[]{:S(2)}) async-start(s8[7962624]{0:T(1024)(128)(4,1)} %bitcast.72), calls=%async_computation.10 | async-start | bytes 7536640
  99.4 22.4 %copy-start.5 = (bf16[4,128,1152]{2,1,0:T(8,128)(2,1)S(1)}, bf16[4,128,1152]{2,1,0:T(8,128)(2,1)}, u32[]{:S(2)}) copy-start(bf16[4,128,1152]{2,1,0:T(8,128)(2,1)} %pick_blocks.5) | copy-start | bytes 3538948
  127.7 81.5 %reduce-scatter.9.cloned.1.call-start = ((), (), s32[]{:S(2)}) async-start(), calls=%async_computation.8 | async-start | bytes 4478976
  155.9 1.5 copy-start.6
  155.9 2.1 copy-start.7
  197.6 19.7 %all-to-all-start.3 = ((bf16[16,32,1152]{2,1,0:T(8,128)(2,1)}), bf16[16,32,1152]{2,1,0:T(8,128)(2,1)S(1)}, u32[]{:S(2)}, u32[]{:S(2)}) async-start(bf16[16,32,1152]{2,1,0:T(8,128)(2,1)} %pick_blocks.7), calls=%async_computation.3 | async-start | bytes 2359296 | tf_op jit(solution)/shard_map/all_to_all | solution.py:294
  217.4 6.4 %copy-start.2 = (bf16[16,32,1152]{2,1,0:T(8,128)(2,1)}, bf16[16,32,1152]{2,1,0:T(8,128)(2,1)S(1)}, u32[]{:S(2)}) copy-start(bf16[16,32,1152]{2,1,0:T(8,128)(2,1)S(1)} %all-to-all-done.3) | copy-start | bytes 3538948
  217.4 21.1 %all-to-all-start.4 = ((bf16[16,72,432]{2,1,0:T(8,128)(2,1)}), bf16[16,72,432]{2,1,0:T(8,128)(2,1)S(1)}, u32[]{:S(2)}, u32[]{:S(2)}) async-start(bf16[16,72,432]{2,1,0:T(8,128)(2,1)} %bitcast.27), calls=%async_computation.4 | async-start | bytes 2359296 | tf_op jit(solution)/shard_map/all_to_all | solution.py:352
  259.2 2.9 %copy-start.4 = (f32[72,3456]{1,0:T(8,128)}, f32[72,3456]{1,0:T(8,128)S(1)}, u32[]{:S(2)}) copy-start(f32[72,3456]{1,0:T(8,128)S(1)} %div.19) | copy-start | bytes 2985988
Sparse Core Ops, SparseCore 0:
  127.8 40.1 reduce-scatter.6
  170.5 38.6 reduce-scatter.8

commit v3 on v2

--- a/solution.py
+++ b/solution.py
@@ -82,13 +82,17 @@
     d_ref[...] = d_s[...].astype(BF16)
 
 
-def attention_call(ids, own, halo, g_own, g_halo, first_pair=0, pairs=HEADS // 2):
+def attention_call(ids, own, halo, g_own, g_halo, first_pair, inner):
     rows, rim = own.shape[1], halo.shape[1]
     total, blocks = rows + rim, rows // BLK
     per_part = HEADS // 2
+    pairs = 2 * inner
 
     def spec(width, part):
-        return pl.BlockSpec((PAIR, width), lambda i: (part * per_part + first_pair + i, 0))
+        return pl.BlockSpec(
+            (PAIR, width),
+            lambda i: (part * per_part + first_pair + i // inner * (per_part // 2) + i % inner, 0),
+        )
 
     return pl.pallas_call(
         attention_kernel,
@@ -275,7 +279,47 @@
     )(index, grads, blocks, gain[None])
 
 
-GROUPS = 2
+def weight_kernel(place_ref, keep_a, keep_b, got_a, got_b, rows_ref, other_ref, out_ref):
+    for part, (keep, got) in enumerate(((keep_a, got_a), (keep_b, got_b))):
+
+        @pl.when(pl.program_id(0) // 2 == part)
+        def _():
+            out_ref[0] = (nn(keep[0], rows_ref[...]) + nn(got[...], other_ref[...])).astype(BF16)
+
+
+def weight_product(place, keep, got, rows, other):
+    count, width = rows.shape
+    block = 3 * HD
+    twice = [2 * (keep[0] is keep[1]), 2 * (got[0] is got[1])]
+
+    def first(i):
+        return jnp.minimum(i, 1)
+
+    def second(i, skip):
+        return jnp.maximum(i - 2, 0) + skip
+
+    whole = pl.BlockSpec((count, width), lambda i, place: (0, 0))
+    return pl.pallas_call(
+        weight_kernel,
+        grid_spec=pltpu.PrefetchScalarGridSpec(
+            num_scalar_prefetch=1,
+            grid=(4,),
+            in_specs=[
+                pl.BlockSpec((1, block, count), lambda i, place: (place[0], first(i), 0)),
+                pl.BlockSpec((1, block, count), lambda i, place: (place[0], second(i, twice[0]), 0)),
+                pl.BlockSpec((block, count), lambda i, place: (first(i), 0)),
+                pl.BlockSpec((block, count), lambda i, place: (second(i, twice[1]), 0)),
+                whole,
+                whole,
+            ],
+            out_specs=pl.BlockSpec((1, block, width), lambda i, place: (lax.rem(i + 4 - place[1], 4), 0, 0)),
+        ),
+        out_shape=jax.ShapeDtypeStruct((4, block, width), BF16),
+        cost_estimate=pl.CostEstimate(
+            flops=16 * block * count * width, bytes_accessed=8 * (block + count) * width, transcendentals=0
+        ),
+        name="weight_product",
+    )(place, *keep, *got, rows, other)
 
 
 def local(loader_rows, lengths, block_order, norm_gain, qkv_weight, upstream_grad):
@@ -324,19 +368,62 @@
     inside = (positions >= 0) & (positions < block_total * BLK)
     ids = jnp.where(inside, counted, -1)
 
-    pairs = HEADS // 2 // GROUPS
-    attended, grads, shares = [], [], []
-    for group in range(GROUPS):
+    core = lax.axis_index("core")
+    place = jnp.stack([core, lax.axis_index("y")])
+    swap = [(0, 1), (1, 0)]
+    scaled_other = lax.ppermute(scaled, "core", swap)
+
+    def attend(ids, first_pair, inner):
         out, grad = attention_call(
-            ids, qkv_own, qkv_halo, upstream_own, upstream_halo, group * pairs, pairs
+            ids, qkv_own, qkv_halo, upstream_own, upstream_halo, first_pair, inner
         )
-        weight_local = nn(grad, scaled).astype(BF16)
-        shares.append(lax.psum_scatter(weight_local, DP, scatter_dimension=0, tiled=True))
-        attended.append(out)
-        grads.append(grad)
-    attention = jnp.concatenate(attended, axis=0).T[None]
-    grad_cols = jnp.concatenate(grads, axis=0).reshape(HEADS, 3, HD, row_count)
+        return out.reshape(2, inner * PAIR, row_count), grad.reshape(2, inner * 3 * PAIR, row_count)
+
+    def to_other(grad):
+        return lax.ppermute(lax.dynamic_index_in_dim(grad, 1 - core, 0, False), "core", swap)
+
+    along = [(i, (i + 1) % 4) for i in range(4)]
+    against = [(j, i) for i, j in along]
+    cut = 112
+
+    def over_packs(product):
+        own, near, far, last = (product[k] for k in range(4))
+        far_up = lax.ppermute(far[:cut], "y", along)
+        far_down = lax.ppermute(far[cut:], "y", against)
+        near = jnp.concatenate(
+            [(near[:cut].astype(F32) + far_up.astype(F32)).astype(BF16), near[cut:]], axis=0
+        )
+        last = jnp.concatenate(
+            [last[:cut], (last[cut:].astype(F32) + far_down.astype(F32)).astype(BF16)], axis=0
+        )
+        up, down = lax.ppermute(near, "y", along), lax.ppermute(last, "y", against)
+        return (own.astype(F32) + up.astype(F32) + down.astype(F32)).astype(BF16)
+
+    share = model_width // seq_count
+
+    def over_rows(part):
+        parts = part.T.reshape(seq_count, share, part.shape[0])
+        parts = lax.all_to_all(parts, SEQ, split_axis=0, concat_axis=0, tiled=True)
+        return jnp.sum(parts.astype(F32), axis=0).astype(BF16)
+
+    out_a, grad_a = attend(ids, 0, 2)
+    got_a = to_other(grad_a)
+    out_b, grad_b = attend(ids, 2, 1)
+    product_a = weight_product(place, (grad_a, grad_a), (got_a, got_a), scaled, scaled_other)
+    ids, product_a = lax.optimization_barrier((ids, product_a))
+    sum_a = over_packs(product_a)
+    got_b = to_other(grad_b)
+    out_c, grad_c = attend(ids, 3, 1)
+    got_c = to_other(grad_c)
+    product_b = weight_product(place, (grad_b, grad_c), (got_b, got_c), scaled, scaled_other)
+
+    sum_b = over_packs(product_b)
+
+    attention = jnp.concatenate([out_a, out_b, out_c], axis=1)
+    attention = attention.reshape(model_width, row_count).T[None]
+    grad_cols = jnp.concatenate([grad_a, grad_b, grad_c], axis=1).reshape(HEADS, 3, HD, row_count)
     grad_cols = grad_cols.transpose(1, 0, 2, 3).reshape(3 * model_width, row_count)
+    grad_cols, product_b = lax.optimization_barrier((grad_cols, product_b))
     input_grad = lax.dot_general(
         grad_cols, qkv_weight, (((0,), (1,)), ((), ())), preferred_element_type=F32
     ).astype(BF16)
@@ -346,15 +433,10 @@
         back_last, returned.reshape(per_device, BLK, model_width), loader_blocks, norm_gain
     ).reshape(1, row_count, model_width)
 
-    share = model_width // seq_count
-    per_pack = 3 * model_width // pack_count
-    partial = jnp.concatenate(shares, axis=0).T.reshape(seq_count, share, per_pack)
-    partial = lax.all_to_all(partial, SEQ, split_axis=0, concat_axis=0, tiled=True)
-    summed = jnp.sum(partial.astype(F32), axis=0).astype(BF16)
+    summed = over_rows(jnp.concatenate([sum_a, sum_b], axis=0))
     weight_cols = lax.all_gather(summed, DP, axis=0)
-    heads = HEADS // GROUPS // pack_count
-    weight_cols = weight_cols.reshape(pack_count, share, GROUPS, heads, 3, HD)
-    weight_grad = weight_cols.transpose(1, 4, 2, 0, 3, 5).reshape(share, 3 * model_width)
+    weight_cols = weight_cols.reshape(4, 2, share, 2, 3, HD)
+    weight_grad = weight_cols.transpose(2, 4, 1, 3, 0, 5).reshape(share, 3 * model_width)
     weight_grad = weight_grad.astype(F32) / pack_count
     weight_rows = lax.dynamic_slice_in_dim(qkv_weight, my_index * share, share, 0).astype(F32)
     gain_rows = lax.dynamic_slice_in_dim(norm_gain, my_index * share, share, 0)

time: 270 us -> 294 us (1.089); the launches traced: 269 us -> 290 us
  blocking collectives: 43.3 us -> 17.5 us
  starting transfers between devices: 32.6 us -> 54.9 us
  local copies, waits for them, and re-layouts: 14.6 us -> 32.1 us
  Pallas kernels: 69.2 us -> 85.9 us
  between operations: 14.3 us -> 1.26 us
  matrix products: 35.5 us -> 25.9 us
  other arithmetic: 9.15 us -> 17.7 us
  waiting for transfers between devices: 50.2 us -> 54.4 us
    all_to_all x1 -> x0, blocking collectives: 25.8 us -> none  [exchange(): return lax.all_to_all(x, SEQ, split_axis=0, concat_axis=0, tiled=True)]
    pallas_call x0 -> x2, Pallas kernels: none -> 14.3 us  [weight_product(): pl.pallas_call(weight_kernel, grid_spec=pltpu.PrefetchScalarGridSpec(num_...]
    ppermute x0 -> x12, starting transfers between devices: none -> 12 us  [the longest x2 4.21 us: over_packs(): far_down = lax.ppermute(far[cut:], 'y', against)]
    dot_general x2 -> x0, matrix products: 11.8 us -> none  [nn(): lax.dot_general(a, b, (((1,), (0,)), ((), ())), preferred_element_type=F32)]
    ppermute x0 -> x12, waiting for transfers between devices: none -> 11 us  [the longest x2 7.51 us: over_packs(): lax.ppermute(last, 'y', against)]
    all_to_all x3 -> x4, starting transfers between devices: 17.4 us -> 26.5 us  [exchange(): return lax.all_to_all(x, SEQ, split_axis=0, concat_axis=0, tiled=True)]
    slice x0 -> x4, local copies, waits for them, and re-layouts: none -> 7.32 us  [the longest x2 3.69 us: over_packs(): near[cut:]]
    convert_element_type x0 -> x6, other arithmetic: none -> 6.9 us  [the longest x2 2.59 us: over_packs(): return (own.astype(F32) + up.astype(F32) + down.astype(F32)).astype(BF16)]
  transfers between devices with their start and end apart: 10 -> 21, of which waited for: 6 -> 6; matrix products, arithmetic and copies ran while one was open for 13% -> 24% of each run, Pallas kernels for 12% -> 23%
where the time goes in v3:
time: 294 us; the launch traced here: 290 us
  Pallas kernels  85.9 us (29%)
  starting transfers between devices  54.9 us (19%)
  waiting for transfers between devices  54.4 us (19%)
  local copies, waits for them, and re-layouts  32.1 us (11%)
  matrix products  25.9 us (9%)
  other arithmetic  17.7 us (6%)
  blocking collectives  17.5 us (6%)
    pallas_call x3, Pallas kernels, attention_call(): pl.pallas_call(attention_kernel, grid=(pairs,), in_specs=[pl.BlockSpec((t...  46.8 us
    all_to_all x4, starting transfers between devices, exchange(): return lax.all_to_all(x, SEQ, split_axis=0, concat_axis=0, tiled=True)  26.5 us
    all_gather x1, blocking collectives, local(): weight_cols = lax.all_gather(summed, DP, axis=0)  17.5 us
    all_to_all x4, waiting for transfers between devices, exchange(): return lax.all_to_all(x, SEQ, split_axis=0, concat_axis=0, tiled=True)  16.8 us
    dot_general x2, matrix products, project(): lax.dot_general(qkv_weight, rows, (((0,), (1,)), ((), ())), preferred_ele...  15.7 us
    pallas_call x2, Pallas kernels, weight_product(): pl.pallas_call(weight_kernel, grid_spec=pltpu.PrefetchScalarGridSpec(num_...  14.3 us
    all_to_all x1, waiting for transfers between devices, over_rows(): parts = lax.all_to_all(parts, SEQ, split_axis=0, concat_axis=0, tiled=True)  13.3 us
    ppermute x2, waiting for transfers between devices, halo(): before = lax.ppermute(x[row_count - BLK:], SEQ, up)  11.1 us
  transfers between devices with their start and end apart: 21, of which 6 were waited for; matrix products, arithmetic and copies ran while one was open for 24% of the time, Pallas kernels for 23%

profile of v3, /device:TPU:1, one launch (start us, length us, event | category | flops | bytes accessed | tf_op | source)
XLA Modules:
  0.0 289.7 jit_solution(15190268006828349370)
XLA Ops:
  1.9 5.4 %route_blocks.1 = (s32[4]{0:T(128)}, s32[16]{0:T(128)}, s32[4]{0:T(128)}, s32[4]{0:T(128)}, s32[16]{0:T(128)}, /*index=5*/s32[4]{0:T(128)}) custom-call(s32[1]{0:T(128)} %bitcast.1.me_ref, s32[64]{0:T(128)} %bitcast.137), custom_call_target="tpu_custom_call" | custom-call | tf_op jit(solution)/shard_map/route_blocks/pallas_call | solution.py:196
  7.4 4.7 %norm_blocks.1 = bf16[4,128,1152]{2,1,0:T(8,128)(2,1)} custom-call(s32[4]{0:T(128)} %get-tuple-element.21.index_ref, bf16[4,128,1152]{2,1,0:T(8,128)(2,1)} %bitcast.115, f32[1,1152]{1,0:T(1,128)} %broadcast_in_dim.33.gain_ref), custom_call_target="tpu_custom_call" | custom-call | tf_op jit(solution)/shard_map/norm_blocks/pallas_call | solution.py:238
  12.1 8.4 %all-to-all-start = ((bf16[16,32,1152]{2,1,0:T(8,128)(2,1)}), bf16[16,32,1152]{2,1,0:T(8,128)(2,1)S(1)}, u32[]{:S(2)}, u32[]{:S(2)}) async-start(bf16[16,32,1152]{2,1,0:T(8,128)(2,1)} %bitcast.120), calls=%async_computation | async-start | bytes 2359296 | tf_op jit(solution)/shard_map/all_to_all | solution.py:338
  21.1 16.8 %all-to-all-done.source_ref = bf16[16,32,1152]{2,1,0:T(8,128)(2,1)S(1)} async-done(((bf16[16,32,1152]{2,1,0:T(8,128)(2,1)}), bf16[16,32,1152]{2,1,0:T(8,128)(2,1)S(1)}, u32[]{:S(2)}, u32[]{:S(2)}) %all-to-all-start) | async-done | bytes 1179680 | tf_op jit(solution)/shard_map/all_to_all | solution.py:338
  39.0 2.4 pick_blocks.4
  41.3 5.1 %all-to-all-start.1 = ((bf16[16,32,1152]{2,1,0:T(8,128)(2,1)}), bf16[16,32,1152]{2,1,0:T(8,128)(2,1)S(1)}, u32[]{:S(2)}, u32[]{:S(2)}) async-start(bf16[16,32,1152]{2,1,0:T(8,128)(2,1)} %pick_blocks.4), calls=%async_computation.1 | async-start | bytes 2359296 | tf_op jit(solution)/shard_map/all_to_all | solution.py:338
  46.6 3.3 %collective-permute-start.2 = (bf16[128,1152]{0,1:T(8,128)(2,1)S(1)}, bf16[128,1152]{0,1:T(8,128)(2,1)S(1)}, u32[]{:S(2)}, u32[]{:S(2)}) collective-permute-start(bf16[128,1152]{0,1:T(8,128)(2,1)S(1)} %get-tuple-element.62), channel_id=1, source_target_pairs={{0,1},{1,2},{2,3},{3,4},{4,5},{5,6},{6,7},{7,8},{8,9},{9,10},{10,1... | collective-permute-start | bytes 884744 | tf_op jit(solution)/shard_map/ppermute | solution.py:344
  53.4 11.1 %collective-permute-done.2 = bf16[128,1152]{0,1:T(8,128)(2,1)S(1)} collective-permute-done((bf16[128,1152]{0,1:T(8,128)(2,1)S(1)}, bf16[128,1152]{0,1:T(8,128)(2,1)S(1)}, u32[]{:S(2)}, u32[]{:S(2)}) %collective-permute-start.2) | collective-permute-done | bytes 294944 | tf_op jit(solution)/shard_map/ppermute | solution.py:344
  64.5 2.1 collective-permute-done.3
  68.5 2.4 pick_blocks.5
  72.0 4.1 %collective-permute-start = (bf16[128,1152]{1,0:T(8,128)(2,1)S(1)}, bf16[128,1152]{1,0:T(8,128)(2,1)S(1)}, u32[]{:S(2)}, u32[]{:S(2)}) collective-permute-start(bf16[128,1152]{1,0:T(8,128)(2,1)S(1)} %get-tuple-element.64), channel_id=1, source_target_pairs={{0,1},{1,2},{2,3},{3,4},{4,5},{5,6},{6,7},{7,8},{8,9},{9,10},{10,1... | collective-permute-start | bytes 884744 | tf_op jit(solution)/shard_map/ppermute | solution.py:344
  77.4 1.6 collective-permute-start.5
  79.0 10.8 %fusion.q_ref.k_ref.v_ref = bf16[3456,512]{1,0:T(8,128)(2,1)} fusion(bf16[512,1152]{1,0:T(8,128)(2,1)} %bitcast.111, bf16[1152,3456]{1,0:T(8,128)(2,1)} %param.10), kind=kOutput, calls=%fused_computation.1 | convolution fusion | flops 4078632960 | bytes 12681216 | tf_op jit(solution)/shard_map/dot_general | solution.py:359
  89.9 4.8 %fusion.1.qh_ref.kh_ref.vh_ref = bf16[3456,256]{1,0:T(8,128)(2,1)} fusion(bf16[1152,3456]{1,0:T(8,128)(2,1)S(1)} %bitcast.135, bf16[128,1152]{1,0:T(8,128)(2,1)S(1)} %collective-permute-done.1, bf16[128,1152]{1,0:T(8,128)(2,1)S(1)} %collective-permute-done), kind=kOutput, calls=%fused_computation.3 | convolution fusion | flops 2040496128 | bytes 10321920 | tf_op jit(solution)/shard_map/dot_general | solution.py:359
  94.7 22.2 %packed_attention.3 = (bf16[576,512]{1,0:T(8,128)(2,1)}, bf16[1728,512]{1,0:T(8,128)(2,1)}) custom-call(s32[768,1]{1,0:T(8,128)} %reshape_select_fusion.col_ref, s32[1,768]{1,0:T(1,128)} %and_select_fusion.row_ref, bf16[3456,512]{1,0:T(8,128)(2,1)} %fusion.q_ref.k_ref.v_ref, bf16[3456,512]{1,0:T(8,128)(2,1)} %fusion.q_ref.k_ref.v_ref, ...), custom_call_target="tpu_custom_call" | custom-call | flops 1811939328 | bytes 5898240 | tf_op jit(solution)/shard_map/packed_attention/pallas_call | solution.py:97
  119.1 12.3 %packed_attention.4 = (bf16[288,512]{1,0:T(8,128)(2,1)}, bf16[864,512]{1,0:T(8,128)(2,1)}) custom-call(s32[768,1]{1,0:T(8,128)} %reshape_select_fusion.col_ref, s32[1,768]{1,0:T(1,128)} %and_select_fusion.row_ref, bf16[3456,512]{1,0:T(8,128)(2,1)} %fusion.q_ref.k_ref.v_ref, bf16[3456,512]{1,0:T(8,128)(2,1)} %fusion.q_ref.k_ref.v_ref, ...), custom_call_target="tpu_custom_call" | custom-call | flops 905969664 | bytes 2949120 | tf_op jit(solution)/shard_map/packed_attention/pallas_call | solution.py:97
  131.3 1.8 dynamic-slice_bitcast_fusion.2
  135.6 7.2 %weight_product.2 = bf16[4,216,1152]{2,1,0:T(8,128)(2,1)} custom-call(s32[2]{0:T(128)} %pad_add_fusion.place_ref, bf16[2,864,512]{2,1,0:T(8,128)(2,1)} %bitcast.106, bf16[2,864,512]{2,1,0:T(8,128)(2,1)} %bitcast.107, bf16[864,512]{1,0:T(8,128)(2,1)} %copy-done.7, bf16[864,512]{1,0:T(8,128)(2,1)} %copy-done.7, bf16[512,1152]{1,0:T(8,128)(2,1)} %bitcast.112, ...), custom_call_target="tpu_custom_call" | custom-call | flops 2038431744 | bytes 6709248 | tf_op jit(solution)/shard_map/weight_product/pallas_call | solution.py:302
  142.7 1.8 slice_bitcast_fusion.9
  144.6 1.8 slice_bitcast_fusion.14
  149.2 1.5 collective-permute-start.10
  150.7 12.4 %packed_attention.5 = (bf16[288,512]{1,0:T(8,128)(2,1)}, bf16[864,512]{1,0:T(8,128)(2,1)}) custom-call(s32[768,1]{1,0:T(8,128)} %broadcast_in_dim.38.col_ref, s32[1,768]{1,0:T(1,128)} %broadcast_in_dim.36.row_ref, bf16[3456,512]{1,0:T(8,128)(2,1)} %fusion.q_ref.k_ref.v_ref, bf16[3456,512]{1,0:T(8,128)(2,1)} %fusion.q_ref.k_ref.v_ref, ...), custom_call_target="tpu_custom_call" | custom-call | flops 905969664 | bytes 2949120 | tf_op jit(solution)/shard_map/packed_attention/pallas_call | solution.py:97
  165.9 2.0 copy.74
  170.0 1.6 collective-permute-start.11
  173.9 7.2 %weight_product.3 = bf16[4,216,1152]{2,1,0:T(8,128)(2,1)} custom-call(s32[2]{0:T(128)} %pad_add_fusion.place_ref, bf16[2,432,512]{2,1,0:T(8,128)(2,1)} %bitcast.124, bf16[2,432,512]{2,1,0:T(8,128)(2,1)} %bitcast.128, bf16[432,512]{1,0:T(8,128)(2,1)} %collective-permute-done.6.got_a, bf16[432,512]{1,0:T(8,128)(2,1)} %collective-permute-done.7.got_b, ...), custom_call_target="tpu_custom_call" | custom-call | flops 2038431744 | bytes 6709248 | tf_op jit(solution)/shard_map/weight_product/pallas_call | solution.py:302
  181.1 1.8 slice_bitcast_fusion.6
  182.9 1.9 slice_bitcast_fusion.12
  184.8 2.7 collective-permute-start.14
  187.4 10.3 %convolution_convert_fusion.2 = bf16[512,1152]{1,0:T(8,128)(2,1)} fusion(bf16[3456,512]{1,0:T(8,128)(2,1)} %bitcast.122, bf16[1152,3456]{1,0:T(8,128)(2,1)} %param.10), kind=kOutput, calls=%fused_computation.5 | convolution fusion | flops 4077453312 | bytes 12681216 | tf_op jit(solution)/shard_map/dot_general | solution.py:427
  197.7 2.4 pick_blocks.6
  200.1 8.6 %all-to-all-start.2 = ((bf16[16,32,1152]{2,1,0:T(8,128)(2,1)}), bf16[16,32,1152]{2,1,0:T(8,128)(2,1)S(1)}, u32[]{:S(2)}, u32[]{:S(2)}) async-start(bf16[16,32,1152]{2,1,0:T(8,128)(2,1)} %bitcast.118), calls=%async_computation.2 | async-start | bytes 2359296 | tf_op jit(solution)/shard_map/all_to_all | solution.py:338
  209.9 1.5 collective-permute-start.15
  212.7 1.4 fusion.5
  214.1 7.5 %collective-permute-done.15 = bf16[216,1152]{1,0:T(8,128)(2,1)S(1)} collective-permute-done((bf16[216,1152]{1,0:T(8,128)(2,1)S(1)}, bf16[216,1152]{1,0:T(8,128)(2,1)S(1)}, u32[]{:S(2)}, u32[]{:S(2)}) %collective-permute-start.15) | collective-permute-done | bytes 497696 | tf_op jit(solution)/shard_map/ppermute | solution.py:399
  221.6 3.5 %collective-permute-done.13 = bf16[216,1152]{1,0:T(8,128)(2,1)S(1)} collective-permute-done((bf16[216,1152]{1,0:T(8,128)(2,1)S(1)}, bf16[216,1152]{1,0:T(8,128)(2,1)S(1)}, u32[]{:S(2)}, u32[]{:S(2)}) %collective-permute-start.13) | collective-permute-done | bytes 497696 | tf_op jit(solution)/shard_map/ppermute | solution.py:399
  226.4 1.6 copy.75
  228.0 6.4 %all-to-all-start.4 = ((bf16[16,72,432]{2,1,0:T(8,128)(2,1)}), bf16[16,72,432]{2,1,0:T(8,128)(2,1)S(1)}, u32[]{:S(2)}, u32[]{:S(2)}) async-start(bf16[16,72,432]{2,1,0:T(8,128)(2,1)} %bitcast.119), calls=%async_computation.4 | async-start | bytes 2359296 | tf_op jit(solution)/shard_map/all_to_all | solution.py:406
  234.4 2.4 pick_blocks.7
  236.9 13.3 %all-to-all-done.4 = bf16[16,72,432]{2,1,0:T(8,128)(2,1)S(1)} async-done(((bf16[16,72,432]{2,1,0:T(8,128)(2,1)}), bf16[16,72,432]{2,1,0:T(8,128)(2,1)S(1)}, u32[]{:S(2)}, u32[]{:S(2)}) %all-to-all-start.4) | async-done | bytes 995360 | tf_op jit(solution)/shard_map/all_to_all | solution.py:406
  250.2 4.4 %all-to-all-start.3 = ((bf16[16,32,1152]{2,1,0:T(8,128)(2,1)}), bf16[16,32,1152]{2,1,0:T(8,128)(2,1)}, u32[]{:S(2)}, u32[]{:S(2)}) async-start(bf16[16,32,1152]{2,1,0:T(8,128)(2,1)} %pick_blocks.7), calls=%async_computation.3 | async-start | bytes 2359296 | tf_op jit(solution)/shard_map/all_to_all | solution.py:338
  255.7 1.4 copy.78
  257.3 17.5 %all-gather = bf16[576,432]{1,0:T(8,128)(2,1)S(1)} all-gather(bf16[72,432]{1,0:T(8,128)(2,1)S(1)} %reduce_sum.37), channel_id=2, replica_groups=mesh['y'=4,'core'=2,'z'=4,'x'=4] {'y','core'}, dimensions={0}, use_global_device_ids=true | all-gather | bytes 559872 | tf_op jit(solution)/shard_map/all_gather | solution.py:437
  275.1 3.2 %div.17 = f32[4,2,72,2,3,72]{2,1,0,5,4,3:T(2,128)S(1)} reshape(f32[576,432]{0,1:T(8,128)S(1)} %convert_multiply_fusion) | data formatting | bytes 1990656 | tf_op jit(solution)/shard_map/div | solution.py:440
  278.3 1.3 copy.77
  279.6 1.9 div.19
  281.6 1.6 multiply_reduce_fusion
  283.2 1.3 dynamic-slice_divide_fusion
  284.5 5.0 %norm_back.1 = bf16[4,128,1152]{2,1,0:T(8,128)(2,1)} custom-call(s32[4]{0:T(128)} %get-tuple-element.27.index_ref, bf16[4,128,1152]{2,1,0:T(8,128)(2,1)} %bitcast.36.grads_ref, bf16[4,128,1152]{2,1,0:T(8,128)(2,1)} %bitcast.116, f32[1,1152]{1,0:T(1,128)} %broadcast_in_dim.33.gain_ref), custom_call_target="tpu_custom_call" | custom-call | tf_op jit(solution)/shard_map/norm_back/pallas_call | solution.py:265
  (92 shorter events, 30.7 us)
Async XLA Ops:
  7.3 13.2 %copy-start.9 = (bf16[1,512,1152]{2,1,0:T(8,128)(2,1)S(1)}, bf16[1,512,1152]{2,1,0:T(8,128)(2,1)}, u32[]{:S(2)}) copy-start(bf16[1,512,1152]{2,1,0:T(8,128)(2,1)} %param.11) | copy-start | bytes 3538948
  12.1 25.9 %all-to-all-start = ((bf16[16,32,1152]{2,1,0:T(8,128)(2,1)}), bf16[16,32,1152]{2,1,0:T(8,128)(2,1)S(1)}, u32[]{:S(2)}, u32[]{:S(2)}) async-start(bf16[16,32,1152]{2,1,0:T(8,128)(2,1)} %bitcast.120), calls=%async_computation | async-start | bytes 2359296 | tf_op jit(solution)/shard_map/all_to_all | solution.py:338
  21.1 25.4 %copy-start = (bf16[1,512,1152]{1,2,0:T(8,128)(2,1)}, bf16[1,512,1152]{1,2,0:T(8,128)(2,1)S(1)}, u32[]{:S(2)}) copy-start(bf16[1,512,1152]{1,2,0:T(8,128)(2,1)S(1)} %copy.70) | copy-start | bytes 3538948
  37.9 1.0 copy-start.5
  41.3 9.8 %copy-start.14 = (s32[1,128]{1,0:T(1,128)S(1)}, s32[1,128]{1,0:T(1,128)}, u32[]{:S(2)}) copy-start(s32[1,128]{1,0:T(1,128)} %param.7) | copy-start | bytes 1540
  41.3 26.1 %all-to-all-start.1 = ((bf16[16,32,1152]{2,1,0:T(8,128)(2,1)}), bf16[16,32,1152]{2,1,0:T(8,128)(2,1)S(1)}, u32[]{:S(2)}, u32[]{:S(2)}) async-start(bf16[16,32,1152]{2,1,0:T(8,128)(2,1)} %pick_blocks.4), calls=%async_computation.1 | async-start | bytes 2359296 | tf_op jit(solution)/shard_map/all_to_all | solution.py:338
  46.6 17.9 %collective-permute-start.2 = (bf16[128,1152]{0,1:T(8,128)(2,1)S(1)}, bf16[128,1152]{0,1:T(8,128)(2,1)S(1)}, u32[]{:S(2)}, u32[]{:S(2)}) collective-permute-start(bf16[128,1152]{0,1:T(8,128)(2,1)S(1)} %get-tuple-element.62), channel_id=1, source_target_pairs={{0,1},{1,2},{2,3},{3,4},{4,5},{5,6},{6,7},{7,8},{8,9},{9,10},{10,1... | collective-permute-start | bytes 884744 | tf_op jit(solution)/shard_map/ppermute | solution.py:344
  49.8 16.7 %collective-permute-start.3 = (bf16[128,1152]{0,1:T(8,128)(2,1)S(1)}, bf16[128,1152]{0,1:T(8,128)(2,1)S(1)}, u32[]{:S(2)}, u32[]{:S(2)}) collective-permute-start(bf16[128,1152]{0,1:T(8,128)(2,1)S(1)} %get-tuple-element.63), channel_id=1, source_target_pairs={{1,0},{2,1},{3,2},{4,3},{5,4},{6,5},{7,6},{8,7},{9,8},{10,9},{11,1... | collective-permute-start | bytes 884744 | tf_op jit(solution)/shard_map/ppermute | solution.py:345
  67.5 1.0 copy-start.4
  72.0 17.9 %collective-permute-start = (bf16[128,1152]{1,0:T(8,128)(2,1)S(1)}, bf16[128,1152]{1,0:T(8,128)(2,1)S(1)}, u32[]{:S(2)}, u32[]{:S(2)}) collective-permute-start(bf16[128,1152]{1,0:T(8,128)(2,1)S(1)} %get-tuple-element.64), channel_id=1, source_target_pairs={{0,1},{1,2},{2,3},{3,4},{4,5},{5,6},{6,7},{7,8},{8,9},{9,10},{10,1... | collective-permute-start | bytes 884744 | tf_op jit(solution)/shard_map/ppermute | solution.py:344
  76.1 13.8 %collective-permute-start.1 = (bf16[128,1152]{1,0:T(8,128)(2,1)S(1)}, bf16[128,1152]{1,0:T(8,128)(2,1)S(1)}, u32[]{:S(2)}, u32[]{:S(2)}) collective-permute-start(bf16[128,1152]{1,0:T(8,128)(2,1)S(1)} %get-tuple-element.65), channel_id=1, source_target_pairs={{1,0},{2,1},{3,2},{4,3},{5,4},{6,5},{7,6},{8,7},{9,8},{10,9},{11,1... | collective-permute-start | bytes 884744 | tf_op jit(solution)/shard_map/ppermute | solution.py:345
  77.4 12.5 %slice-start = ((s8[7962624]{0:T(1024)(128)(4,1)}), s8[4194304]{0:T(1024)(128)(4,1)S(1)}, s32[]{:S(2)}) async-start(s8[7962624]{0:T(1024)(128)(4,1)} %bitcast.134), calls=%async_computation.5 | async-start | bytes 8388608
  77.4 12.5 %slice-start.1 = ((s8[7962624]{0:T(1024)(128)(4,1)}), s8[3768320]{0:T(1024)(128)(4,1)S(1)}, s32[]{:S(2)}) async-start(s8[7962624]{0:T(1024)(128)(4,1)} %bitcast.134), calls=%async_computation.6 | async-start | bytes 7536640
  77.4 56.2 %collective-permute-start.5 = (bf16[512,1152]{1,0:T(8,128)(2,1)}, bf16[512,1152]{1,0:T(8,128)(2,1)S(1)}, u32[]{:S(2)}, u32[]{:S(2)}) collective-permute-start(bf16[512,1152]{1,0:T(8,128)(2,1)} %bitcast.110), channel_id=1, source_target_pairs={{0,16},{16,0},{1,17},{17,1},{2,18},{18,2},{3,19},{19,3},{4,20},{20... | collective-permute-start | bytes 3538952 | tf_op jit(solution)/shard_map/ppermute | solution.py:374
  118.2 15.5 %collective-permute-start.4 = (bf16[864,512]{1,0:T(8,128)(2,1)S(1)}, bf16[864,512]{1,0:T(8,128)(2,1)S(1)}, u32[]{:S(2)}, u32[]{:S(2)}) collective-permute-start(bf16[864,512]{1,0:T(8,128)(2,1)S(1)} %dynamic-slice_bitcast_fusion), channel_id=1, source_target_pairs={{0,16},{16,0},{1,17},{17,1},{2,18},{18,2},{3,19},{19,3},{4,20},{20... | collective-permute-start | bytes 2654216 | tf_op jit(solution)/shard_map/ppermute | solution.py:383
  133.2 40.7 %collective-permute-start.6 = (bf16[432,512]{1,0:T(8,128)(2,1)}, bf16[432,512]{1,0:T(8,128)(2,1)}, u32[]{:S(2)}, u32[]{:S(2)}) collective-permute-start(bf16[432,512]{1,0:T(8,128)(2,1)} %dynamic-slice_bitcast_fusion.2), channel_id=1, source_target_pairs={{0,16},{16,0},{1,17},{17,1},{2,18},{18,2},{3,19},{19,3},{4,20},{20... | collective-permute-start | bytes 1327112 | tf_op jit(solution)/shard_map/ppermute | solution.py:383
  133.6 0.9 copy-start.7
  134.6 1.0 copy-start.10
  147.9 23.8 %collective-permute-start.8 = (bf16[112,1152]{1,0:T(8,128)(2,1)}, bf16[112,1152]{1,0:T(8,128)(2,1)}, u32[]{:S(2)}, u32[]{:S(2)}) collective-permute-start(bf16[112,1152]{1,0:T(8,128)(2,1)} %get-tuple-element.54), channel_id=1, source_target_pairs={{0,32},{32,64},{64,96},{96,0},{1,33},{33,65},{65,97},{97,1},{2,34}... | collective-permute-start | bytes 774152 | tf_op jit(solution)/shard_map/ppermute | solution.py:391
  149.2 15.5 %copy-start.8 = (bf16[864,512]{1,0:T(8,128)(2,1)S(1)}, bf16[864,512]{1,0:T(8,128)(2,1)}, u32[]{:S(2)}) copy-start(bf16[864,512]{1,0:T(8,128)(2,1)} %get-tuple-element.30) | copy-start | bytes 2654212
  149.2 18.8 %collective-permute-start.10 = (bf16[104,1152]{1,0:T(8,128)(2,1)}, bf16[104,1152]{1,0:T(8,128)(2,1)}, u32[]{:S(2)}, u32[]{:S(2)}) collective-permute-start(bf16[104,1152]{1,0:T(8,128)(2,1)} %get-tuple-element.57), channel_id=1, source_target_pairs={{32,0},{64,32},{96,64},{0,96},{33,1},{65,33},{97,65},{1,97},{34,2}... | collective-permute-start | bytes 718856 | tf_op jit(solution)/shard_map/ppermute | solution.py:392
  150.7 13.9 %copy-start.1 = (bf16[1728,512]{1,0:T(8,128)(2,1)S(1)}, bf16[1728,512]{1,0:T(8,128)(2,1)}, u32[]{:S(2)}) copy-start(bf16[1728,512]{1,0:T(8,128)(2,1)} %get-tuple-element.24) | copy-start | bytes 5308420
  164.1 9.8 %collective-permute-start.7 = (bf16[432,512]{1,0:T(8,128)(2,1)S(1)}, bf16[432,512]{1,0:T(8,128)(2,1)}, u32[]{:S(2)}, u32[]{:S(2)}) collective-permute-start(bf16[432,512]{1,0:T(8,128)(2,1)S(1)} %dynamic-slice_bitcast_fusion.1), channel_id=1, source_target_pairs={{0,16},{16,0},{1,17},{17,1},{2,18},{18,2},{3,19},{19,3},{4,20},{20... | collective-permute-start | bytes 1327112 | tf_op jit(solution)/shard_map/ppermute | solution.py:383
  165.9 2.3 copy-start.2
  170.0 42.7 %collective-permute-start.11 = (bf16[216,1152]{1,0:T(8,128)(2,1)}, bf16[216,1152]{1,0:T(8,128)(2,1)}, u32[]{:S(2)}, u32[]{:S(2)}) collective-permute-start(bf16[216,1152]{1,0:T(8,128)(2,1)} %pad_maximum_fusion.3), channel_id=1, source_target_pairs={{32,0},{64,32},{96,64},{0,96},{33,1},{65,33},{97,65},{1,97},{34,2}... | collective-permute-start | bytes 1493000 | tf_op jit(solution)/shard_map/ppermute | solution.py:399
  173.5 39.3 %collective-permute-start.9 = (bf16[216,1152]{1,0:T(8,128)(2,1)}, bf16[216,1152]{1,0:T(8,128)(2,1)}, u32[]{:S(2)}, u32[]{:S(2)}) collective-permute-start(bf16[216,1152]{1,0:T(8,128)(2,1)} %pad_maximum_fusion.2), channel_id=1, source_target_pairs={{0,32},{32,64},{64,96},{96,0},{1,33},{33,65},{65,97},{97,1},{2,34}... | collective-permute-start | bytes 1493000 | tf_op jit(solution)/shard_map/ppermute | solution.py:399
  184.8 26.7 %collective-permute-start.12 = (bf16[112,1152]{1,0:T(8,128)(2,1)}, bf16[112,1152]{1,0:T(8,128)(2,1)}, u32[]{:S(2)}, u32[]{:S(2)}) collective-permute-start(bf16[112,1152]{1,0:T(8,128)(2,1)} %get-tuple-element.58), channel_id=1, source_target_pairs={{0,32},{32,64},{64,96},{96,0},{1,33},{33,65},{65,97},{97,1},{2,34}... | collective-permute-start | bytes 774152 | tf_op jit(solution)/shard_map/ppermute | solution.py:391
  184.8 23.9 %collective-permute-start.14 = (bf16[104,1152]{1,0:T(8,128)(2,1)}, bf16[104,1152]{1,0:T(8,128)(2,1)}, u32[]{:S(2)}, u32[]{:S(2)}) collective-permute-start(bf16[104,1152]{1,0:T(8,128)(2,1)} %get-tuple-element.61), channel_id=1, source_target_pairs={{32,0},{64,32},{96,64},{0,96},{33,1},{65,33},{97,65},{1,97},{34,2}... | collective-permute-start | bytes 718856 | tf_op jit(solution)/shard_map/ppermute | solution.py:392
  200.1 27.9 %all-to-all-start.2 = ((bf16[16,32,1152]{2,1,0:T(8,128)(2,1)}), bf16[16,32,1152]{2,1,0:T(8,128)(2,1)S(1)}, u32[]{:S(2)}, u32[]{:S(2)}) async-start(bf16[16,32,1152]{2,1,0:T(8,128)(2,1)} %bitcast.118), calls=%async_computation.2 | async-start | bytes 2359296 | tf_op jit(solution)/shard_map/all_to_all | solution.py:338
  208.7 3.9 %copy-start.11 = (bf16[104,1152]{1,0:T(8,128)(2,1)S(1)}, bf16[104,1152]{1,0:T(8,128)(2,1)}, u32[]{:S(2)}) copy-start(bf16[104,1152]{1,0:T(8,128)(2,1)} %get-tuple-element.60) | copy-start | bytes 718852
  209.9 11.7 %collective-permute-start.15 = (bf16[216,1152]{1,0:T(8,128)(2,1)S(1)}, bf16[216,1152]{1,0:T(8,128)(2,1)S(1)}, u32[]{:S(2)}, u32[]{:S(2)}) collective-permute-start(bf16[216,1152]{1,0:T(8,128)(2,1)S(1)} %pad_maximum_fusion.5), channel_id=1, source_target_pairs={{32,0},{64,32},{96,64},{0,96},{33,1},{65,33},{97,65},{1,97},{34,2}... | collective-permute-start | bytes 1493000 | tf_op jit(solution)/shard_map/ppermute | solution.py:399
  212.6 12.5 %collective-permute-start.13 = (bf16[216,1152]{1,0:T(8,128)(2,1)S(1)}, bf16[216,1152]{1,0:T(8,128)(2,1)S(1)}, u32[]{:S(2)}, u32[]{:S(2)}) collective-permute-start(bf16[216,1152]{1,0:T(8,128)(2,1)S(1)} %pad_maximum_fusion.4), channel_id=1, source_target_pairs={{0,32},{32,64},{64,96},{96,0},{1,33},{33,65},{65,97},{97,1},{2,34}... | collective-permute-start | bytes 1493000 | tf_op jit(solution)/shard_map/ppermute | solution.py:399
  228.0 6.4 %copy-start.3 = (bf16[16,32,1152]{2,1,0:T(8,128)(2,1)}, bf16[16,32,1152]{2,1,0:T(8,128)(2,1)S(1)}, u32[]{:S(2)}) copy-start(bf16[16,32,1152]{2,1,0:T(8,128)(2,1)S(1)} %all-to-all-done.2.source_ref) | copy-start | bytes 3538948
  228.0 22.2 %all-to-all-start.4 = ((bf16[16,72,432]{2,1,0:T(8,128)(2,1)}), bf16[16,72,432]{2,1,0:T(8,128)(2,1)S(1)}, u32[]{:S(2)}, u32[]{:S(2)}) async-start(bf16[16,72,432]{2,1,0:T(8,128)(2,1)} %bitcast.119), calls=%async_computation.4 | async-start | bytes 2359296 | tf_op jit(solution)/shard_map/all_to_all | solution.py:406
  234.4 20.2 %copy-start.13 = (bf16[288,512]{1,0:T(8,128)(2,1)S(1)}, bf16[288,512]{1,0:T(8,128)(2,1)}, u32[]{:S(2)}) copy-start(bf16[288,512]{1,0:T(8,128)(2,1)} %get-tuple-element.23) | copy-start | bytes 884740
  236.9 17.8 %copy-start.12 = (bf16[576,512]{1,0:T(8,128)(2,1)S(1)}, bf16[576,512]{1,0:T(8,128)(2,1)}, u32[]{:S(2)}) copy-start(bf16[576,512]{1,0:T(8,128)(2,1)} %get-tuple-element.22) | copy-start | bytes 1769476
  250.2 34.2 %all-to-all-start.3 = ((bf16[16,32,1152]{2,1,0:T(8,128)(2,1)}), bf16[16,32,1152]{2,1,0:T(8,128)(2,1)}, u32[]{:S(2)}, u32[]{:S(2)}) async-start(bf16[16,32,1152]{2,1,0:T(8,128)(2,1)} %pick_blocks.7), calls=%async_computation.3 | async-start | bytes 2359296 | tf_op jit(solution)/shard_map/all_to_all | solution.py:338
  281.6 7.9 %copy-start.6 = (f32[72,3456]{1,0:T(8,128)}, f32[72,3456]{1,0:T(8,128)S(1)}, u32[]{:S(2)}) copy-start(f32[72,3456]{1,0:T(8,128)S(1)} %div.19) | copy-start | bytes 2985988

commit v4 on v2

--- a/solution.py
+++ b/solution.py
@@ -132,7 +132,7 @@
         hue[p] = -1
         return 0
 
-    lax.fori_loop(0, count, clear, 0)
+    lax.fori_loop(0, count, clear, 0, unroll=8)
 
     def split(bits, partner, mate, seed):
         def start(i, _):
@@ -183,7 +183,7 @@
 
         return 0
 
-    lax.fori_loop(0, count, cross, 0)
+    lax.fori_loop(0, count, cross, 0, unroll=8)
 
 
 def route(me, order):
@@ -205,16 +205,7 @@
 
 
 def pick(index, source):
-    shape = (index.shape[0],) + source.shape[1:]
-    size = 2 * shape[0] * shape[1] * shape[2]
-    return pl.pallas_call(
-        pick_kernel,
-        in_specs=[pl.BlockSpec(memory_space=pltpu.SMEM), pl.BlockSpec(memory_space=pltpu.VMEM)],
-        out_specs=pl.BlockSpec(memory_space=pltpu.VMEM),
-        out_shape=jax.ShapeDtypeStruct(shape, source.dtype),
-        cost_estimate=pl.CostEstimate(flops=0, bytes_accessed=2 * size, transcendentals=0),
-        name="pick_blocks",
-    )(index, source)
+    return whole_call(pick_kernel, index, source, name="pick_blocks")
 
 
 def statistics(values):
@@ -225,57 +216,44 @@
 
 
 def norm_kernel(index_ref, rows_ref, gain_ref, out_ref):
-    normed, _ = statistics(rows_ref[0].astype(F32))
-    out_ref[0] = (normed * gain_ref[...]).astype(BF16)
+    for i in range(out_ref.shape[0]):
+        normed, _ = statistics(rows_ref[index_ref[i]].astype(F32))
+        out_ref[i] = (normed * gain_ref[...][None]).astype(BF16)
+
+
+def whole_call(kernel, index, *arrays, name):
+    size = 2 * (1 + len(arrays)) * arrays[0].size
+    return pl.pallas_call(
+        kernel,
+        in_specs=[pl.BlockSpec(memory_space=pltpu.SMEM)]
+        + [pl.BlockSpec(memory_space=pltpu.VMEM)] * len(arrays),
+        out_specs=pl.BlockSpec(memory_space=pltpu.VMEM),
+        out_shape=jax.ShapeDtypeStruct((index.shape[0],) + arrays[0].shape[1:], BF16),
+        compiler_params=pltpu.CompilerParams(vmem_limit_bytes=16 * 2**20),
+        cost_estimate=pl.CostEstimate(flops=size, bytes_accessed=size, transcendentals=0),
+        name=name,
+    )(index, *arrays)
 
 
 def norm_blocks(index, blocks, gain):
-    count, rows, width = blocks.shape
-    return pl.pallas_call(
-        norm_kernel,
-        grid_spec=pltpu.PrefetchScalarGridSpec(
-            num_scalar_prefetch=1,
-            grid=(count,),
-            in_specs=[
-                pl.BlockSpec((1, rows, width), lambda i, index: (index[i], 0, 0)),
-                pl.BlockSpec((1, width), lambda i, index: (0, 0)),
-            ],
-            out_specs=pl.BlockSpec((1, rows, width), lambda i, index: (i, 0, 0)),
-        ),
-        out_shape=jax.ShapeDtypeStruct(blocks.shape, BF16),
-        name="norm_blocks",
-    )(index, blocks, gain[None])
+    return whole_call(norm_kernel, index, blocks, gain, name="norm_blocks")
 
 
 def norm_back_kernel(index_ref, grads_ref, rows_ref, gain_ref, out_ref):
-    normed, inverse_std = statistics(rows_ref[0].astype(F32))
-    pushed = grads_ref[0].astype(F32) * gain_ref[...]
-    along = jnp.mean(pushed * normed, axis=1, keepdims=True)
-    out_ref[0] = (
-        inverse_std * (pushed - jnp.mean(pushed, axis=1, keepdims=True) - normed * along)
-    ).astype(BF16)
+    for i in range(out_ref.shape[0]):
+        normed, inverse_std = statistics(rows_ref[i].astype(F32))
+        pushed = grads_ref[index_ref[i]].astype(F32) * gain_ref[...][None]
+        along = jnp.mean(pushed * normed, axis=1, keepdims=True)
+        out_ref[i] = (
+            inverse_std * (pushed - jnp.mean(pushed, axis=1, keepdims=True) - normed * along)
+        ).astype(BF16)
 
 
 def norm_back(index, grads, blocks, gain):
-    count, rows, width = blocks.shape
-    return pl.pallas_call(
-        norm_back_kernel,
-        grid_spec=pltpu.PrefetchScalarGridSpec(
-            num_scalar_prefetch=1,
-            grid=(count,),
-            in_specs=[
-                pl.BlockSpec((1, rows, width), lambda i, index: (index[i], 0, 0)),
-                pl.BlockSpec((1, rows, width), lambda i, index: (i, 0, 0)),
-                pl.BlockSpec((1, width), lambda i, index: (0, 0)),
-            ],
-            out_specs=pl.BlockSpec((1, rows, width), lambda i, index: (i, 0, 0)),
-        ),
-        out_shape=jax.ShapeDtypeStruct(blocks.shape, BF16),
-        name="norm_back",
-    )(index, grads, blocks, gain[None])
-
-
-GROUPS = 2
+    return whole_call(norm_back_kernel, index, grads, blocks, gain, name="norm_back")
+
+
+GROUPS = 1
 
 
 def local(loader_rows, lengths, block_order, norm_gain, qkv_weight, upstream_grad):

time: 270 us -> 258 us (0.956)
  Pallas kernels: 69.2 us -> 56.5 us
  waiting for transfers between devices: 50.2 us -> 54.7 us
  other arithmetic: 9.15 us -> 5.43 us
  local copies, waits for them, and re-layouts: 14.6 us -> 17.7 us
    reduce_scatter x0 -> x1, waiting for transfers between devices: none -> 12.9 us  [local(): lax.psum_scatter(weight_local, DP, scatter_dimension=0, tiled=True)]
    pallas_call x6, Pallas kernels: 19.2 us -> 9.91 us  [whole_call(): pl.pallas_call(kernel, in_specs=[pl.BlockSpec(memory_space=pltpu.SMEM)] +...]
    unnamed x4 -> x1, waiting for transfers between devices: 6.58 us -> 0.02 us
    all_to_all x3, waiting for transfers between devices: 22.3 us -> 17.5 us  [exchange(): return lax.all_to_all(x, SEQ, split_axis=0, concat_axis=0, tiled=True)]
    div x3, local copies, waits for them, and re-layouts: 2.64 us -> 6.73 us  [local(): weight_grad = weight_grad.astype(F32) / pack_count]
    all_to_all x1, waiting for transfers between devices: 8.25 us -> 11.2 us  [local(): lax.all_to_all(partial, SEQ, split_axis=0, concat_axis=0, tiled=True)]
    pallas_call x2 -> x1, Pallas kernels: 44.6 us -> 41.9 us  [attention_call(): pl.pallas_call(attention_kernel, grid=(pairs,), in_specs=[pl.BlockSpec((t...]
    dot_general x2 -> x1, matrix products: 11.8 us -> 9.65 us  [nn(): lax.dot_general(a, b, (((1,), (0,)), ((), ())), preferred_element_type=F32)]
  transfers between devices with their start and end apart: 10 -> 9, of which waited for: 6 -> 6; matrix products, arithmetic and copies ran while one was open for 13% -> 11% of each run, Pallas kernels for 12% -> 2%
where the time goes in v4:
time: 258 us
  Pallas kernels  56.5 us (22%)
  waiting for transfers between devices  54.7 us (21%)
  blocking collectives  41.8 us (16%)
  starting transfers between devices  33.7 us (13%)
  matrix products  33.4 us (13%)
  local copies, waits for them, and re-layouts  17.7 us (7%)
  between operations  14.4 us (6%)
  other arithmetic  5.43 us (2%)
    pallas_call x1, Pallas kernels, attention_call(): pl.pallas_call(attention_kernel, grid=(pairs,), in_specs=[pl.BlockSpec((t...  41.9 us
    all_to_all x1, blocking collectives, exchange(): return lax.all_to_all(x, SEQ, split_axis=0, concat_axis=0, tiled=True)  25.5 us
    all_to_all x3, waiting for transfers between devices, exchange(): return lax.all_to_all(x, SEQ, split_axis=0, concat_axis=0, tiled=True)  17.5 us
    all_to_all x3, starting transfers between devices, exchange(): return lax.all_to_all(x, SEQ, split_axis=0, concat_axis=0, tiled=True)  17.3 us
    all_gather x1, blocking collectives, local(): weight_cols = lax.all_gather(summed, DP, axis=0)  16.3 us
    dot_general x2, matrix products, project(): lax.dot_general(qkv_weight, rows, (((0,), (1,)), ((), ())), preferred_ele...  16.3 us
    reduce_scatter x1, waiting for transfers between devices, local(): lax.psum_scatter(weight_local, DP, scatter_dimension=0, tiled=True)  12.9 us
    all_to_all x1, waiting for transfers between devices, local(): lax.all_to_all(partial, SEQ, split_axis=0, concat_axis=0, tiled=True)  11.2 us
  transfers between devices with their start and end apart: 9, of which 6 were waited for; matrix products, arithmetic and copies ran while one was open for 11% of the time, Pallas kernels for 2%

profile of v4, /device:TPU:1, one launch (start us, length us, event | category | flops | bytes accessed | tf_op | source)
XLA Modules:
  0.0 257.6 jit_solution(12327467657084510815)
XLA Ops:
  7.2 4.7 %route_blocks.1 = (s32[4]{0:T(128)}, s32[16]{0:T(128)}, s32[4]{0:T(128)}, s32[4]{0:T(128)}, s32[16]{0:T(128)}, /*index=5*/s32[4]{0:T(128)}) custom-call(s32[1]{0:T(128)} %bitcast.1.me_ref, s32[64]{0:T(128)} %bitcast.67), custom_call_target="tpu_custom_call" | custom-call | tf_op jit(solution)/shard_map/route_blocks/pallas_call | solution.py:192
  11.9 1.3 copy-done
  13.1 0.7 copy-done.2
  13.8 0.7 copy-done.8
  14.5 2.3 norm_blocks.1
  16.8 8.5 %all-to-all-start = ((bf16[16,32,1152]{2,1,0:T(8,128)(2,1)}), bf16[16,32,1152]{2,1,0:T(8,128)(2,1)S(1)}, u32[]{:S(2)}, u32[]{:S(2)}) async-start(bf16[16,32,1152]{2,1,0:T(8,128)(2,1)} %bitcast.4), calls=%async_computation | async-start | bytes 2359296 | tf_op jit(solution)/shard_map/all_to_all | solution.py:272
  25.4 0.6 copy.66
  26.0 16.8 %all-to-all-done.source_ref = bf16[16,32,1152]{2,1,0:T(8,128)(2,1)S(1)} async-done(((bf16[16,32,1152]{2,1,0:T(8,128)(2,1)}), bf16[16,32,1152]{2,1,0:T(8,128)(2,1)S(1)}, u32[]{:S(2)}, u32[]{:S(2)}) %all-to-all-start) | async-done | bytes 1179680 | tf_op jit(solution)/shard_map/all_to_all | solution.py:272
  42.8 1.6 pick_blocks.4
  44.4 5.0 %all-to-all-start.1 = ((bf16[16,32,1152]{2,1,0:T(8,128)(2,1)}), bf16[16,32,1152]{2,1,0:T(8,128)(2,1)S(1)}, u32[]{:S(2)}, u32[]{:S(2)}) async-start(bf16[16,32,1152]{2,1,0:T(8,128)(2,1)} %pick_blocks.4), calls=%async_computation.1 | async-start | bytes 2359296 | tf_op jit(solution)/shard_map/all_to_all | solution.py:272
  49.6 3.3 %collective-permute-start.2 = (bf16[128,1152]{0,1:T(8,128)(2,1)S(1)}, bf16[128,1152]{0,1:T(8,128)(2,1)S(1)}, u32[]{:S(2)}, u32[]{:S(2)}) collective-permute-start(bf16[128,1152]{0,1:T(8,128)(2,1)S(1)} %get-tuple-element.44), channel_id=1, source_target_pairs={{0,1},{1,2},{2,3},{3,4},{4,5},{5,6},{6,7},{7,8},{8,9},{9,10},{10,1... | collective-permute-start | bytes 884744 | tf_op jit(solution)/shard_map/ppermute | solution.py:278
  52.9 1.3 collective-permute-start.3
  54.3 0.2 reduce-window.8
  54.6 0.3 convert_reduce_fusion
  54.9 0.6 and_select_fusion.row_ref
  55.5 0.9 reshape_select_fusion.col_ref
  56.4 11.0 %collective-permute-done.2 = bf16[128,1152]{0,1:T(8,128)(2,1)S(1)} collective-permute-done((bf16[128,1152]{0,1:T(8,128)(2,1)S(1)}, bf16[128,1152]{0,1:T(8,128)(2,1)S(1)}, u32[]{:S(2)}, u32[]{:S(2)}) %collective-permute-start.2) | collective-permute-done | bytes 294944 | tf_op jit(solution)/shard_map/ppermute | solution.py:278
  67.4 2.1 collective-permute-done.3
  69.5 0.9 maximum_bitcast_fusion.gh_ref
  70.4 0.6 pick_blocks.5
  71.1 4.4 %collective-permute-start = (bf16[128,1152]{1,0:T(8,128)(2,1)S(1)}, bf16[128,1152]{1,0:T(8,128)(2,1)S(1)}, u32[]{:S(2)}, u32[]{:S(2)}) collective-permute-start(bf16[128,1152]{1,0:T(8,128)(2,1)S(1)} %get-tuple-element.46), channel_id=1, source_target_pairs={{0,1},{1,2},{2,3},{3,4},{4,5},{5,6},{6,7},{7,8},{8,9},{9,10},{10,1... | collective-permute-start | bytes 884744 | tf_op jit(solution)/shard_map/ppermute | solution.py:278
  75.5 1.5 collective-permute-start.1
  77.0 11.4 %fusion.q_ref.k_ref.v_ref = bf16[3456,512]{1,0:T(8,128)(2,1)} fusion(bf16[512,1152]{1,0:T(8,128)(2,1)S(1)} %bitcast.54, bf16[1152,3456]{1,0:T(8,128)(2,1)} %param.10), kind=kOutput, calls=%fused_computation.2 | convolution fusion | flops 4078632960 | bytes 12681216 | tf_op jit(solution)/shard_map/dot_general | solution.py:293
  88.5 4.8 %fusion.1.qh_ref.kh_ref.vh_ref = bf16[3456,256]{1,0:T(8,128)(2,1)} fusion(bf16[1152,3456]{1,0:T(8,128)(2,1)S(1)} %bitcast.65, bf16[128,1152]{1,0:T(8,128)(2,1)S(1)} %collective-permute-done.1, bf16[128,1152]{1,0:T(8,128)(2,1)S(1)} %collective-permute-done), kind=kOutput, calls=%fused_computation.4 | convolution fusion | flops 2040496128 | bytes 10321920 | tf_op jit(solution)/shard_map/dot_general | solution.py:293
  93.3 41.9 %packed_attention.1 = (bf16[1152,512]{1,0:T(8,128)(2,1)}, bf16[3456,512]{1,0:T(8,128)(2,1)}) custom-call(s32[768,1]{1,0:T(8,128)} %reshape_select_fusion.col_ref, s32[1,768]{1,0:T(1,128)} %and_select_fusion.row_ref, bf16[3456,512]{1,0:T(8,128)(2,1)} %fusion.q_ref.k_ref.v_ref, bf16[3456,512]{1,0:T(8,128)(2,1)} %fusion.q_ref.k_ref.v_ref, ...), custom_call_target="tpu_custom_call" | custom-call | flops 3623878656 | bytes 11796480 | tf_op jit(solution)/shard_map/packed_attention/pallas_call | solution.py:93
  135.2 9.7 %convolution_convert_fusion = bf16[3456,1152]{1,0:T(8,128)(2,1)} fusion(bf16[3456,512]{1,0:T(8,128)(2,1)} %get-tuple-element.19, bf16[512,1152]{1,0:T(8,128)(2,1)S(1)} %bitcast.55), kind=kOutput, calls=%fused_computation | convolution fusion | flops 4080844800 | bytes 12681216 | tf_op jit(solution)/shard_map/dot_general | solution.py:25
  144.9 2.0 copy-done.12
  146.8 0.3 copy.69
  147.2 7.5 %convolution_convert_fusion.3 = bf16[512,1152]{1,0:T(8,128)(2,1)S(1)} fusion(bf16[3456,512]{1,0:T(8,128)(2,1)S(1)} %bitcast.60, bf16[1152,3456]{1,0:T(8,128)(2,1)} %param.10), kind=kOutput, calls=%fused_computation.5 | convolution fusion | flops 4077453312 | bytes 12681216 | tf_op jit(solution)/shard_map/dot_general | solution.py:318
  154.7 0.6 pick_blocks.6
  155.3 25.5 %all_to_all.25.source_ref = bf16[16,32,1152]{2,1,0:T(8,128)(2,1)S(1)} all-to-all(bf16[16,32,1152]{2,1,0:T(8,128)(2,1)S(1)} %bitcast.50), channel_id=1, replica_groups=mesh['y'=4,'core'=2,'z'=4,'x'=4] {'z','x'}, dimensions={0} | all-to-all | bytes 2359296 | tf_op jit(solution)/shard_map/all_to_all | solution.py:272
  180.8 1.6 pick_blocks.7
  182.5 3.7 %all-to-all-start.3 = ((bf16[16,32,1152]{2,1,0:T(8,128)(2,1)}), bf16[16,32,1152]{2,1,0:T(8,128)(2,1)S(1)}, u32[]{:S(2)}, u32[]{:S(2)}) async-start(bf16[16,32,1152]{2,1,0:T(8,128)(2,1)} %pick_blocks.7), calls=%async_computation.3 | async-start | bytes 2359296 | tf_op jit(solution)/shard_map/all_to_all | solution.py:272
  186.2 12.9 %reduce-scatter.2.cloned.1.call-done = bf16[432,1152]{1,0:T(8,128)(2,1)} async-done(((bf16[3456,1152]{1,0:T(8,128)(2,1)}), bf16[432,1152]{1,0:T(8,128)(2,1)}) %reduce-scatter.2.cloned.1.call-update) | async-done | bytes 995344 | tf_op jit(solution)/shard_map/reduce_scatter | solution.py:312
  199.1 2.4 copy.70
  201.5 0.8 all-to-all-done.3
  202.3 5.9 %all-to-all-start.4 = ((bf16[16,72,432]{2,1,0:T(8,128)(2,1)}), bf16[16,72,432]{2,1,0:T(8,128)(2,1)S(1)}, u32[]{:S(2)}, u32[]{:S(2)}) async-start(bf16[16,72,432]{2,1,0:T(8,128)(2,1)} %bitcast.26), calls=%async_computation.5 | async-start | bytes 2359296 | tf_op jit(solution)/shard_map/all_to_all | solution.py:330
  208.2 2.5 copy.73
  210.7 3.0 %norm_back.1 = bf16[4,128,1152]{2,1,0:T(8,128)(2,1)} custom-call(s32[4]{0:T(128)S(1)} %copy-done.9, bf16[4,128,1152]{2,1,0:T(8,128)(2,1)S(1)} %bitcast.51, bf16[4,128,1152]{2,1,0:T(8,128)(2,1)S(1)} %bitcast.53, f32[1152]{0:T(1024)S(1)} %copy-done.3), custom_call_target="tpu_custom_call" | custom-call | flops 4718592 | bytes 4718592 | tf_op jit(solution)/shard_map/norm_back/pallas_call | solution.py:226
  213.7 11.2 %all-to-all-done.4 = bf16[16,72,432]{2,1,0:T(8,128)(2,1)S(1)} async-done(((bf16[16,72,432]{2,1,0:T(8,128)(2,1)}), bf16[16,72,432]{2,1,0:T(8,128)(2,1)S(1)}, u32[]{:S(2)}, u32[]{:S(2)}) %all-to-all-start.4) | async-done | bytes 995360 | tf_op jit(solution)/shard_map/all_to_all | solution.py:330
  224.9 0.2 reduce_sum.37
  225.1 16.3 %all-gather = bf16[576,432]{1,0:T(8,128)(2,1)S(1)} all-gather(bf16[72,432]{1,0:T(8,128)(2,1)S(1)} %reduce_sum.37), channel_id=2, replica_groups=mesh['y'=4,'core'=2,'z'=4,'x'=4] {'y','core'}, dimensions={0}, use_global_device_ids=true | all-gather | bytes 559872 | tf_op jit(solution)/shard_map/all_gather | solution.py:332
  241.4 0.3 copy.71
  241.8 0.8 div.17
  242.6 2.4 copy.72
  245.0 3.5 %div.19 = f32[72,3456]{1,0:T(8,128)S(1)} reshape(f32[72,3,1,8,2,72]{5,4,3,1,0,2:T(2,128)} %copy.72) | data formatting | bytes 1990656 | tf_op jit(solution)/shard_map/div | solution.py:336
  248.6 1.6 multiply_reduce_fusion
  250.2 0.6 dynamic-slice_divide_fusion
  (42 shorter events, 0.5 us)
Async XLA Ops:
  11.8 1.3 copy-start
  13.1 0.7 copy-start.2
  13.8 0.7 copy-start.8
  16.8 8.6 %copy-start.13 = (bf16[1,512,1152]{2,1,0:T(8,128)(2,1)S(1)}, bf16[1,512,1152]{2,1,0:T(8,128)(2,1)}, u32[]{:S(2)}) copy-start(bf16[1,512,1152]{2,1,0:T(8,128)(2,1)} %param.11) | copy-start | bytes 3538948
  16.8 26.0 %all-to-all-start = ((bf16[16,32,1152]{2,1,0:T(8,128)(2,1)}), bf16[16,32,1152]{2,1,0:T(8,128)(2,1)S(1)}, u32[]{:S(2)}, u32[]{:S(2)}) async-start(bf16[16,32,1152]{2,1,0:T(8,128)(2,1)} %bitcast.4), calls=%async_computation | async-start | bytes 2359296 | tf_op jit(solution)/shard_map/all_to_all | solution.py:272
  25.4 17.4 %copy-start.7 = (s32[16]{0:T(128)S(1)}, s32[16]{0:T(128)}, u32[]{:S(2)}) copy-start(s32[16]{0:T(128)} %get-tuple-element.13.index_ref) | copy-start | bytes 196
  26.0 23.5 %copy-start.10 = (bf16[1,512,1152]{1,2,0:T(8,128)(2,1)}, bf16[1,512,1152]{1,2,0:T(8,128)(2,1)S(1)}, u32[]{:S(2)}) copy-start(bf16[1,512,1152]{1,2,0:T(8,128)(2,1)S(1)} %copy.66) | copy-start | bytes 3538948
  44.4 25.9 %all-to-all-start.1 = ((bf16[16,32,1152]{2,1,0:T(8,128)(2,1)}), bf16[16,32,1152]{2,1,0:T(8,128)(2,1)S(1)}, u32[]{:S(2)}, u32[]{:S(2)}) async-start(bf16[16,32,1152]{2,1,0:T(8,128)(2,1)} %pick_blocks.4), calls=%async_computation.1 | async-start | bytes 2359296 | tf_op jit(solution)/shard_map/all_to_all | solution.py:272
  49.4 4.7 %copy-start.14 = (s32[1,128]{1,0:T(1,128)S(1)}, s32[1,128]{1,0:T(1,128)}, u32[]{:S(2)}) copy-start(s32[1,128]{1,0:T(1,128)} %param.7) | copy-start | bytes 1540
  49.5 149.6 %reduce-scatter.2.cloned.1.call-start = ((), (), s32[]{:S(2)}) async-start(), calls=%async_computation.6 | async-start | bytes 8957952 | tf_op jit(solution)/shard_map/reduce_scatter | solution.py:312
  49.6 20.8 %copy-start.6 = (s32[4]{0:T(128)S(1)}, s32[4]{0:T(128)}, u32[]{:S(2)}) copy-start(s32[4]{0:T(128)} %get-tuple-element.12.index_ref) | copy-start | bytes 52
  49.6 17.9 %collective-permute-start.2 = (bf16[128,1152]{0,1:T(8,128)(2,1)S(1)}, bf16[128,1152]{0,1:T(8,128)(2,1)S(1)}, u32[]{:S(2)}, u32[]{:S(2)}) collective-permute-start(bf16[128,1152]{0,1:T(8,128)(2,1)S(1)} %get-tuple-element.44), channel_id=1, source_target_pairs={{0,1},{1,2},{2,3},{3,4},{4,5},{5,6},{6,7},{7,8},{8,9},{9,10},{10,1... | collective-permute-start | bytes 884744 | tf_op jit(solution)/shard_map/ppermute | solution.py:278
  52.9 16.6 %collective-permute-start.3 = (bf16[128,1152]{0,1:T(8,128)(2,1)S(1)}, bf16[128,1152]{0,1:T(8,128)(2,1)S(1)}, u32[]{:S(2)}, u32[]{:S(2)}) collective-permute-start(bf16[128,1152]{0,1:T(8,128)(2,1)S(1)} %get-tuple-element.45), channel_id=1, source_target_pairs={{1,0},{2,1},{3,2},{4,3},{5,4},{6,5},{7,6},{8,7},{9,8},{10,9},{11,1... | collective-permute-start | bytes 884744 | tf_op jit(solution)/shard_map/ppermute | solution.py:279
  71.0 17.4 %slice-start = ((s8[7962624]{0:T(1024)(128)(4,1)}), s8[4194304]{0:T(1024)(128)(4,1)S(1)}, s32[]{:S(2)}) async-start(s8[7962624]{0:T(1024)(128)(4,1)} %bitcast.64), calls=%async_computation.7 | async-start | bytes 8388608
  71.1 17.3 %collective-permute-start = (bf16[128,1152]{1,0:T(8,128)(2,1)S(1)}, bf16[128,1152]{1,0:T(8,128)(2,1)S(1)}, u32[]{:S(2)}, u32[]{:S(2)}) collective-permute-start(bf16[128,1152]{1,0:T(8,128)(2,1)S(1)} %get-tuple-element.46), channel_id=1, source_target_pairs={{0,1},{1,2},{2,3},{3,4},{4,5},{5,6},{6,7},{7,8},{8,9},{9,10},{10,1... | collective-permute-start | bytes 884744 | tf_op jit(solution)/shard_map/ppermute | solution.py:278
  75.5 12.9 %collective-permute-start.1 = (bf16[128,1152]{1,0:T(8,128)(2,1)S(1)}, bf16[128,1152]{1,0:T(8,128)(2,1)S(1)}, u32[]{:S(2)}, u32[]{:S(2)}) collective-permute-start(bf16[128,1152]{1,0:T(8,128)(2,1)S(1)} %get-tuple-element.47), channel_id=1, source_target_pairs={{1,0},{2,1},{3,2},{4,3},{5,4},{6,5},{7,6},{8,7},{9,8},{10,9},{11,1... | collective-permute-start | bytes 884744 | tf_op jit(solution)/shard_map/ppermute | solution.py:279
  77.0 11.5 %slice-start.1 = ((s8[7962624]{0:T(1024)(128)(4,1)}), s8[3768320]{0:T(1024)(128)(4,1)S(1)}, s32[]{:S(2)}) async-start(s8[7962624]{0:T(1024)(128)(4,1)} %bitcast.64), calls=%async_computation.8 | async-start | bytes 7536640
  144.8 2.0 copy-start.12
  147.2 7.5 %copy-start.5 = (s32[4]{0:T(128)S(1)}, s32[4]{0:T(128)}, u32[]{:S(2)}) copy-start(s32[4]{0:T(128)} %get-tuple-element.18.index_ref) | copy-start | bytes 52
  155.3 25.5 %copy-start.4 = (s32[16]{0:T(128)S(1)}, s32[16]{0:T(128)}, u32[]{:S(2)}) copy-start(s32[16]{0:T(128)} %get-tuple-element.17.index_ref) | copy-start | bytes 196
  182.5 19.8 %all-to-all-start.3 = ((bf16[16,32,1152]{2,1,0:T(8,128)(2,1)}), bf16[16,32,1152]{2,1,0:T(8,128)(2,1)S(1)}, u32[]{:S(2)}, u32[]{:S(2)}) async-start(bf16[16,32,1152]{2,1,0:T(8,128)(2,1)} %pick_blocks.7), calls=%async_computation.3 | async-start | bytes 2359296 | tf_op jit(solution)/shard_map/all_to_all | solution.py:272
  202.3 22.7 %all-to-all-start.4 = ((bf16[16,72,432]{2,1,0:T(8,128)(2,1)}), bf16[16,72,432]{2,1,0:T(8,128)(2,1)S(1)}, u32[]{:S(2)}, u32[]{:S(2)}) async-start(bf16[16,72,432]{2,1,0:T(8,128)(2,1)} %bitcast.26), calls=%async_computation.5 | async-start | bytes 2359296 | tf_op jit(solution)/shard_map/all_to_all | solution.py:330
  208.2 2.5 copy-start.1
  208.2 2.5 copy-start.3
  208.2 2.5 copy-start.9
  248.5 2.2 copy-start.11
Sparse Core Ops, SparseCore 0:
  145.0 54.0 reduce-scatter.1

commit v5 on v4

--- a/solution.py
+++ b/solution.py
@@ -16,7 +16,9 @@
 F32 = jnp.float32
 EPSILON = 1e-06
 SCORE_SCALE = HD ** (-0.5)
+EXP2_SCALE = SCORE_SCALE * 1.4426950408889634
 HIDDEN_BIAS = -1e30
+LAG = 2
 DP = ("y", "core")
 SEQ = ("z", "x")
 
@@ -43,7 +45,7 @@
             same = col_ref[b * BLK : (b + 1) * BLK, :] == row_ref[:, first * BLK : (last + 1) * BLK]
             bias_ref[b, :, : (last + 1 - first) * BLK] = jnp.where(same, 0.0, HIDDEN_BIAS)
 
-    for head in range(2):
+    def operands(head):
         lo, hi = head * HD, (head + 1) * HD
 
         def whole(own, halo):
@@ -51,34 +53,59 @@
             return jnp.concatenate([rim[:, :BLK], mid, rim[:, BLK:]], axis=1)
 
         q32, g32 = whole(q_ref, qh_ref), whole(g_ref, gh_ref)
-        q, g = q32.astype(BF16), g32.astype(BF16)
         k, v = whole(k_ref, kh_ref).astype(BF16), whole(v_ref, vh_ref).astype(BF16)
+        return q32, g32, q32.astype(BF16), g32.astype(BF16), k, v
+
+    heads = [operands(head) for head in range(2)]
+    for part in (1, 2, 4, 5):
+        d_s[part * HD : (part + 1) * HD, :] = jnp.zeros((HD, rows), F32)
+
+    def window(b):
+        first, last = max(b - 1, 0), min(b + 1, blocks + 1)
+        return first, last, slice(first * BLK, (last + 1) * BLK), slice(b * BLK, (b + 1) * BLK)
+
+    def products(head, b):
+        q32, g32, _, _, k, v = heads[head]
+        _, _, near, here = window(b)
+        scores = nn(q32[:, here].T.astype(BF16), k[:, near])
+        grad_probs = nn(g32[:, here].T.astype(BF16), v[:, near])
+        return scores, grad_probs
+
+    def softmax(head, b, scores, grad_probs):
+        weights = jnp.exp2(scores * EXP2_SCALE + bias_ref[b, :, : scores.shape[1]])
+        probs = weights * (1.0 / jnp.sum(weights, axis=1, keepdims=True))
+        centred = jnp.sum(probs * grad_probs, axis=1, keepdims=True)
+        return probs.astype(BF16), (probs * (grad_probs - centred)).astype(BF16)
+
+    def results(head, b, rounded, grad_scores):
+        _, _, q, g, k, v = heads[head]
+        first, last, near, here = window(b)
         q_at, k_at, v_at = (slice((3 * head + part) * HD, (3 * head + part + 1) * HD) for part in range(3))
-        d_s[k_at, :] = jnp.zeros((HD, rows), F32)
-        d_s[v_at, :] = jnp.zeros((HD, rows), F32)
-        for b in range(blocks + 2):
-            first, last = max(b - 1, 0), min(b + 1, blocks + 1)
-            width = (last + 1 - first) * BLK
-            k_win = k[:, first * BLK : (last + 1) * BLK]
-            v_win = v[:, first * BLK : (last + 1) * BLK]
-            here = slice(b * BLK, (b + 1) * BLK)
-            scores = nn(q32[:, here].T.astype(BF16), k_win)
-            grad_probs = nn(g32[:, here].T.astype(BF16), v_win)
-            weights = jnp.exp(scores * SCORE_SCALE + bias_ref[b, :, :width])
-            probs = weights * (1.0 / jnp.sum(weights, axis=1, keepdims=True))
-            rounded = probs.astype(BF16)
-            centred = jnp.sum(probs * grad_probs, axis=1, keepdims=True)
-            grad_scores = (probs * (grad_probs - centred) * SCORE_SCALE).astype(BF16)
-            if 1 <= b <= blocks:
-                own = slice((b - 1) * BLK, b * BLK)
-                o_s[lo:hi, own] = nt(v_win, rounded)
-                d_s[q_at, own] = nt(k_win, grad_scores)
-            k0, k1 = max(first, 1), min(last, blocks)
-            seen = slice((k0 - first) * BLK, (k1 + 1 - first) * BLK)
-            into = slice((k0 - 1) * BLK, k1 * BLK)
-            d_s[k_at, into] += nn(q[:, here], grad_scores[:, seen])
-            d_s[v_at, into] += nn(g[:, here], rounded[:, seen])
+        if 1 <= b <= blocks:
+            own = slice((b - 1) * BLK, b * BLK)
+            o_s[head * HD : (head + 1) * HD, own] = nt(v[:, near], rounded)
+            d_s[q_at, own] = nt(k[:, near], grad_scores)
+        k0, k1 = max(first, 1), min(last, blocks)
+        seen = slice((k0 - first) * BLK, (k1 + 1 - first) * BLK)
+        into = slice((k0 - 1) * BLK, k1 * BLK)
+        d_s[k_at, into] += nn(q[:, here], grad_scores[:, seen])
+        d_s[v_at, into] += nn(g[:, here], rounded[:, seen])
+
+    items = [(head, b) for b in range(blocks + 2) for head in range(2)]
+    scored, softened = {}, {}
+    for step in range(len(items) + 2 * LAG):
+        if step < len(items):
+            scored[step] = products(*items[step])
+        if 0 <= step - LAG < len(items):
+            softened[step - LAG] = softmax(*items[step - LAG], *scored.pop(step - LAG))
+        if 0 <= step - 2 * LAG:
+            results(*items[step - 2 * LAG], *softened.pop(step - 2 * LAG))
     o_ref[...] = o_s[...].astype(BF16)
+    for head in range(2):
+        for part, factor in enumerate((SCORE_SCALE, SCORE_SCALE, None)):
+            at = slice((3 * head + part) * HD, (3 * head + part + 1) * HD)
+            if factor is not None:
+                d_s[at, :] = d_s[at, :] * factor
     d_ref[...] = d_s[...].astype(BF16)
 
 
@@ -122,7 +149,13 @@
     )(ids[:, None], ids[None, :], own, own, own, halo, halo, halo, g_own, g_halo)
 
 
-def route_kernel(me_ref, order_ref, first_ref, cross_ref, last_ref, back_first_ref, back_cross_ref, back_last_ref, place, half, hue):
+def route_kernel(
+    me_ref, order_ref, rows_ref, gain_ref,
+    out_ref, first_ref, cross_ref, last_ref, back_first_ref, back_cross_ref, back_last_ref,
+    place, half, hue, buffer, arrived,
+):
+    fetch = pltpu.make_async_copy(rows_ref, buffer, arrived)
+    fetch.start()
     me = me_ref[0]
     count = order_ref.shape[0]
 
@@ -184,19 +217,26 @@
         return 0
 
     lax.fori_loop(0, count, cross, 0, unroll=8)
-
-
-def route(me, order):
+    fetch.wait()
+    for i in range(out_ref.shape[0]):
+        normed, _ = statistics(buffer[first_ref[i]].astype(F32))
+        out_ref[i] = (normed * gain_ref[...][None]).astype(BF16)
+
+
+def route(me, order, blocks, gain):
     smem = pl.BlockSpec(memory_space=pltpu.SMEM)
+    vmem = pl.BlockSpec(memory_space=pltpu.VMEM)
     sizes = (4, 16, 4, 4, 16, 4)
     return pl.pallas_call(
         route_kernel,
-        in_specs=[smem, smem],
-        out_specs=[smem] * len(sizes),
-        out_shape=[jax.ShapeDtypeStruct((n,), jnp.int32) for n in sizes],
-        scratch_shapes=[pltpu.SMEM(order.shape, jnp.int32)] * 3,
+        in_specs=[smem, smem, pl.BlockSpec(memory_space=pl.ANY), vmem],
+        out_specs=[vmem] + [smem] * len(sizes),
+        out_shape=[jax.ShapeDtypeStruct(blocks.shape, BF16)]
+        + [jax.ShapeDtypeStruct((n,), jnp.int32) for n in sizes],
+        scratch_shapes=[pltpu.SMEM(order.shape, jnp.int32)] * 3
+        + [pltpu.VMEM(blocks.shape, BF16), pltpu.SemaphoreType.DMA(())],
         name="route_blocks",
-    )(me[None], order)
+    )(me[None], order, blocks, gain)
 
 
 def pick_kernel(index_ref, source_ref, out_ref):
@@ -213,12 +253,6 @@
     spread = jnp.mean((values - centre) ** 2, axis=1, keepdims=True)
     inverse_std = lax.rsqrt(spread + EPSILON)
     return (values - centre) * inverse_std, inverse_std
-
-
-def norm_kernel(index_ref, rows_ref, gain_ref, out_ref):
-    for i in range(out_ref.shape[0]):
-        normed, _ = statistics(rows_ref[index_ref[i]].astype(F32))
-        out_ref[i] = (normed * gain_ref[...][None]).astype(BF16)
 
 
 def whole_call(kernel, index, *arrays, name):
@@ -235,10 +269,6 @@
     )(index, *arrays)
 
 
-def norm_blocks(index, blocks, gain):
-    return whole_call(norm_kernel, index, blocks, gain, name="norm_blocks")
-
-
 def norm_back_kernel(index_ref, grads_ref, rows_ref, gain_ref, out_ref):
     for i in range(out_ref.shape[0]):
         normed, inverse_std = statistics(rows_ref[i].astype(F32))
@@ -253,7 +283,35 @@
     return whole_call(norm_back_kernel, index, grads, blocks, gain, name="norm_back")
 
 
-GROUPS = 1
+def assemble_kernel(parts_ref, weight_ref, gain_ref, out_ref, gain_grad_ref):
+    packs, share, _ = parts_ref.shape
+    heads = HEADS // packs
+    width = out_ref.shape[1] // 3
+    for pack in range(packs):
+        cols = parts_ref[pack].astype(F32) * (1.0 / packs)
+        for head in range(heads):
+            for part in range(3):
+                at = part * width + (pack * heads + head) * HD
+                start = (3 * head + part) * HD
+                out_ref[:, at : at + HD] = cols[:, start : start + HD]
+    total = jnp.sum(out_ref[...] * weight_ref[...].astype(F32), axis=1, keepdims=True)
+    gain_grad_ref[...] = total / gain_ref[...]
+
+
+def assemble(parts, weight_rows, gain_rows):
+    packs, share, per_pack = parts.shape
+    vmem = pl.BlockSpec(memory_space=pltpu.VMEM)
+    return pl.pallas_call(
+        assemble_kernel,
+        in_specs=[vmem] * 3,
+        out_specs=[vmem] * 2,
+        out_shape=[
+            jax.ShapeDtypeStruct((share, packs * per_pack), F32),
+            jax.ShapeDtypeStruct((share, 1), F32),
+        ],
+        compiler_params=pltpu.CompilerParams(vmem_limit_bytes=16 * 2**20),
+        name="assemble",
+    )(parts, weight_rows, gain_rows)
 
 
 def local(loader_rows, lengths, block_order, norm_gain, qkv_weight, upstream_grad):
@@ -265,7 +323,10 @@
     order_row = block_order[0]
     block_total = order_row.shape[0]
     piece = BLK * per_device // seq_count
-    first, cross, last, back_first, back_cross, back_last = route(my_index, order_row)
+    loader_blocks = loader_rows[0].reshape(per_device, BLK, model_width)
+    outgoing, _, cross, last, back_first, back_cross, back_last = route(
+        my_index, order_row, loader_blocks, norm_gain
+    )
 
     def exchange(x):
         x = x.reshape(seq_count, piece, model_width)
@@ -283,8 +344,6 @@
     upstream_own = upstream.T
     upstream_halo = halo(upstream).T
 
-    loader_blocks = loader_rows[0].reshape(per_device, BLK, model_width)
-    outgoing = norm_blocks(first, loader_blocks, norm_gain)
     spread = exchange(pick(cross, exchange(outgoing)))
     scaled = pick(last, spread.reshape(per_device, BLK, model_width)).reshape(row_count, model_width)
     scaled_halo = halo(scaled)
@@ -302,18 +361,11 @@
     inside = (positions >= 0) & (positions < block_total * BLK)
     ids = jnp.where(inside, counted, -1)
 
-    pairs = HEADS // 2 // GROUPS
-    attended, grads, shares = [], [], []
-    for group in range(GROUPS):
-        out, grad = attention_call(
-            ids, qkv_own, qkv_halo, upstream_own, upstream_halo, group * pairs, pairs
-        )
-        weight_local = nn(grad, scaled).astype(BF16)
-        shares.append(lax.psum_scatter(weight_local, DP, scatter_dimension=0, tiled=True))
-        attended.append(out)
-        grads.append(grad)
-    attention = jnp.concatenate(attended, axis=0).T[None]
-    grad_cols = jnp.concatenate(grads, axis=0).reshape(HEADS, 3, HD, row_count)
+    attended, grads = attention_call(ids, qkv_own, qkv_halo, upstream_own, upstream_halo)
+    weight_local = nn(grads, scaled).astype(BF16)
+    weight_part = lax.psum_scatter(weight_local, DP, scatter_dimension=0, tiled=True)
+    attention = attended.T[None]
+    grad_cols = grads.reshape(HEADS, 3, HD, row_count)
     grad_cols = grad_cols.transpose(1, 0, 2, 3).reshape(3 * model_width, row_count)
     input_grad = lax.dot_general(
         grad_cols, qkv_weight, (((0,), (1,)), ((), ())), preferred_element_type=F32
@@ -326,17 +378,14 @@
 
     share = model_width // seq_count
     per_pack = 3 * model_width // pack_count
-    partial = jnp.concatenate(shares, axis=0).T.reshape(seq_count, share, per_pack)
+    partial = weight_part.T.reshape(seq_count, share, per_pack)
     partial = lax.all_to_all(partial, SEQ, split_axis=0, concat_axis=0, tiled=True)
     summed = jnp.sum(partial.astype(F32), axis=0).astype(BF16)
     weight_cols = lax.all_gather(summed, DP, axis=0)
-    heads = HEADS // GROUPS // pack_count
-    weight_cols = weight_cols.reshape(pack_count, share, GROUPS, heads, 3, HD)
-    weight_grad = weight_cols.transpose(1, 4, 2, 0, 3, 5).reshape(share, 3 * model_width)
-    weight_grad = weight_grad.astype(F32) / pack_count
-    weight_rows = lax.dynamic_slice_in_dim(qkv_weight, my_index * share, share, 0).astype(F32)
-    gain_rows = lax.dynamic_slice_in_dim(norm_gain, my_index * share, share, 0)
-    gain_grad = jnp.sum(weight_rows * weight_grad, axis=1) / gain_rows
+    weight_rows = lax.dynamic_slice_in_dim(qkv_weight, my_index * share, share, 0)
+    gain_rows = lax.dynamic_slice_in_dim(norm_gain, my_index * share, share, 0)[:, None]
+    weight_grad, gain_grad = assemble(weight_cols, weight_rows, gain_rows)
+    gain_grad = gain_grad[:, 0]
     return (attention, loader_grad, weight_grad, gain_grad)
 
 

time: 258 us -> 226 us (0.88)
  Pallas kernels: 56.5 us -> 33.7 us
  local copies, waits for them, and re-layouts: 17.7 us -> 9.28 us
    pallas_call x1, Pallas kernels: 41.9 us -> 18.6 us  [attention_call(): pl.pallas_call(attention_kernel, grid=(pairs,), in_specs=[pl.BlockSpec((t...]
    div x3 -> x0, local copies, waits for them, and re-layouts: 6.73 us -> none  [local(): weight_grad = weight_grad.astype(F32) / pack_count]
    pallas_call x1 -> x2, Pallas kernels: 4.67 us -> 7.53 us  [the longest x1 5.92 us: route(): pl.pallas_call(route_kernel, in_specs=[smem, smem, pl.BlockSpec(memory_sp...]
    unnamed x36 -> x28, local copies, waits for them, and re-layouts: 7.75 us -> 5.13 us
    pallas_call x6 -> x5, Pallas kernels: 9.91 us -> 7.59 us  [whole_call(): pl.pallas_call(kernel, in_specs=[pl.BlockSpec(memory_space=pltpu.SMEM)] +...]
  transfers between devices with their start and end apart: 9 -> 9, of which waited for: 6 -> 6; matrix products, arithmetic and copies ran while one was open for 11% -> 13% of each run, Pallas kernels for 2% -> 2%
where the time goes in v5:
time: 226 us; the launch traced here: 225 us
  waiting for transfers between devices  52.9 us (23%)
  blocking collectives  42.5 us (19%)
  Pallas kernels  33.7 us (15%)
  starting transfers between devices  33.6 us (15%)
  matrix products  33.6 us (15%)
  between operations  14.3 us (6%)
  local copies, waits for them, and re-layouts  9.28 us (4%)
  other arithmetic  5.06 us (2%)
    all_to_all x1, blocking collectives, exchange(): return lax.all_to_all(x, SEQ, split_axis=0, concat_axis=0, tiled=True)  25.5 us
    pallas_call x1, Pallas kernels, attention_call(): pl.pallas_call(attention_kernel, grid=(pairs,), in_specs=[pl.BlockSpec((t...  18.6 us
    all_to_all x3, waiting for transfers between devices, exchange(): return lax.all_to_all(x, SEQ, split_axis=0, concat_axis=0, tiled=True)  17.7 us
    all_to_all x3, starting transfers between devices, exchange(): return lax.all_to_all(x, SEQ, split_axis=0, concat_axis=0, tiled=True)  17.3 us
    all_gather x1, blocking collectives, local(): weight_cols = lax.all_gather(summed, DP, axis=0)  17 us
    dot_general x2, matrix products, project(): lax.dot_general(qkv_weight, rows, (((0,), (1,)), ((), ())), preferred_ele...  16.2 us
    reduce_scatter x1, waiting for transfers between devices, local(): lax.psum_scatter(weight_local, DP, scatter_dimension=0, tiled=True)  12.7 us
    ppermute x2, waiting for transfers between devices, halo(): before = lax.ppermute(x[row_count - BLK:], SEQ, up)  11 us
  transfers between devices with their start and end apart: 9, of which 6 were waited for; matrix products, arithmetic and copies ran while one was open for 13% of the time, Pallas kernels for 2%

profile of v5, /device:TPU:1, one launch (start us, length us, event | category | flops | bytes accessed | tf_op | source)
XLA Modules:
  0.0 225.0 jit_solution(1965734642245659324)
XLA Ops:
  7.2 5.9 %route_blocks.1 = (bf16[4,128,1152]{2,1,0:T(8,128)(2,1)}, s32[4]{0:T(128)}, s32[16]{0:T(128)}, s32[4]{0:T(128)}, s32[4]{0:T(128)}, /*index=5*/s32[16]{0:T(128)}, s32[4]{0:T(128)}) custom-call(s32[1]{0:T(128)} %bitcast.1.me_ref, s32[64]{0:T(128)} %bitcast.65, bf16[4,128,1152]{2,1,0:T(8,128)(2,1)} %bitcast.49, f32[1152]{0:T(1024)} %gain_ref.3), custom_call_target="tpu_custom_call" | custom-call | tf_op jit(solution)/shard_map/route_blocks/pallas_call | solution.py:230
  13.1 8.6 %all-to-all-start = ((bf16[16,32,1152]{2,1,0:T(8,128)(2,1)}), bf16[16,32,1152]{2,1,0:T(8,128)(2,1)S(1)}, u32[]{:S(2)}, u32[]{:S(2)}) async-start(bf16[16,32,1152]{2,1,0:T(8,128)(2,1)} %bitcast.60), calls=%async_computation | async-start | bytes 2359296 | tf_op jit(solution)/shard_map/all_to_all | solution.py:333
  21.7 0.6 copy.33
  22.3 16.8 %all-to-all-done.source_ref = bf16[16,32,1152]{2,1,0:T(8,128)(2,1)S(1)} async-done(((bf16[16,32,1152]{2,1,0:T(8,128)(2,1)}), bf16[16,32,1152]{2,1,0:T(8,128)(2,1)S(1)}, u32[]{:S(2)}, u32[]{:S(2)}) %all-to-all-start) | async-done | bytes 1179680 | tf_op jit(solution)/shard_map/all_to_all | solution.py:333
  39.1 1.6 pick_blocks.4
  40.8 5.0 %all-to-all-start.1 = ((bf16[16,32,1152]{2,1,0:T(8,128)(2,1)}), bf16[16,32,1152]{2,1,0:T(8,128)(2,1)S(1)}, u32[]{:S(2)}, u32[]{:S(2)}) async-start(bf16[16,32,1152]{2,1,0:T(8,128)(2,1)} %pick_blocks.4), calls=%async_computation.1 | async-start | bytes 2359296 | tf_op jit(solution)/shard_map/all_to_all | solution.py:333
  45.8 0.0 reduce-scatter.2.cloned.1.call-start
  45.9 3.3 %collective-permute-start.2 = (bf16[128,1152]{0,1:T(8,128)(2,1)S(1)}, bf16[128,1152]{0,1:T(8,128)(2,1)S(1)}, u32[]{:S(2)}, u32[]{:S(2)}) collective-permute-start(bf16[128,1152]{0,1:T(8,128)(2,1)S(1)} %get-tuple-element.36), channel_id=1, source_target_pairs={{0,1},{1,2},{2,3},{3,4},{4,5},{5,6},{6,7},{7,8},{8,9},{9,10},{10,1... | collective-permute-start | bytes 884744 | tf_op jit(solution)/shard_map/ppermute | solution.py:339
  49.2 1.3 collective-permute-start.3
  50.5 0.1 copy.29
  50.6 0.2 reduce-window.8
  50.8 0.1 reduce.1
  50.9 0.3 convert_reduce_fusion
  51.2 0.6 and_select_fusion.row_ref
  51.8 0.9 reshape_select_fusion.col_ref
  52.8 11.0 %collective-permute-done.2 = bf16[128,1152]{0,1:T(8,128)(2,1)S(1)} collective-permute-done((bf16[128,1152]{0,1:T(8,128)(2,1)S(1)}, bf16[128,1152]{0,1:T(8,128)(2,1)S(1)}, u32[]{:S(2)}, u32[]{:S(2)}) %collective-permute-start.2) | collective-permute-done | bytes 294944 | tf_op jit(solution)/shard_map/ppermute | solution.py:339
  63.8 2.1 collective-permute-done.3
  65.9 0.9 maximum_bitcast_fusion.gh_ref
  66.8 0.6 pick_blocks.5
  67.5 4.4 %collective-permute-start = (bf16[128,1152]{1,0:T(8,128)(2,1)S(1)}, bf16[128,1152]{1,0:T(8,128)(2,1)S(1)}, u32[]{:S(2)}, u32[]{:S(2)}) collective-permute-start(bf16[128,1152]{1,0:T(8,128)(2,1)S(1)} %get-tuple-element.38), channel_id=1, source_target_pairs={{0,1},{1,2},{2,3},{3,4},{4,5},{5,6},{6,7},{7,8},{8,9},{9,10},{10,1... | collective-permute-start | bytes 884744 | tf_op jit(solution)/shard_map/ppermute | solution.py:339
  71.8 1.5 collective-permute-start.1
  73.3 0.0 slice-start.1
  73.3 11.5 %fusion.q_ref.k_ref.v_ref = bf16[3456,512]{1,0:T(8,128)(2,1)} fusion(bf16[512,1152]{1,0:T(8,128)(2,1)S(1)} %bitcast.52, bf16[1152,3456]{1,0:T(8,128)(2,1)} %param.10), kind=kOutput, calls=%fused_computation.2 | convolution fusion | flops 4078632960 | bytes 12681216 | tf_op jit(solution)/shard_map/dot_general | solution.py:352
  84.8 4.8 %fusion.1.qh_ref.kh_ref.vh_ref = bf16[3456,256]{1,0:T(8,128)(2,1)} fusion(bf16[1152,3456]{1,0:T(8,128)(2,1)S(1)} %bitcast.64, bf16[128,1152]{1,0:T(8,128)(2,1)S(1)} %collective-permute-done.1, bf16[128,1152]{1,0:T(8,128)(2,1)S(1)} %collective-permute-done), kind=kOutput, calls=%fused_computation.4 | convolution fusion | flops 2040496128 | bytes 10321920 | tf_op jit(solution)/shard_map/dot_general | solution.py:352
  89.6 18.6 %packed_attention.1 = (bf16[1152,512]{1,0:T(8,128)(2,1)}, bf16[3456,512]{1,0:T(8,128)(2,1)}) custom-call(s32[768,1]{1,0:T(8,128)} %reshape_select_fusion.col_ref, s32[1,768]{1,0:T(1,128)} %and_select_fusion.row_ref, bf16[3456,512]{1,0:T(8,128)(2,1)} %fusion.q_ref.k_ref.v_ref, bf16[3456,512]{1,0:T(8,128)(2,1)} %fusion.q_ref.k_ref.v_ref, ...), custom_call_target="tpu_custom_call" | custom-call | flops 3623878656 | bytes 11796480 | tf_op jit(solution)/shard_map/packed_attention/pallas_call | solution.py:120
  108.2 9.6 %convolution_convert_fusion = bf16[3456,1152]{1,0:T(8,128)(2,1)} fusion(bf16[3456,512]{1,0:T(8,128)(2,1)} %get-tuple-element.21, bf16[512,1152]{1,0:T(8,128)(2,1)S(1)} %bitcast.53), kind=kOutput, calls=%fused_computation | convolution fusion | flops 4080844800 | bytes 12681216 | tf_op jit(solution)/shard_map/dot_general | solution.py:27
  117.8 0.0 reduce-scatter.2.cloned.1.call-update
  117.8 2.0 copy-done.8
  119.8 0.3 copy.36
  120.1 7.7 %convolution_convert_fusion.3 = bf16[512,1152]{1,0:T(8,128)(2,1)S(1)} fusion(bf16[3456,512]{1,0:T(8,128)(2,1)S(1)} %bitcast.58, bf16[1152,3456]{1,0:T(8,128)(2,1)} %param.10), kind=kOutput, calls=%fused_computation.5 | convolution fusion | flops 4077453312 | bytes 12681216 | tf_op jit(solution)/shard_map/dot_general | solution.py:370
  127.9 0.6 pick_blocks.6
  128.5 25.5 %all_to_all.25.source_ref = bf16[16,32,1152]{2,1,0:T(8,128)(2,1)S(1)} all-to-all(bf16[16,32,1152]{2,1,0:T(8,128)(2,1)S(1)} %bitcast.48), channel_id=1, replica_groups=mesh['y'=4,'core'=2,'z'=4,'x'=4] {'z','x'}, dimensions={0} | all-to-all | bytes 2359296 | tf_op jit(solution)/shard_map/all_to_all | solution.py:333
  154.0 1.6 pick_blocks.7
  155.7 3.7 %all-to-all-start.3 = ((bf16[16,32,1152]{2,1,0:T(8,128)(2,1)}), bf16[16,32,1152]{2,1,0:T(8,128)(2,1)S(1)}, u32[]{:S(2)}, u32[]{:S(2)}) async-start(bf16[16,32,1152]{2,1,0:T(8,128)(2,1)} %pick_blocks.7), calls=%async_computation.3 | async-start | bytes 2359296 | tf_op jit(solution)/shard_map/all_to_all | solution.py:333
  159.4 12.7 %reduce-scatter.2.cloned.1.call-done = bf16[432,1152]{1,0:T(8,128)(2,1)} async-done(((bf16[3456,1152]{1,0:T(8,128)(2,1)}), bf16[432,1152]{1,0:T(8,128)(2,1)}) %reduce-scatter.2.cloned.1.call-update) | async-done | bytes 995344 | tf_op jit(solution)/shard_map/reduce_scatter | solution.py:366
  172.1 2.4 %copy.37 = bf16[1152,432]{1,0:T(8,128)(2,1)} copy(bf16[1152,432]{0,1:T(8,128)(2,1)} %bitcast.62) | data formatting | bytes 1990656 | tf_op jit(solution)/shard_map/transpose | solution.py:381
  174.5 0.9 all-to-all-done.3
  175.4 5.9 %all-to-all-start.4 = ((bf16[16,72,432]{2,1,0:T(8,128)(2,1)}), bf16[16,72,432]{2,1,0:T(8,128)(2,1)}, u32[]{:S(2)}, u32[]{:S(2)}) async-start(bf16[16,72,432]{2,1,0:T(8,128)(2,1)} %bitcast.26), calls=%async_computation.5 | async-start | bytes 2359296 | tf_op jit(solution)/shard_map/all_to_all | solution.py:382
  181.3 0.1 dynamic-slice_bitcast_fusion
  181.4 0.1 copy.38.gain_ref
  181.5 1.1 constant_dynamic-slice_fusion.weight_ref
  182.6 2.5 %copy.39 = bf16[1,512,1152]{2,1,0:T(8,128)(2,1)} copy(bf16[1,512,1152]{1,2,0:T(8,128)(2,1)} %bitcast.59) | data formatting | bytes 2359296
  185.1 3.0 %norm_back.1 = bf16[4,128,1152]{2,1,0:T(8,128)(2,1)} custom-call(s32[4]{0:T(128)S(1)} %copy-done.6, bf16[4,128,1152]{2,1,0:T(8,128)(2,1)S(1)} %bitcast.51, bf16[4,128,1152]{2,1,0:T(8,128)(2,1)S(1)} %bitcast.50, f32[1152]{0:T(1024)S(1)} %copy-done.1), custom_call_target="tpu_custom_call" | custom-call | flops 4718592 | bytes 4718592 | tf_op jit(solution)/shard_map/norm_back/pallas_call | solution.py:260
  188.1 9.3 %all-to-all-done.4 = bf16[16,72,432]{2,1,0:T(8,128)(2,1)} async-done(((bf16[16,72,432]{2,1,0:T(8,128)(2,1)}), bf16[16,72,432]{2,1,0:T(8,128)(2,1)}, u32[]{:S(2)}, u32[]{:S(2)}) %all-to-all-start.4) | async-done | bytes 995360 | tf_op jit(solution)/shard_map/all_to_all | solution.py:382
  197.5 1.5 reduce_sum.28
  198.9 17.0 %all-gather = bf16[576,432]{1,0:T(8,128)(2,1)S(1)} all-gather(bf16[72,432]{1,0:T(8,128)(2,1)S(1)} %reduce_sum.28), channel_id=2, replica_groups=mesh['y'=4,'core'=2,'z'=4,'x'=4] {'y','core'}, dimensions={0}, use_global_device_ids=true | all-gather | bytes 559872 | tf_op jit(solution)/shard_map/all_gather | solution.py:384
  215.9 1.6 assemble.1
  217.5 0.6 reduce.2
  (31 shorter events, 0.2 us)
Async XLA Ops:
  13.1 8.6 %copy-start.9 = (bf16[1,512,1152]{2,1,0:T(8,128)(2,1)S(1)}, bf16[1,512,1152]{2,1,0:T(8,128)(2,1)}, u32[]{:S(2)}) copy-start(bf16[1,512,1152]{2,1,0:T(8,128)(2,1)} %param.11) | copy-start | bytes 3538948
  13.1 26.0 %all-to-all-start = ((bf16[16,32,1152]{2,1,0:T(8,128)(2,1)}), bf16[16,32,1152]{2,1,0:T(8,128)(2,1)S(1)}, u32[]{:S(2)}, u32[]{:S(2)}) async-start(bf16[16,32,1152]{2,1,0:T(8,128)(2,1)} %bitcast.60), calls=%async_computation | async-start | bytes 2359296 | tf_op jit(solution)/shard_map/all_to_all | solution.py:333
  21.7 17.5 %copy-start.5 = (s32[16]{0:T(128)S(1)}, s32[16]{0:T(128)}, u32[]{:S(2)}) copy-start(s32[16]{0:T(128)} %get-tuple-element.15.index_ref) | copy-start | bytes 196
  22.3 23.5 %copy-start.7 = (bf16[1,512,1152]{1,2,0:T(8,128)(2,1)}, bf16[1,512,1152]{1,2,0:T(8,128)(2,1)S(1)}, u32[]{:S(2)}) copy-start(bf16[1,512,1152]{1,2,0:T(8,128)(2,1)S(1)} %copy.33) | copy-start | bytes 3538948
  40.8 26.0 %all-to-all-start.1 = ((bf16[16,32,1152]{2,1,0:T(8,128)(2,1)}), bf16[16,32,1152]{2,1,0:T(8,128)(2,1)S(1)}, u32[]{:S(2)}, u32[]{:S(2)}) async-start(bf16[16,32,1152]{2,1,0:T(8,128)(2,1)} %pick_blocks.4), calls=%async_computation.1 | async-start | bytes 2359296 | tf_op jit(solution)/shard_map/all_to_all | solution.py:333
  45.8 4.7 %copy-start.10 = (s32[1,128]{1,0:T(1,128)S(1)}, s32[1,128]{1,0:T(1,128)}, u32[]{:S(2)}) copy-start(s32[1,128]{1,0:T(1,128)} %param.7) | copy-start | bytes 1540
  45.8 126.3 %reduce-scatter.2.cloned.1.call-start = ((), (), s32[]{:S(2)}) async-start(), calls=%async_computation.6 | async-start | bytes 8957952 | tf_op jit(solution)/shard_map/reduce_scatter | solution.py:366
  45.9 20.8 %copy-start.4 = (s32[4]{0:T(128)S(1)}, s32[4]{0:T(128)}, u32[]{:S(2)}) copy-start(s32[4]{0:T(128)} %get-tuple-element.14.index_ref) | copy-start | bytes 52
  45.9 17.9 %collective-permute-start.2 = (bf16[128,1152]{0,1:T(8,128)(2,1)S(1)}, bf16[128,1152]{0,1:T(8,128)(2,1)S(1)}, u32[]{:S(2)}, u32[]{:S(2)}) collective-permute-start(bf16[128,1152]{0,1:T(8,128)(2,1)S(1)} %get-tuple-element.36), channel_id=1, source_target_pairs={{0,1},{1,2},{2,3},{3,4},{4,5},{5,6},{6,7},{7,8},{8,9},{9,10},{10,1... | collective-permute-start | bytes 884744 | tf_op jit(solution)/shard_map/ppermute | solution.py:339
  49.2 16.7 %collective-permute-start.3 = (bf16[128,1152]{0,1:T(8,128)(2,1)S(1)}, bf16[128,1152]{0,1:T(8,128)(2,1)S(1)}, u32[]{:S(2)}, u32[]{:S(2)}) collective-permute-start(bf16[128,1152]{0,1:T(8,128)(2,1)S(1)} %get-tuple-element.37), channel_id=1, source_target_pairs={{1,0},{2,1},{3,2},{4,3},{5,4},{6,5},{7,6},{8,7},{9,8},{10,9},{11,1... | collective-permute-start | bytes 884744 | tf_op jit(solution)/shard_map/ppermute | solution.py:340
  67.4 17.4 %slice-start = ((s8[7962624]{0:T(1024)(128)(4,1)}), s8[4194304]{0:T(1024)(128)(4,1)S(1)}, s32[]{:S(2)}) async-start(s8[7962624]{0:T(1024)(128)(4,1)} %bitcast.63), calls=%async_computation.7 | async-start | bytes 8388608
  67.5 17.3 %collective-permute-start = (bf16[128,1152]{1,0:T(8,128)(2,1)S(1)}, bf16[128,1152]{1,0:T(8,128)(2,1)S(1)}, u32[]{:S(2)}, u32[]{:S(2)}) collective-permute-start(bf16[128,1152]{1,0:T(8,128)(2,1)S(1)} %get-tuple-element.38), channel_id=1, source_target_pairs={{0,1},{1,2},{2,3},{3,4},{4,5},{5,6},{6,7},{7,8},{8,9},{9,10},{10,1... | collective-permute-start | bytes 884744 | tf_op jit(solution)/shard_map/ppermute | solution.py:339
  71.8 13.0 %collective-permute-start.1 = (bf16[128,1152]{1,0:T(8,128)(2,1)S(1)}, bf16[128,1152]{1,0:T(8,128)(2,1)S(1)}, u32[]{:S(2)}, u32[]{:S(2)}) collective-permute-start(bf16[128,1152]{1,0:T(8,128)(2,1)S(1)} %get-tuple-element.39), channel_id=1, source_target_pairs={{1,0},{2,1},{3,2},{4,3},{5,4},{6,5},{7,6},{8,7},{9,8},{10,9},{11,1... | collective-permute-start | bytes 884744 | tf_op jit(solution)/shard_map/ppermute | solution.py:340
  73.3 11.5 %slice-start.1 = ((s8[7962624]{0:T(1024)(128)(4,1)}), s8[3768320]{0:T(1024)(128)(4,1)S(1)}, s32[]{:S(2)}) async-start(s8[7962624]{0:T(1024)(128)(4,1)} %bitcast.63), calls=%async_computation.8 | async-start | bytes 7536640
  117.8 2.0 copy-start.8
  120.1 7.7 %copy-start.3 = (s32[4]{0:T(128)S(1)}, s32[4]{0:T(128)}, u32[]{:S(2)}) copy-start(s32[4]{0:T(128)} %get-tuple-element.20.index_ref) | copy-start | bytes 52
  128.5 25.5 %copy-start.2 = (s32[16]{0:T(128)S(1)}, s32[16]{0:T(128)}, u32[]{:S(2)}) copy-start(s32[16]{0:T(128)} %get-tuple-element.19.index_ref) | copy-start | bytes 196
  155.7 19.8 %all-to-all-start.3 = ((bf16[16,32,1152]{2,1,0:T(8,128)(2,1)}), bf16[16,32,1152]{2,1,0:T(8,128)(2,1)S(1)}, u32[]{:S(2)}, u32[]{:S(2)}) async-start(bf16[16,32,1152]{2,1,0:T(8,128)(2,1)} %pick_blocks.7), calls=%async_computation.3 | async-start | bytes 2359296 | tf_op jit(solution)/shard_map/all_to_all | solution.py:333
  175.4 5.9 %copy-start.1 = (f32[1152]{0:T(1024)S(1)}, f32[1152]{0:T(1024)}, u32[]{:S(2)}) copy-start(f32[1152]{0:T(1024)} %gain_ref.3) | copy-start | bytes 13828
  175.4 22.0 %all-to-all-start.4 = ((bf16[16,72,432]{2,1,0:T(8,128)(2,1)}), bf16[16,72,432]{2,1,0:T(8,128)(2,1)}, u32[]{:S(2)}, u32[]{:S(2)}) async-start(bf16[16,72,432]{2,1,0:T(8,128)(2,1)} %bitcast.26), calls=%async_computation.5 | async-start | bytes 2359296 | tf_op jit(solution)/shard_map/all_to_all | solution.py:382
  182.6 2.5 %copy-start = (bf16[1,512,1152]{2,1,0:T(8,128)(2,1)S(1)}, bf16[1,512,1152]{2,1,0:T(8,128)(2,1)}, u32[]{:S(2)}) copy-start(bf16[1,512,1152]{2,1,0:T(8,128)(2,1)} %param.6) | copy-start | bytes 3538948
  182.6 2.5 %copy-start.6 = (s32[4]{0:T(128)S(1)}, s32[4]{0:T(128)}, u32[]{:S(2)}) copy-start(s32[4]{0:T(128)} %get-tuple-element.18.index_ref) | copy-start | bytes 52
Sparse Core Ops, SparseCore 0:
  117.9 54.0 reduce-scatter.1

commit v6 on v5

--- a/solution.py
+++ b/solution.py
@@ -32,8 +32,8 @@
 
 
 def attention_kernel(
-    col_ref, row_ref, q_ref, k_ref, v_ref, qh_ref, kh_ref, vh_ref, g_ref, gh_ref,
-    o_ref, d_ref, bias_ref, o_s, d_s,
+    col_ref, row_ref, q_ref, k_ref, v_ref, qh_ref, kh_ref, vh_ref, g_ref, gh_ref, rows_ref,
+    o_ref, d_ref, w_ref, bias_ref, o_s, d_s,
 ):
     blocks = q_ref.shape[1] // BLK
     rows = q_ref.shape[1]
@@ -106,10 +106,15 @@
             at = slice((3 * head + part) * HD, (3 * head + part + 1) * HD)
             if factor is not None:
                 d_s[at, :] = d_s[at, :] * factor
-    d_ref[...] = d_s[...].astype(BF16)
-
-
-def attention_call(ids, own, halo, g_own, g_halo, first_pair=0, pairs=HEADS // 2):
+    grads = d_s[...].astype(BF16)
+    d_ref[...] = grads
+    third = rows_ref.shape[1] // 3
+    for part in range(3):
+        cols = slice(part * third, (part + 1) * third)
+        w_ref[:, cols] = nn(grads, rows_ref[:, cols]).astype(BF16)
+
+
+def attention_call(ids, own, halo, g_own, g_halo, scaled, first_pair=0, pairs=HEADS // 2):
     rows, rim = own.shape[1], halo.shape[1]
     total, blocks = rows + rim, rows // BLK
     per_part = HEADS // 2
@@ -126,14 +131,17 @@
             spec(rows, 0), spec(rows, 1), spec(rows, 2),
             spec(rim, 0), spec(rim, 1), spec(rim, 2),
             spec(rows, 0), spec(rim, 0),
+            pl.BlockSpec(scaled.shape, lambda i: (0, 0)),
         ],
         out_specs=[
             pl.BlockSpec((PAIR, rows), lambda i: (i, 0)),
             pl.BlockSpec((3 * PAIR, rows), lambda i: (i, 0)),
+            pl.BlockSpec((3 * PAIR, scaled.shape[1]), lambda i: (i, 0)),
         ],
         out_shape=[
             jax.ShapeDtypeStruct((pairs * PAIR, rows), BF16),
             jax.ShapeDtypeStruct((pairs * 3 * PAIR, rows), BF16),
+            jax.ShapeDtypeStruct((pairs * 3 * PAIR, scaled.shape[1]), BF16),
         ],
         scratch_shapes=[
             pltpu.VMEM((blocks + 2, BLK, 3 * BLK), F32),
@@ -146,7 +154,7 @@
             transcendentals=pairs * 2 * 16 * BLK * BLK,
         ),
         name="packed_attention",
-    )(ids[:, None], ids[None, :], own, own, own, halo, halo, halo, g_own, g_halo)
+    )(ids[:, None], ids[None, :], own, own, own, halo, halo, halo, g_own, g_halo, scaled)
 
 
 def route_kernel(
@@ -361,8 +369,9 @@
     inside = (positions >= 0) & (positions < block_total * BLK)
     ids = jnp.where(inside, counted, -1)
 
-    attended, grads = attention_call(ids, qkv_own, qkv_halo, upstream_own, upstream_halo)
-    weight_local = nn(grads, scaled).astype(BF16)
+    attended, grads, weight_local = attention_call(
+        ids, qkv_own, qkv_halo, upstream_own, upstream_halo, scaled
+    )
     weight_part = lax.psum_scatter(weight_local, DP, scatter_dimension=0, tiled=True)
     attention = attended.T[None]
     grad_cols = grads.reshape(HEADS, 3, HD, row_count)

time: 226 us -> 223 us (0.987)
  matrix products: 33.6 us -> 23.9 us
  Pallas kernels: 33.7 us -> 40.1 us
    dot_general x1 -> x0, matrix products: 9.63 us -> none  [nn(): lax.dot_general(a, b, (((1,), (0,)), ((), ())), preferred_element_type=F32)]
    pallas_call x1, Pallas kernels: 18.6 us -> 25 us  [attention_call(): pl.pallas_call(attention_kernel, grid=(pairs,), in_specs=[pl.BlockSpec((t...]
    unnamed x28 -> x30, local copies, waits for them, and re-layouts: 5.13 us -> 5.13 us
where the time goes in v6:
time: 223 us; the launch traced here: 222 us
  waiting for transfers between devices  52.9 us (24%)
  blocking collectives  42.6 us (19%)
  Pallas kernels  40.1 us (18%)
  starting transfers between devices  33.6 us (15%)
  matrix products  23.9 us (11%)
  between operations  14.4 us (6%)
  local copies, waits for them, and re-layouts  9.28 us (4%)
  other arithmetic  5.05 us (2%)
    all_to_all x1, blocking collectives, exchange(): return lax.all_to_all(x, SEQ, split_axis=0, concat_axis=0, tiled=True)  25.5 us
    pallas_call x1, Pallas kernels, attention_call(): pl.pallas_call(attention_kernel, grid=(pairs,), in_specs=[pl.BlockSpec((t...  25 us
    all_to_all x3, waiting for transfers between devices, exchange(): return lax.all_to_all(x, SEQ, split_axis=0, concat_axis=0, tiled=True)  17.8 us
    all_to_all x3, starting transfers between devices, exchange(): return lax.all_to_all(x, SEQ, split_axis=0, concat_axis=0, tiled=True)  17.3 us
    all_gather x1, blocking collectives, local(): weight_cols = lax.all_gather(summed, DP, axis=0)  17.1 us
    dot_general x2, matrix products, project(): lax.dot_general(qkv_weight, rows, (((0,), (1,)), ((), ())), preferred_ele...  16.2 us
    reduce_scatter x1, waiting for transfers between devices, local(): lax.psum_scatter(weight_local, DP, scatter_dimension=0, tiled=True)  12.7 us
    ppermute x2, waiting for transfers between devices, halo(): before = lax.ppermute(x[row_count - BLK:], SEQ, up)  11.1 us
  transfers between devices with their start and end apart: 9, of which 6 were waited for; matrix products, arithmetic and copies ran while one was open for 13% of the time, Pallas kernels for 2%

profile of v6, /device:TPU:1, one launch (start us, length us, event | category | flops | bytes accessed | tf_op | source)
XLA Modules:
  0.0 221.7 jit_solution(5770294786540675)
XLA Ops:
  7.2 5.9 %route_blocks.1 = (bf16[4,128,1152]{2,1,0:T(8,128)(2,1)}, s32[4]{0:T(128)}, s32[16]{0:T(128)}, s32[4]{0:T(128)}, s32[4]{0:T(128)}, /*index=5*/s32[16]{0:T(128)}, s32[4]{0:T(128)}) custom-call(s32[1]{0:T(128)} %bitcast.1.me_ref, s32[64]{0:T(128)} %bitcast.63, bf16[4,128,1152]{2,1,0:T(8,128)(2,1)} %bitcast.49, f32[1152]{0:T(1024)} %gain_ref.3), custom_call_target="tpu_custom_call" | custom-call | tf_op jit(solution)/shard_map/route_blocks/pallas_call | solution.py:238
  13.1 8.6 %all-to-all-start = ((bf16[16,32,1152]{2,1,0:T(8,128)(2,1)}), bf16[16,32,1152]{2,1,0:T(8,128)(2,1)S(1)}, u32[]{:S(2)}, u32[]{:S(2)}) async-start(bf16[16,32,1152]{2,1,0:T(8,128)(2,1)} %bitcast.58), calls=%async_computation | async-start | bytes 2359296 | tf_op jit(solution)/shard_map/all_to_all | solution.py:341
  21.7 0.6 copy.33
  22.3 16.8 %all-to-all-done.source_ref = bf16[16,32,1152]{2,1,0:T(8,128)(2,1)S(1)} async-done(((bf16[16,32,1152]{2,1,0:T(8,128)(2,1)}), bf16[16,32,1152]{2,1,0:T(8,128)(2,1)S(1)}, u32[]{:S(2)}, u32[]{:S(2)}) %all-to-all-start) | async-done | bytes 1179680 | tf_op jit(solution)/shard_map/all_to_all | solution.py:341
  39.1 1.6 pick_blocks.4
  40.8 5.0 %all-to-all-start.1 = ((bf16[16,32,1152]{2,1,0:T(8,128)(2,1)}), bf16[16,32,1152]{2,1,0:T(8,128)(2,1)S(1)}, u32[]{:S(2)}, u32[]{:S(2)}) async-start(bf16[16,32,1152]{2,1,0:T(8,128)(2,1)} %pick_blocks.4), calls=%async_computation.1 | async-start | bytes 2359296 | tf_op jit(solution)/shard_map/all_to_all | solution.py:341
  45.8 0.0 reduce-scatter.2.cloned.1.call-start
  45.9 3.3 %collective-permute-start.2 = (bf16[128,1152]{0,1:T(8,128)(2,1)S(1)}, bf16[128,1152]{0,1:T(8,128)(2,1)S(1)}, u32[]{:S(2)}, u32[]{:S(2)}) collective-permute-start(bf16[128,1152]{0,1:T(8,128)(2,1)S(1)} %get-tuple-element.38), channel_id=1, source_target_pairs={{0,1},{1,2},{2,3},{3,4},{4,5},{5,6},{6,7},{7,8},{8,9},{9,10},{10,1... | collective-permute-start | bytes 884744 | tf_op jit(solution)/shard_map/ppermute | solution.py:347
  49.2 1.3 collective-permute-start.3
  50.5 0.1 copy.29
  50.6 0.2 reduce-window.8
  50.8 0.1 reduce.1
  50.9 0.3 convert_reduce_fusion
  51.2 0.6 and_select_fusion.row_ref
  51.8 0.9 reshape_select_fusion.col_ref
  52.7 11.0 %collective-permute-done.2 = bf16[128,1152]{0,1:T(8,128)(2,1)S(1)} collective-permute-done((bf16[128,1152]{0,1:T(8,128)(2,1)S(1)}, bf16[128,1152]{0,1:T(8,128)(2,1)S(1)}, u32[]{:S(2)}, u32[]{:S(2)}) %collective-permute-start.2) | collective-permute-done | bytes 294944 | tf_op jit(solution)/shard_map/ppermute | solution.py:347
  63.8 2.1 collective-permute-done.3
  65.9 0.9 maximum_bitcast_fusion.gh_ref
  66.7 0.6 pick_blocks.5
  67.4 0.0 slice-start
  67.5 4.4 %collective-permute-start = (bf16[128,1152]{1,0:T(8,128)(2,1)S(1)}, bf16[128,1152]{1,0:T(8,128)(2,1)S(1)}, u32[]{:S(2)}, u32[]{:S(2)}) collective-permute-start(bf16[128,1152]{1,0:T(8,128)(2,1)S(1)} %get-tuple-element.40), channel_id=1, source_target_pairs={{0,1},{1,2},{2,3},{3,4},{4,5},{5,6},{6,7},{7,8},{8,9},{9,10},{10,1... | collective-permute-start | bytes 884744 | tf_op jit(solution)/shard_map/ppermute | solution.py:347
  71.8 1.5 collective-permute-start.1
  73.3 0.0 slice-start.1
  73.3 11.5 %fusion.q_ref.k_ref.v_ref = bf16[3456,512]{1,0:T(8,128)(2,1)} fusion(bf16[512,1152]{1,0:T(8,128)(2,1)S(1)} %bitcast.45, bf16[1152,3456]{1,0:T(8,128)(2,1)} %param.10), kind=kOutput, calls=%fused_computation.1 | convolution fusion | flops 4078632960 | bytes 12681216 | tf_op jit(solution)/shard_map/dot_general | solution.py:360
  84.8 4.8 %fusion.1.qh_ref.kh_ref.vh_ref = bf16[3456,256]{1,0:T(8,128)(2,1)} fusion(bf16[1152,3456]{1,0:T(8,128)(2,1)S(1)} %bitcast.62, bf16[128,1152]{1,0:T(8,128)(2,1)S(1)} %collective-permute-done.1, bf16[128,1152]{1,0:T(8,128)(2,1)S(1)} %collective-permute-done), kind=kOutput, calls=%fused_computation.3 | convolution fusion | flops 2040496128 | bytes 10321920 | tf_op jit(solution)/shard_map/dot_general | solution.py:360
  89.6 25.0 %packed_attention.1 = (bf16[1152,512]{1,0:T(8,128)(2,1)}, bf16[3456,512]{1,0:T(8,128)(2,1)}, bf16[3456,1152]{1,0:T(8,128)(2,1)}) custom-call(s32[768,1]{1,0:T(8,128)} %reshape_select_fusion.col_ref, s32[1,768]{1,0:T(1,128)} %and_select_fusion.row_ref, bf16[3456,512]{1,0:T(8,128)(2,1)} %fusion.q_ref.k_ref.v_ref, bf16[3456,512]{1,0:T(8,128)(2,1)} %fusion.q_ref.k_ref.v_ref, ...), custom_call_target="tpu_custom_call" | custom-call | flops 3623878656 | bytes 11796480 | tf_op jit(solution)/shard_map/packed_attention/pallas_call | solution.py:125
  114.5 0.0 reduce-scatter.2.cloned.1.call-update
  114.6 2.0 copy-done.9
  116.5 0.3 copy.36
  116.9 7.7 %convolution_convert_fusion.2 = bf16[512,1152]{1,0:T(8,128)(2,1)S(1)} fusion(bf16[3456,512]{1,0:T(8,128)(2,1)S(1)} %bitcast.56, bf16[1152,3456]{1,0:T(8,128)(2,1)} %param.10), kind=kOutput, calls=%fused_computation.4 | convolution fusion | flops 4077453312 | bytes 12681216 | tf_op jit(solution)/shard_map/dot_general | solution.py:379
  124.6 0.6 pick_blocks.6
  125.2 25.5 %all_to_all.25.source_ref = bf16[16,32,1152]{2,1,0:T(8,128)(2,1)S(1)} all-to-all(bf16[16,32,1152]{2,1,0:T(8,128)(2,1)S(1)} %bitcast.48), channel_id=1, replica_groups=mesh['y'=4,'core'=2,'z'=4,'x'=4] {'z','x'}, dimensions={0} | all-to-all | bytes 2359296 | tf_op jit(solution)/shard_map/all_to_all | solution.py:341
  150.8 1.6 pick_blocks.7
  152.4 3.7 %all-to-all-start.3 = ((bf16[16,32,1152]{2,1,0:T(8,128)(2,1)}), bf16[16,32,1152]{2,1,0:T(8,128)(2,1)S(1)}, u32[]{:S(2)}, u32[]{:S(2)}) async-start(bf16[16,32,1152]{2,1,0:T(8,128)(2,1)} %pick_blocks.7), calls=%async_computation.3 | async-start | bytes 2359296 | tf_op jit(solution)/shard_map/all_to_all | solution.py:341
  156.1 12.7 %reduce-scatter.2.cloned.1.call-done = bf16[432,1152]{1,0:T(8,128)(2,1)} async-done(((bf16[3456,1152]{1,0:T(8,128)(2,1)}), bf16[432,1152]{1,0:T(8,128)(2,1)}) %reduce-scatter.2.cloned.1.call-update) | async-done | bytes 995344 | tf_op jit(solution)/shard_map/reduce_scatter | solution.py:375
  168.8 2.4 %copy.37 = bf16[1152,432]{1,0:T(8,128)(2,1)} copy(bf16[1152,432]{0,1:T(8,128)(2,1)} %bitcast.60) | data formatting | bytes 1990656 | tf_op jit(solution)/shard_map/transpose | solution.py:390
  171.2 1.0 all-to-all-done.3
  172.2 5.8 %all-to-all-start.4 = ((bf16[16,72,432]{2,1,0:T(8,128)(2,1)}), bf16[16,72,432]{2,1,0:T(8,128)(2,1)}, u32[]{:S(2)}, u32[]{:S(2)}) async-start(bf16[16,72,432]{2,1,0:T(8,128)(2,1)} %bitcast.26), calls=%async_computation.5 | async-start | bytes 2359296 | tf_op jit(solution)/shard_map/all_to_all | solution.py:391
  178.0 0.1 dynamic-slice_bitcast_fusion
  178.1 0.1 copy.38.gain_ref
  178.2 1.1 constant_dynamic-slice_fusion.weight_ref
  179.3 2.5 %copy.39 = bf16[1,512,1152]{2,1,0:T(8,128)(2,1)} copy(bf16[1,512,1152]{1,2,0:T(8,128)(2,1)} %bitcast.57) | data formatting | bytes 2359296
  181.8 3.0 %norm_back.1 = bf16[4,128,1152]{2,1,0:T(8,128)(2,1)} custom-call(s32[4]{0:T(128)S(1)} %copy-done.7, bf16[4,128,1152]{2,1,0:T(8,128)(2,1)S(1)} %bitcast.51, bf16[4,128,1152]{2,1,0:T(8,128)(2,1)S(1)} %bitcast.50, f32[1152]{0:T(1024)S(1)} %copy-done.2), custom_call_target="tpu_custom_call" | custom-call | flops 4718592 | bytes 4718592 | tf_op jit(solution)/shard_map/norm_back/pallas_call | solution.py:268
  184.8 9.3 %all-to-all-done.4 = bf16[16,72,432]{2,1,0:T(8,128)(2,1)} async-done(((bf16[16,72,432]{2,1,0:T(8,128)(2,1)}), bf16[16,72,432]{2,1,0:T(8,128)(2,1)}, u32[]{:S(2)}, u32[]{:S(2)}) %all-to-all-start.4) | async-done | bytes 995360 | tf_op jit(solution)/shard_map/all_to_all | solution.py:391
  194.1 1.5 reduce_sum.28
  195.6 17.1 %all-gather = bf16[576,432]{1,0:T(8,128)(2,1)S(1)} all-gather(bf16[72,432]{1,0:T(8,128)(2,1)S(1)} %reduce_sum.28), channel_id=2, replica_groups=mesh['y'=4,'core'=2,'z'=4,'x'=4] {'y','core'}, dimensions={0}, use_global_device_ids=true | all-gather | bytes 559872 | tf_op jit(solution)/shard_map/all_gather | solution.py:393
  212.6 1.6 assemble.1
  214.2 0.6 reduce.2
  (32 shorter events, 0.2 us)
Async XLA Ops:
  13.1 8.6 %copy-start.10 = (bf16[1,512,1152]{2,1,0:T(8,128)(2,1)S(1)}, bf16[1,512,1152]{2,1,0:T(8,128)(2,1)}, u32[]{:S(2)}) copy-start(bf16[1,512,1152]{2,1,0:T(8,128)(2,1)} %param.11) | copy-start | bytes 3538948
  13.1 26.0 %all-to-all-start = ((bf16[16,32,1152]{2,1,0:T(8,128)(2,1)}), bf16[16,32,1152]{2,1,0:T(8,128)(2,1)S(1)}, u32[]{:S(2)}, u32[]{:S(2)}) async-start(bf16[16,32,1152]{2,1,0:T(8,128)(2,1)} %bitcast.58), calls=%async_computation | async-start | bytes 2359296 | tf_op jit(solution)/shard_map/all_to_all | solution.py:341
  21.7 17.4 %copy-start.6 = (s32[16]{0:T(128)S(1)}, s32[16]{0:T(128)}, u32[]{:S(2)}) copy-start(s32[16]{0:T(128)} %get-tuple-element.16.index_ref) | copy-start | bytes 196
  22.3 23.5 %copy-start.8 = (bf16[1,512,1152]{1,2,0:T(8,128)(2,1)}, bf16[1,512,1152]{1,2,0:T(8,128)(2,1)S(1)}, u32[]{:S(2)}) copy-start(bf16[1,512,1152]{1,2,0:T(8,128)(2,1)S(1)} %copy.33) | copy-start | bytes 3538948
  40.8 26.0 %all-to-all-start.1 = ((bf16[16,32,1152]{2,1,0:T(8,128)(2,1)}), bf16[16,32,1152]{2,1,0:T(8,128)(2,1)S(1)}, u32[]{:S(2)}, u32[]{:S(2)}) async-start(bf16[16,32,1152]{2,1,0:T(8,128)(2,1)} %pick_blocks.4), calls=%async_computation.1 | async-start | bytes 2359296 | tf_op jit(solution)/shard_map/all_to_all | solution.py:341
  45.8 4.7 %copy-start.11 = (s32[1,128]{1,0:T(1,128)S(1)}, s32[1,128]{1,0:T(1,128)}, u32[]{:S(2)}) copy-start(s32[1,128]{1,0:T(1,128)} %param.7) | copy-start | bytes 1540
  45.8 123.0 %reduce-scatter.2.cloned.1.call-start = ((), (), s32[]{:S(2)}) async-start(), calls=%async_computation.6 | async-start | bytes 8957952 | tf_op jit(solution)/shard_map/reduce_scatter | solution.py:375
  45.9 20.8 %copy-start.5 = (s32[4]{0:T(128)S(1)}, s32[4]{0:T(128)}, u32[]{:S(2)}) copy-start(s32[4]{0:T(128)} %get-tuple-element.15.index_ref) | copy-start | bytes 52
  45.9 17.9 %collective-permute-start.2 = (bf16[128,1152]{0,1:T(8,128)(2,1)S(1)}, bf16[128,1152]{0,1:T(8,128)(2,1)S(1)}, u32[]{:S(2)}, u32[]{:S(2)}) collective-permute-start(bf16[128,1152]{0,1:T(8,128)(2,1)S(1)} %get-tuple-element.38), channel_id=1, source_target_pairs={{0,1},{1,2},{2,3},{3,4},{4,5},{5,6},{6,7},{7,8},{8,9},{9,10},{10,1... | collective-permute-start | bytes 884744 | tf_op jit(solution)/shard_map/ppermute | solution.py:347
  49.2 16.7 %collective-permute-start.3 = (bf16[128,1152]{0,1:T(8,128)(2,1)S(1)}, bf16[128,1152]{0,1:T(8,128)(2,1)S(1)}, u32[]{:S(2)}, u32[]{:S(2)}) collective-permute-start(bf16[128,1152]{0,1:T(8,128)(2,1)S(1)} %get-tuple-element.39), channel_id=1, source_target_pairs={{1,0},{2,1},{3,2},{4,3},{5,4},{6,5},{7,6},{8,7},{9,8},{10,9},{11,1... | collective-permute-start | bytes 884744 | tf_op jit(solution)/shard_map/ppermute | solution.py:348
  67.4 17.4 %copy-start = (bf16[4,128,1152]{2,1,0:T(8,128)(2,1)}, bf16[4,128,1152]{2,1,0:T(8,128)(2,1)S(1)}, u32[]{:S(2)}) copy-start(bf16[4,128,1152]{2,1,0:T(8,128)(2,1)S(1)} %pick_blocks.5) | copy-start | bytes 3538948
  67.4 17.4 %slice-start = ((s8[7962624]{0:T(1024)(128)(4,1)}), s8[4194304]{0:T(1024)(128)(4,1)S(1)}, s32[]{:S(2)}) async-start(s8[7962624]{0:T(1024)(128)(4,1)} %bitcast.61), calls=%async_computation.7 | async-start | bytes 8388608
  67.5 17.3 %collective-permute-start = (bf16[128,1152]{1,0:T(8,128)(2,1)S(1)}, bf16[128,1152]{1,0:T(8,128)(2,1)S(1)}, u32[]{:S(2)}, u32[]{:S(2)}) collective-permute-start(bf16[128,1152]{1,0:T(8,128)(2,1)S(1)} %get-tuple-element.40), channel_id=1, source_target_pairs={{0,1},{1,2},{2,3},{3,4},{4,5},{5,6},{6,7},{7,8},{8,9},{9,10},{10,1... | collective-permute-start | bytes 884744 | tf_op jit(solution)/shard_map/ppermute | solution.py:347
  71.8 13.0 %collective-permute-start.1 = (bf16[128,1152]{1,0:T(8,128)(2,1)S(1)}, bf16[128,1152]{1,0:T(8,128)(2,1)S(1)}, u32[]{:S(2)}, u32[]{:S(2)}) collective-permute-start(bf16[128,1152]{1,0:T(8,128)(2,1)S(1)} %get-tuple-element.41), channel_id=1, source_target_pairs={{1,0},{2,1},{3,2},{4,3},{5,4},{6,5},{7,6},{8,7},{9,8},{10,9},{11,1... | collective-permute-start | bytes 884744 | tf_op jit(solution)/shard_map/ppermute | solution.py:348
  73.3 11.5 %slice-start.1 = ((s8[7962624]{0:T(1024)(128)(4,1)}), s8[3768320]{0:T(1024)(128)(4,1)S(1)}, s32[]{:S(2)}) async-start(s8[7962624]{0:T(1024)(128)(4,1)} %bitcast.61), calls=%async_computation.8 | async-start | bytes 7536640
  114.5 2.0 copy-start.9
  116.9 7.7 %copy-start.4 = (s32[4]{0:T(128)S(1)}, s32[4]{0:T(128)}, u32[]{:S(2)}) copy-start(s32[4]{0:T(128)} %get-tuple-element.21.index_ref) | copy-start | bytes 52
  125.2 25.5 %copy-start.3 = (s32[16]{0:T(128)S(1)}, s32[16]{0:T(128)}, u32[]{:S(2)}) copy-start(s32[16]{0:T(128)} %get-tuple-element.20.index_ref) | copy-start | bytes 196
  152.4 19.8 %all-to-all-start.3 = ((bf16[16,32,1152]{2,1,0:T(8,128)(2,1)}), bf16[16,32,1152]{2,1,0:T(8,128)(2,1)S(1)}, u32[]{:S(2)}, u32[]{:S(2)}) async-start(bf16[16,32,1152]{2,1,0:T(8,128)(2,1)} %pick_blocks.7), calls=%async_computation.3 | async-start | bytes 2359296 | tf_op jit(solution)/shard_map/all_to_all | solution.py:341
  172.2 5.8 %copy-start.2 = (f32[1152]{0:T(1024)S(1)}, f32[1152]{0:T(1024)}, u32[]{:S(2)}) copy-start(f32[1152]{0:T(1024)} %gain_ref.3) | copy-start | bytes 13828
  172.2 21.9 %all-to-all-start.4 = ((bf16[16,72,432]{2,1,0:T(8,128)(2,1)}), bf16[16,72,432]{2,1,0:T(8,128)(2,1)}, u32[]{:S(2)}, u32[]{:S(2)}) async-start(bf16[16,72,432]{2,1,0:T(8,128)(2,1)} %bitcast.26), calls=%async_computation.5 | async-start | bytes 2359296 | tf_op jit(solution)/shard_map/all_to_all | solution.py:391
  179.3 2.5 %copy-start.1 = (bf16[1,512,1152]{2,1,0:T(8,128)(2,1)S(1)}, bf16[1,512,1152]{2,1,0:T(8,128)(2,1)}, u32[]{:S(2)}) copy-start(bf16[1,512,1152]{2,1,0:T(8,128)(2,1)} %param.6) | copy-start | bytes 3538948
  179.3 2.5 %copy-start.7 = (s32[4]{0:T(128)S(1)}, s32[4]{0:T(128)}, u32[]{:S(2)}) copy-start(s32[4]{0:T(128)} %get-tuple-element.19.index_ref) | copy-start | bytes 52
Sparse Core Ops, SparseCore 0:
  114.7 54.0 reduce-scatter.1

commit v7 on v6

--- a/solution.py
+++ b/solution.py
@@ -139,9 +139,9 @@
             pl.BlockSpec((3 * PAIR, scaled.shape[1]), lambda i: (i, 0)),
         ],
         out_shape=[
-            jax.ShapeDtypeStruct((pairs * PAIR, rows), BF16),
-            jax.ShapeDtypeStruct((pairs * 3 * PAIR, rows), BF16),
-            jax.ShapeDtypeStruct((pairs * 3 * PAIR, scaled.shape[1]), BF16),
+            pltpu.HBM((pairs * PAIR, rows), BF16),
+            pltpu.HBM((pairs * 3 * PAIR, rows), BF16),
+            pltpu.HBM((pairs * 3 * PAIR, scaled.shape[1]), BF16),
         ],
         scratch_shapes=[
             pltpu.VMEM((blocks + 2, BLK, 3 * BLK), F32),
@@ -153,6 +153,7 @@
             bytes_accessed=pairs * PAIR * (rows * 8 + rim * 4) * 2,
             transcendentals=pairs * 2 * 16 * BLK * BLK,
         ),
+        compiler_params=pltpu.CompilerParams(vmem_limit_bytes=24 * 2**20),
         name="packed_attention",
     )(ids[:, None], ids[None, :], own, own, own, halo, halo, halo, g_own, g_halo, scaled)
 

time: 223 us -> 219 us (0.982)
  matrix products: 23.9 us -> 21.5 us
    dot_general x2, matrix products: 16.2 us -> 13.8 us  [project(): lax.dot_general(qkv_weight, rows, (((0,), (1,)), ((), ())), preferred_ele...]
    unnamed x30 -> x28, local copies, waits for them, and re-layouts: 5.13 us -> 5.83 us
where the time goes in v7:
time: 219 us; the launch traced here: 218 us
  waiting for transfers between devices  52.8 us (24%)
  blocking collectives  42.8 us (20%)
  Pallas kernels  37.9 us (17%)
  starting transfers between devices  34.1 us (16%)
  matrix products  21.5 us (10%)
  between operations  14.4 us (7%)
  local copies, waits for them, and re-layouts  10.7 us (5%)
  other arithmetic  3.95 us (2%)
    all_to_all x1, blocking collectives, exchange(): return lax.all_to_all(x, SEQ, split_axis=0, concat_axis=0, tiled=True)  25.7 us
    pallas_call x1, Pallas kernels, attention_call(): pl.pallas_call(attention_kernel, grid=(pairs,), in_specs=[pl.BlockSpec((t...  22.8 us
    all_to_all x3, waiting for transfers between devices, exchange(): return lax.all_to_all(x, SEQ, split_axis=0, concat_axis=0, tiled=True)  17.7 us
    all_to_all x3, starting transfers between devices, exchange(): return lax.all_to_all(x, SEQ, split_axis=0, concat_axis=0, tiled=True)  17.3 us
    all_gather x1, blocking collectives, local(): weight_cols = lax.all_gather(summed, DP, axis=0)  17 us
    dot_general x2, matrix products, project(): lax.dot_general(qkv_weight, rows, (((0,), (1,)), ((), ())), preferred_ele...  13.8 us
    reduce_scatter x1, waiting for transfers between devices, local(): lax.psum_scatter(weight_local, DP, scatter_dimension=0, tiled=True)  12.7 us
    ppermute x2, waiting for transfers between devices, halo(): before = lax.ppermute(x[row_count - BLK:], SEQ, up)  11.7 us
  transfers between devices with their start and end apart: 9, of which 6 were waited for; matrix products, arithmetic and copies ran while one was open for 13% of the time, Pallas kernels for 2%

profile of v7, /device:TPU:1, one launch (start us, length us, event | category | flops | bytes accessed | tf_op | source)
XLA Modules:
  0.0 218.1 jit_solution(18077353056147617766)
XLA Ops:
  7.2 5.9 %route_blocks.1 = (bf16[4,128,1152]{2,1,0:T(8,128)(2,1)}, s32[4]{0:T(128)}, s32[16]{0:T(128)}, s32[4]{0:T(128)}, s32[4]{0:T(128)}, /*index=5*/s32[16]{0:T(128)}, s32[4]{0:T(128)}) custom-call(s32[1]{0:T(128)} %bitcast.1.me_ref, s32[64]{0:T(128)} %bitcast.63, bf16[4,128,1152]{2,1,0:T(8,128)(2,1)} %bitcast.50, f32[1152]{0:T(1024)} %gain_ref.3), custom_call_target="tpu_custom_call" | custom-call | tf_op jit(solution)/shard_map/route_blocks/pallas_call | solution.py:239
  13.1 8.6 %all-to-all-start = ((bf16[16,32,1152]{2,1,0:T(8,128)(2,1)}), bf16[16,32,1152]{2,1,0:T(8,128)(2,1)S(1)}, u32[]{:S(2)}, u32[]{:S(2)}) async-start(bf16[16,32,1152]{2,1,0:T(8,128)(2,1)} %bitcast.58), calls=%async_computation | async-start | bytes 2359296 | tf_op jit(solution)/shard_map/all_to_all | solution.py:342
  21.7 0.6 copy.33
  22.3 16.8 %all-to-all-done.source_ref = bf16[16,32,1152]{2,1,0:T(8,128)(2,1)S(1)} async-done(((bf16[16,32,1152]{2,1,0:T(8,128)(2,1)}), bf16[16,32,1152]{2,1,0:T(8,128)(2,1)S(1)}, u32[]{:S(2)}, u32[]{:S(2)}) %all-to-all-start) | async-done | bytes 1179680 | tf_op jit(solution)/shard_map/all_to_all | solution.py:342
  39.1 1.6 pick_blocks.4
  40.7 5.0 %all-to-all-start.1 = ((bf16[16,32,1152]{2,1,0:T(8,128)(2,1)}), bf16[16,32,1152]{2,1,0:T(8,128)(2,1)S(1)}, u32[]{:S(2)}, u32[]{:S(2)}) async-start(bf16[16,32,1152]{2,1,0:T(8,128)(2,1)} %pick_blocks.4), calls=%async_computation.1 | async-start | bytes 2359296 | tf_op jit(solution)/shard_map/all_to_all | solution.py:342
  45.7 0.0 reduce-scatter.2.cloned.1.call-start
  45.8 0.8 slice_bitcast_fusion.1
  46.6 3.4 %collective-permute-start.2 = (bf16[128,1152]{0,1:T(8,128)(2,1)}, bf16[128,1152]{0,1:T(8,128)(2,1)S(1)}, u32[]{:S(2)}, u32[]{:S(2)}) collective-permute-start(bf16[128,1152]{0,1:T(8,128)(2,1)} %get-tuple-element.38), channel_id=1, source_target_pairs={{0,1},{1,2},{2,3},{3,4},{4,5},{5,6},{6,7},{7,8},{8,9},{9,10},{10,1... | collective-permute-start | bytes 884744 | tf_op jit(solution)/shard_map/ppermute | solution.py:348
  50.0 1.3 collective-permute-start.3
  51.3 0.1 copy.29
  51.4 0.2 reduce-window.8
  51.6 0.1 reduce.1
  51.7 0.3 convert_reduce_fusion
  52.0 0.2 reshape_select_fusion.col_ref
  52.2 11.7 %collective-permute-done.2 = bf16[128,1152]{0,1:T(8,128)(2,1)S(1)} collective-permute-done((bf16[128,1152]{0,1:T(8,128)(2,1)}, bf16[128,1152]{0,1:T(8,128)(2,1)S(1)}, u32[]{:S(2)}, u32[]{:S(2)}) %collective-permute-start.2) | collective-permute-done | bytes 294944 | tf_op jit(solution)/shard_map/ppermute | solution.py:348
  63.8 0.7 copy-done.9
  64.5 1.4 collective-permute-done.3
  65.9 1.1 maximum_bitcast_fusion.gh_ref
  67.0 0.6 pick_blocks.5
  67.7 4.8 %collective-permute-start = (bf16[128,1152]{1,0:T(8,128)(2,1)S(1)}, bf16[128,1152]{1,0:T(8,128)(2,1)S(1)}, u32[]{:S(2)}, u32[]{:S(2)}) collective-permute-start(bf16[128,1152]{1,0:T(8,128)(2,1)S(1)} %get-tuple-element.40), channel_id=1, source_target_pairs={{0,1},{1,2},{2,3},{3,4},{4,5},{5,6},{6,7},{7,8},{8,9},{9,10},{10,1... | collective-permute-start | bytes 884744 | tf_op jit(solution)/shard_map/ppermute | solution.py:348
  72.5 1.5 collective-permute-start.1
  74.0 0.0 slice-start.1
  74.0 10.2 %fusion.q_ref.k_ref.v_ref = bf16[3456,512]{1,0:T(8,128)(2,1)S(1)} fusion(bf16[512,1152]{1,0:T(8,128)(2,1)S(1)} %bitcast.46, bf16[1152,3456]{1,0:T(8,128)(2,1)} %param.10), kind=kOutput, calls=%fused_computation.1 | convolution fusion | flops 4078632960 | bytes 12681216 | tf_op jit(solution)/shard_map/dot_general | solution.py:361
  84.3 3.5 %fusion.1.qh_ref.kh_ref.vh_ref = bf16[3456,256]{1,0:T(8,128)(2,1)S(1)} fusion(bf16[1152,3456]{1,0:T(8,128)(2,1)S(1)} %bitcast.62, bf16[128,1152]{1,0:T(8,128)(2,1)S(1)} %collective-permute-done.1, bf16[128,1152]{1,0:T(8,128)(2,1)S(1)} %collective-permute-done), kind=kOutput, calls=%fused_computation.3 | convolution fusion | flops 2040496128 | bytes 10321920 | tf_op jit(solution)/shard_map/dot_general | solution.py:361
  87.8 22.8 %packed_attention.1 = (bf16[1152,512]{1,0:T(8,128)(2,1)}, bf16[3456,512]{1,0:T(8,128)(2,1)}, bf16[3456,1152]{1,0:T(8,128)(2,1)}) custom-call(s32[768,1]{1,0:T(8,128)S(1)} %reshape_select_fusion.col_ref, s32[1,768]{1,0:T(1,128)S(1)} %and_select_fusion.row_ref, bf16[3456,512]{1,0:T(8,128)(2,1)S(1)} %fusion.q_ref.k_ref.v_ref, ...), custom_call_target="tpu_custom_call" | custom-call | flops 3623878656 | bytes 11796480 | tf_op jit(solution)/shard_map/packed_attention/pallas_call | solution.py:125
  110.7 0.0 reduce-scatter.2.cloned.1.call-update
  110.7 2.0 copy-done.7
  112.7 0.3 copy.36
  113.0 7.7 %convolution_convert_fusion.2 = bf16[512,1152]{1,0:T(8,128)(2,1)S(1)} fusion(bf16[3456,512]{1,0:T(8,128)(2,1)S(1)} %bitcast.56, bf16[1152,3456]{1,0:T(8,128)(2,1)} %param.10), kind=kOutput, calls=%fused_computation.4 | convolution fusion | flops 4077453312 | bytes 12681216 | tf_op jit(solution)/shard_map/dot_general | solution.py:380
  120.7 0.6 pick_blocks.6
  121.4 25.7 %all_to_all.25.source_ref = bf16[16,32,1152]{2,1,0:T(8,128)(2,1)S(1)} all-to-all(bf16[16,32,1152]{2,1,0:T(8,128)(2,1)S(1)} %bitcast.49), channel_id=1, replica_groups=mesh['y'=4,'core'=2,'z'=4,'x'=4] {'z','x'}, dimensions={0} | all-to-all | bytes 2359296 | tf_op jit(solution)/shard_map/all_to_all | solution.py:342
  147.1 1.6 pick_blocks.7
  148.7 3.7 %all-to-all-start.3 = ((bf16[16,32,1152]{2,1,0:T(8,128)(2,1)}), bf16[16,32,1152]{2,1,0:T(8,128)(2,1)S(1)}, u32[]{:S(2)}, u32[]{:S(2)}) async-start(bf16[16,32,1152]{2,1,0:T(8,128)(2,1)} %pick_blocks.7), calls=%async_computation.3 | async-start | bytes 2359296 | tf_op jit(solution)/shard_map/all_to_all | solution.py:342
  152.4 12.7 %reduce-scatter.2.cloned.1.call-done = bf16[432,1152]{1,0:T(8,128)(2,1)} async-done(((bf16[3456,1152]{1,0:T(8,128)(2,1)}), bf16[432,1152]{1,0:T(8,128)(2,1)}) %reduce-scatter.2.cloned.1.call-update) | async-done | bytes 995344 | tf_op jit(solution)/shard_map/reduce_scatter | solution.py:376
  165.2 2.4 %copy.37 = bf16[1152,432]{1,0:T(8,128)(2,1)} copy(bf16[1152,432]{0,1:T(8,128)(2,1)} %bitcast.60) | data formatting | bytes 1990656 | tf_op jit(solution)/shard_map/transpose | solution.py:391
  167.6 1.0 all-to-all-done.3
  168.5 5.9 %all-to-all-start.4 = ((bf16[16,72,432]{2,1,0:T(8,128)(2,1)}), bf16[16,72,432]{2,1,0:T(8,128)(2,1)}, u32[]{:S(2)}, u32[]{:S(2)}) async-start(bf16[16,72,432]{2,1,0:T(8,128)(2,1)} %bitcast.26), calls=%async_computation.5 | async-start | bytes 2359296 | tf_op jit(solution)/shard_map/all_to_all | solution.py:392
  174.4 0.1 dynamic-slice_bitcast_fusion
  174.5 0.1 copy.38.gain_ref
  174.6 1.1 constant_dynamic-slice_fusion.weight_ref
  175.7 2.5 %copy.39 = bf16[1,512,1152]{2,1,0:T(8,128)(2,1)} copy(bf16[1,512,1152]{1,2,0:T(8,128)(2,1)} %bitcast.57) | data formatting | bytes 2359296
  178.2 3.0 %norm_back.1 = bf16[4,128,1152]{2,1,0:T(8,128)(2,1)} custom-call(s32[4]{0:T(128)S(1)} %copy-done.6, bf16[4,128,1152]{2,1,0:T(8,128)(2,1)S(1)} %bitcast.52, bf16[4,128,1152]{2,1,0:T(8,128)(2,1)S(1)} %bitcast.51, f32[1152]{0:T(1024)S(1)} %copy-done.1), custom_call_target="tpu_custom_call" | custom-call | flops 4718592 | bytes 4718592 | tf_op jit(solution)/shard_map/norm_back/pallas_call | solution.py:269
  181.2 9.3 %all-to-all-done.4 = bf16[16,72,432]{2,1,0:T(8,128)(2,1)} async-done(((bf16[16,72,432]{2,1,0:T(8,128)(2,1)}), bf16[16,72,432]{2,1,0:T(8,128)(2,1)}, u32[]{:S(2)}, u32[]{:S(2)}) %all-to-all-start.4) | async-done | bytes 995360 | tf_op jit(solution)/shard_map/all_to_all | solution.py:392
  190.5 1.5 reduce_sum.28
  192.0 17.0 %all-gather = bf16[576,432]{1,0:T(8,128)(2,1)S(1)} all-gather(bf16[72,432]{1,0:T(8,128)(2,1)S(1)} %reduce_sum.28), channel_id=2, replica_groups=mesh['y'=4,'core'=2,'z'=4,'x'=4] {'y','core'}, dimensions={0}, use_global_device_ids=true | all-gather | bytes 559872 | tf_op jit(solution)/shard_map/all_gather | solution.py:394
  209.0 1.6 assemble.1
  210.6 0.6 reduce.2
  (30 shorter events, 0.1 us)
Async XLA Ops:
  13.1 8.6 %copy-start.8 = (bf16[1,512,1152]{2,1,0:T(8,128)(2,1)S(1)}, bf16[1,512,1152]{2,1,0:T(8,128)(2,1)}, u32[]{:S(2)}) copy-start(bf16[1,512,1152]{2,1,0:T(8,128)(2,1)} %param.11) | copy-start | bytes 3538948
  13.1 26.0 %all-to-all-start = ((bf16[16,32,1152]{2,1,0:T(8,128)(2,1)}), bf16[16,32,1152]{2,1,0:T(8,128)(2,1)S(1)}, u32[]{:S(2)}, u32[]{:S(2)}) async-start(bf16[16,32,1152]{2,1,0:T(8,128)(2,1)} %bitcast.58), calls=%async_computation | async-start | bytes 2359296 | tf_op jit(solution)/shard_map/all_to_all | solution.py:342
  21.7 17.4 %copy-start.5 = (s32[16]{0:T(128)S(1)}, s32[16]{0:T(128)}, u32[]{:S(2)}) copy-start(s32[16]{0:T(128)} %get-tuple-element.16.index_ref) | copy-start | bytes 196
  40.7 26.3 %all-to-all-start.1 = ((bf16[16,32,1152]{2,1,0:T(8,128)(2,1)}), bf16[16,32,1152]{2,1,0:T(8,128)(2,1)S(1)}, u32[]{:S(2)}, u32[]{:S(2)}) async-start(bf16[16,32,1152]{2,1,0:T(8,128)(2,1)} %pick_blocks.4), calls=%async_computation.1 | async-start | bytes 2359296 | tf_op jit(solution)/shard_map/all_to_all | solution.py:342
  45.7 5.5 %copy-start.10 = (s32[1,128]{1,0:T(1,128)S(1)}, s32[1,128]{1,0:T(1,128)}, u32[]{:S(2)}) copy-start(s32[1,128]{1,0:T(1,128)} %param.7) | copy-start | bytes 1540
  45.7 119.4 %reduce-scatter.2.cloned.1.call-start = ((), (), s32[]{:S(2)}) async-start(), calls=%async_computation.6 | async-start | bytes 8957952 | tf_op jit(solution)/shard_map/reduce_scatter | solution.py:376
  46.6 20.5 %copy-start.4 = (s32[4]{0:T(128)S(1)}, s32[4]{0:T(128)}, u32[]{:S(2)}) copy-start(s32[4]{0:T(128)} %get-tuple-element.15.index_ref) | copy-start | bytes 52
  46.6 17.3 %collective-permute-start.2 = (bf16[128,1152]{0,1:T(8,128)(2,1)}, bf16[128,1152]{0,1:T(8,128)(2,1)S(1)}, u32[]{:S(2)}, u32[]{:S(2)}) collective-permute-start(bf16[128,1152]{0,1:T(8,128)(2,1)} %get-tuple-element.38), channel_id=1, source_target_pairs={{0,1},{1,2},{2,3},{3,4},{4,5},{5,6},{6,7},{7,8},{8,9},{9,10},{10,1... | collective-permute-start | bytes 884744 | tf_op jit(solution)/shard_map/ppermute | solution.py:348
  50.0 15.9 %collective-permute-start.3 = (bf16[128,1152]{0,1:T(8,128)(2,1)S(1)}, bf16[128,1152]{0,1:T(8,128)(2,1)}, u32[]{:S(2)}, u32[]{:S(2)}) collective-permute-start(bf16[128,1152]{0,1:T(8,128)(2,1)S(1)} %get-tuple-element.39), channel_id=1, source_target_pairs={{1,0},{2,1},{3,2},{4,3},{5,4},{6,5},{7,6},{8,7},{9,8},{10,9},{11,1... | collective-permute-start | bytes 884744 | tf_op jit(solution)/shard_map/ppermute | solution.py:349
  63.8 0.7 copy-start.9
  67.7 16.6 %slice-start = ((s8[7962624]{0:T(1024)(128)(4,1)}), s8[4194304]{0:T(1024)(128)(4,1)S(1)}, s32[]{:S(2)}) async-start(s8[7962624]{0:T(1024)(128)(4,1)} %bitcast.61), calls=%async_computation.7 | async-start | bytes 8388608
  67.7 16.5 %collective-permute-start = (bf16[128,1152]{1,0:T(8,128)(2,1)S(1)}, bf16[128,1152]{1,0:T(8,128)(2,1)S(1)}, u32[]{:S(2)}, u32[]{:S(2)}) collective-permute-start(bf16[128,1152]{1,0:T(8,128)(2,1)S(1)} %get-tuple-element.40), channel_id=1, source_target_pairs={{0,1},{1,2},{2,3},{3,4},{4,5},{5,6},{6,7},{7,8},{8,9},{9,10},{10,1... | collective-permute-start | bytes 884744 | tf_op jit(solution)/shard_map/ppermute | solution.py:348
  72.5 11.7 %collective-permute-start.1 = (bf16[128,1152]{1,0:T(8,128)(2,1)S(1)}, bf16[128,1152]{1,0:T(8,128)(2,1)S(1)}, u32[]{:S(2)}, u32[]{:S(2)}) collective-permute-start(bf16[128,1152]{1,0:T(8,128)(2,1)S(1)} %get-tuple-element.41), channel_id=1, source_target_pairs={{1,0},{2,1},{3,2},{4,3},{5,4},{6,5},{7,6},{8,7},{9,8},{10,9},{11,1... | collective-permute-start | bytes 884744 | tf_op jit(solution)/shard_map/ppermute | solution.py:349
  74.0 10.3 %slice-start.1 = ((s8[7962624]{0:T(1024)(128)(4,1)}), s8[3768320]{0:T(1024)(128)(4,1)S(1)}, s32[]{:S(2)}) async-start(s8[7962624]{0:T(1024)(128)(4,1)} %bitcast.61), calls=%async_computation.8 | async-start | bytes 7536640
  110.7 2.0 copy-start.7
  113.0 7.7 %copy-start.3 = (s32[4]{0:T(128)S(1)}, s32[4]{0:T(128)}, u32[]{:S(2)}) copy-start(s32[4]{0:T(128)} %get-tuple-element.21.index_ref) | copy-start | bytes 52
  121.4 25.7 %copy-start.2 = (s32[16]{0:T(128)S(1)}, s32[16]{0:T(128)}, u32[]{:S(2)}) copy-start(s32[16]{0:T(128)} %get-tuple-element.20.index_ref) | copy-start | bytes 196
  148.7 19.8 %all-to-all-start.3 = ((bf16[16,32,1152]{2,1,0:T(8,128)(2,1)}), bf16[16,32,1152]{2,1,0:T(8,128)(2,1)S(1)}, u32[]{:S(2)}, u32[]{:S(2)}) async-start(bf16[16,32,1152]{2,1,0:T(8,128)(2,1)} %pick_blocks.7), calls=%async_computation.3 | async-start | bytes 2359296 | tf_op jit(solution)/shard_map/all_to_all | solution.py:342
  168.5 5.9 %copy-start.1 = (f32[1152]{0:T(1024)S(1)}, f32[1152]{0:T(1024)}, u32[]{:S(2)}) copy-start(f32[1152]{0:T(1024)} %gain_ref.3) | copy-start | bytes 13828
  168.5 22.0 %all-to-all-start.4 = ((bf16[16,72,432]{2,1,0:T(8,128)(2,1)}), bf16[16,72,432]{2,1,0:T(8,128)(2,1)}, u32[]{:S(2)}, u32[]{:S(2)}) async-start(bf16[16,72,432]{2,1,0:T(8,128)(2,1)} %bitcast.26), calls=%async_computation.5 | async-start | bytes 2359296 | tf_op jit(solution)/shard_map/all_to_all | solution.py:392
  175.7 2.5 %copy-start = (bf16[1,512,1152]{2,1,0:T(8,128)(2,1)S(1)}, bf16[1,512,1152]{2,1,0:T(8,128)(2,1)}, u32[]{:S(2)}) copy-start(bf16[1,512,1152]{2,1,0:T(8,128)(2,1)} %param.6) | copy-start | bytes 3538948
  175.7 2.5 %copy-start.6 = (s32[4]{0:T(128)S(1)}, s32[4]{0:T(128)}, u32[]{:S(2)}) copy-start(s32[4]{0:T(128)} %get-tuple-element.19.index_ref) | copy-start | bytes 52
Sparse Core Ops, SparseCore 0:
  110.8 54.3 reduce-scatter.1

commit v8 on v7

--- a/solution.py
+++ b/solution.py
@@ -18,7 +18,7 @@
 SCORE_SCALE = HD ** (-0.5)
 EXP2_SCALE = SCORE_SCALE * 1.4426950408889634
 HIDDEN_BIAS = -1e30
-LAG = 2
+LAG = 3
 DP = ("y", "core")
 SEQ = ("z", "x")
 
@@ -107,7 +107,10 @@
             if factor is not None:
                 d_s[at, :] = d_s[at, :] * factor
     grads = d_s[...].astype(BF16)
-    d_ref[...] = grads
+    for part in range(3):
+        first, second = part * HD, (3 + part) * HD
+        both = [d_s[first : first + HD, :], d_s[second : second + HD, :]]
+        d_ref[part] = jnp.concatenate(both, axis=0).astype(BF16)
     third = rows_ref.shape[1] // 3
     for part in range(3):
         cols = slice(part * third, (part + 1) * third)
@@ -135,12 +138,12 @@
         ],
         out_specs=[
             pl.BlockSpec((PAIR, rows), lambda i: (i, 0)),
-            pl.BlockSpec((3 * PAIR, rows), lambda i: (i, 0)),
+            pl.BlockSpec((3, PAIR, rows), lambda i: (0, i, 0)),
             pl.BlockSpec((3 * PAIR, scaled.shape[1]), lambda i: (i, 0)),
         ],
         out_shape=[
             pltpu.HBM((pairs * PAIR, rows), BF16),
-            pltpu.HBM((pairs * 3 * PAIR, rows), BF16),
+            pltpu.HBM((3, pairs * PAIR, rows), BF16),
             pltpu.HBM((pairs * 3 * PAIR, scaled.shape[1]), BF16),
         ],
         scratch_shapes=[
@@ -375,8 +378,7 @@
     )
     weight_part = lax.psum_scatter(weight_local, DP, scatter_dimension=0, tiled=True)
     attention = attended.T[None]
-    grad_cols = grads.reshape(HEADS, 3, HD, row_count)
-    grad_cols = grad_cols.transpose(1, 0, 2, 3).reshape(3 * model_width, row_count)
+    grad_cols = grads.reshape(3 * model_width, row_count)
     input_grad = lax.dot_general(
         grad_cols, qkv_weight, (((0,), (1,)), ((), ())), preferred_element_type=F32
     ).astype(BF16)

time: 219 us -> 219 us (level)
  transfers between devices with their start and end apart: 9 -> 9, of which waited for: 6 -> 6; matrix products, arithmetic and copies ran while one was open for 13% -> 12% of each run, Pallas kernels for 2% -> 2%
where the time goes in v8:
time: 219 us; the launch traced here: 218 us
  waiting for transfers between devices  53.2 us (24%)
  blocking collectives  42.5 us (19%)
  Pallas kernels  38.1 us (17%)
  starting transfers between devices  34.5 us (16%)
  matrix products  21.2 us (10%)
  between operations  14.4 us (7%)
  local copies, waits for them, and re-layouts  10.4 us (5%)
  other arithmetic  3.95 us (2%)
    all_to_all x1, blocking collectives, exchange(): return lax.all_to_all(x, SEQ, split_axis=0, concat_axis=0, tiled=True)  25.9 us
    pallas_call x1, Pallas kernels, attention_call(): pl.pallas_call(attention_kernel, grid=(pairs,), in_specs=[pl.BlockSpec((t...  22.9 us
    all_to_all x3, waiting for transfers between devices, exchange(): return lax.all_to_all(x, SEQ, split_axis=0, concat_axis=0, tiled=True)  17.5 us
    all_to_all x3, starting transfers between devices, exchange(): return lax.all_to_all(x, SEQ, split_axis=0, concat_axis=0, tiled=True)  17.3 us
    all_gather x1, blocking collectives, local(): weight_cols = lax.all_gather(summed, DP, axis=0)  16.6 us
    dot_general x2, matrix products, project(): lax.dot_general(qkv_weight, rows, (((0,), (1,)), ((), ())), preferred_ele...  13.8 us
    reduce_scatter x1, waiting for transfers between devices, local(): lax.psum_scatter(weight_local, DP, scatter_dimension=0, tiled=True)  13 us
    ppermute x2, waiting for transfers between devices, halo(): before = lax.ppermute(x[row_count - BLK:], SEQ, up)  11.7 us
  transfers between devices with their start and end apart: 9, of which 6 were waited for; matrix products, arithmetic and copies ran while one was open for 12% of the time, Pallas kernels for 2%

profile of v8, /device:TPU:1, one launch (start us, length us, event | category | flops | bytes accessed | tf_op | source)
XLA Modules:
  0.0 218.3 jit_solution(17853778210481026058)
XLA Ops:
  7.2 5.9 %route_blocks.1 = (bf16[4,128,1152]{2,1,0:T(8,128)(2,1)}, s32[4]{0:T(128)}, s32[16]{0:T(128)}, s32[4]{0:T(128)}, s32[4]{0:T(128)}, /*index=5*/s32[16]{0:T(128)}, s32[4]{0:T(128)}) custom-call(s32[1]{0:T(128)} %bitcast.1.me_ref, s32[64]{0:T(128)} %bitcast.58, bf16[4,128,1152]{2,1,0:T(8,128)(2,1)} %bitcast.47, f32[1152]{0:T(1024)} %gain_ref.3), custom_call_target="tpu_custom_call" | custom-call | tf_op jit(solution)/shard_map/route_blocks/pallas_call | solution.py:242
  13.1 8.6 %all-to-all-start = ((bf16[16,32,1152]{2,1,0:T(8,128)(2,1)}), bf16[16,32,1152]{2,1,0:T(8,128)(2,1)S(1)}, u32[]{:S(2)}, u32[]{:S(2)}) async-start(bf16[16,32,1152]{2,1,0:T(8,128)(2,1)} %bitcast.53), calls=%async_computation | async-start | bytes 2359296 | tf_op jit(solution)/shard_map/all_to_all | solution.py:345
  21.7 0.6 copy.32
  22.3 16.8 %all-to-all-done.source_ref = bf16[16,32,1152]{2,1,0:T(8,128)(2,1)S(1)} async-done(((bf16[16,32,1152]{2,1,0:T(8,128)(2,1)}), bf16[16,32,1152]{2,1,0:T(8,128)(2,1)S(1)}, u32[]{:S(2)}, u32[]{:S(2)}) %all-to-all-start) | async-done | bytes 1179680 | tf_op jit(solution)/shard_map/all_to_all | solution.py:345
  39.2 1.6 pick_blocks.4
  40.8 5.0 %all-to-all-start.1 = ((bf16[16,32,1152]{2,1,0:T(8,128)(2,1)}), bf16[16,32,1152]{2,1,0:T(8,128)(2,1)S(1)}, u32[]{:S(2)}, u32[]{:S(2)}) async-start(bf16[16,32,1152]{2,1,0:T(8,128)(2,1)} %pick_blocks.4), calls=%async_computation.1 | async-start | bytes 2359296 | tf_op jit(solution)/shard_map/all_to_all | solution.py:345
  45.8 0.0 reduce-scatter.2.cloned.1.call-start
  45.9 0.8 slice_bitcast_fusion.1
  46.6 3.4 %collective-permute-start.2 = (bf16[128,1152]{0,1:T(8,128)(2,1)}, bf16[128,1152]{0,1:T(8,128)(2,1)S(1)}, u32[]{:S(2)}, u32[]{:S(2)}) collective-permute-start(bf16[128,1152]{0,1:T(8,128)(2,1)} %get-tuple-element.38), channel_id=1, source_target_pairs={{0,1},{1,2},{2,3},{3,4},{4,5},{5,6},{6,7},{7,8},{8,9},{9,10},{10,1... | collective-permute-start | bytes 884744 | tf_op jit(solution)/shard_map/ppermute | solution.py:351
  50.0 1.3 collective-permute-start.3
  51.3 0.1 copy.28
  51.5 0.2 reduce-window.8
  51.6 0.1 reduce.1
  51.8 0.3 convert_reduce_fusion
  52.1 0.2 reshape_select_fusion.col_ref
  52.2 11.7 %collective-permute-done.2 = bf16[128,1152]{0,1:T(8,128)(2,1)S(1)} collective-permute-done((bf16[128,1152]{0,1:T(8,128)(2,1)}, bf16[128,1152]{0,1:T(8,128)(2,1)S(1)}, u32[]{:S(2)}, u32[]{:S(2)}) %collective-permute-start.2) | collective-permute-done | bytes 294944 | tf_op jit(solution)/shard_map/ppermute | solution.py:351
  64.0 0.7 copy-done.8
  64.7 1.4 collective-permute-done.3
  66.0 1.1 maximum_bitcast_fusion.gh_ref
  67.2 0.6 pick_blocks.5
  67.8 0.0 slice-start
  67.9 4.8 %collective-permute-start = (bf16[128,1152]{1,0:T(8,128)(2,1)S(1)}, bf16[128,1152]{1,0:T(8,128)(2,1)S(1)}, u32[]{:S(2)}, u32[]{:S(2)}) collective-permute-start(bf16[128,1152]{1,0:T(8,128)(2,1)S(1)} %get-tuple-element.40), channel_id=1, source_target_pairs={{0,1},{1,2},{2,3},{3,4},{4,5},{5,6},{6,7},{7,8},{8,9},{9,10},{10,1... | collective-permute-start | bytes 884744 | tf_op jit(solution)/shard_map/ppermute | solution.py:351
  72.6 1.5 collective-permute-start.1
  74.1 0.0 slice-start.1
  74.1 10.2 %fusion.q_ref.k_ref.v_ref = bf16[3456,512]{1,0:T(8,128)(2,1)S(1)} fusion(bf16[512,1152]{1,0:T(8,128)(2,1)S(1)} %bitcast.43, bf16[1152,3456]{1,0:T(8,128)(2,1)} %param.10), kind=kOutput, calls=%fused_computation.1 | convolution fusion | flops 4078632960 | bytes 12681216 | tf_op jit(solution)/shard_map/dot_general | solution.py:364
  84.4 3.5 %fusion.1.qh_ref.kh_ref.vh_ref = bf16[3456,256]{1,0:T(8,128)(2,1)S(1)} fusion(bf16[1152,3456]{1,0:T(8,128)(2,1)S(1)} %bitcast.57, bf16[128,1152]{1,0:T(8,128)(2,1)S(1)} %collective-permute-done.1, bf16[128,1152]{1,0:T(8,128)(2,1)S(1)} %collective-permute-done), kind=kOutput, calls=%fused_computation.3 | convolution fusion | flops 2040496128 | bytes 10321920 | tf_op jit(solution)/shard_map/dot_general | solution.py:364
  88.0 22.9 %packed_attention.1 = (bf16[1152,512]{1,0:T(8,128)(2,1)}, bf16[3,1152,512]{2,1,0:T(8,128)(2,1)}, bf16[3456,1152]{1,0:T(8,128)(2,1)}) custom-call(s32[768,1]{1,0:T(8,128)S(1)} %reshape_select_fusion.col_ref, s32[1,768]{1,0:T(1,128)S(1)} %and_select_fusion.row_ref, bf16[3456,512]{1,0:T(8,128)(2,1)S(1)} %fusion.q_ref.k_ref.v_ref, ...), custom_call_target="tpu_custom_call" | custom-call | flops 3623878656 | bytes 11796480 | tf_op jit(solution)/shard_map/packed_attention/pallas_call | solution.py:128
  110.9 0.0 reduce-scatter.2.cloned.1.call-update
  110.9 2.0 copy-done.10
  112.9 7.5 %convolution_convert_fusion.2 = bf16[512,1152]{1,0:T(8,128)(2,1)S(1)} fusion(bf16[3456,512]{1,0:T(8,128)(2,1)S(1)} %bitcast.60, bf16[1152,3456]{1,0:T(8,128)(2,1)} %param.10), kind=kOutput, calls=%fused_computation.4 | convolution fusion | flops 4077453312 | bytes 12681216 | tf_op jit(solution)/shard_map/dot_general | solution.py:382
  120.4 0.6 pick_blocks.6
  121.1 25.9 %all_to_all.25.source_ref = bf16[16,32,1152]{2,1,0:T(8,128)(2,1)S(1)} all-to-all(bf16[16,32,1152]{2,1,0:T(8,128)(2,1)S(1)} %bitcast.46), channel_id=1, replica_groups=mesh['y'=4,'core'=2,'z'=4,'x'=4] {'z','x'}, dimensions={0} | all-to-all | bytes 2359296 | tf_op jit(solution)/shard_map/all_to_all | solution.py:345
  147.0 1.6 pick_blocks.7
  148.6 3.7 %all-to-all-start.3 = ((bf16[16,32,1152]{2,1,0:T(8,128)(2,1)}), bf16[16,32,1152]{2,1,0:T(8,128)(2,1)S(1)}, u32[]{:S(2)}, u32[]{:S(2)}) async-start(bf16[16,32,1152]{2,1,0:T(8,128)(2,1)} %pick_blocks.7), calls=%async_computation.3 | async-start | bytes 2359296 | tf_op jit(solution)/shard_map/all_to_all | solution.py:345
  152.3 13.0 %reduce-scatter.2.cloned.1.call-done = bf16[432,1152]{1,0:T(8,128)(2,1)} async-done(((bf16[3456,1152]{1,0:T(8,128)(2,1)}), bf16[432,1152]{1,0:T(8,128)(2,1)}) %reduce-scatter.2.cloned.1.call-update) | async-done | bytes 995344 | tf_op jit(solution)/shard_map/reduce_scatter | solution.py:379
  165.3 2.4 %copy.35 = bf16[1152,432]{1,0:T(8,128)(2,1)} copy(bf16[1152,432]{0,1:T(8,128)(2,1)} %bitcast.55) | data formatting | bytes 1990656 | tf_op jit(solution)/shard_map/transpose | solution.py:393
  167.7 0.6 all-to-all-done.3
  168.4 6.2 %all-to-all-start.4 = ((bf16[16,72,432]{2,1,0:T(8,128)(2,1)}), bf16[16,72,432]{2,1,0:T(8,128)(2,1)}, u32[]{:S(2)}, u32[]{:S(2)}) async-start(bf16[16,72,432]{2,1,0:T(8,128)(2,1)} %bitcast.24), calls=%async_computation.5 | async-start | bytes 2359296 | tf_op jit(solution)/shard_map/all_to_all | solution.py:394
  174.6 0.1 dynamic-slice_bitcast_fusion
  174.7 0.1 copy.36.gain_ref
  174.8 1.1 constant_dynamic-slice_fusion.weight_ref
  175.9 2.5 %copy.37 = bf16[1,512,1152]{2,1,0:T(8,128)(2,1)} copy(bf16[1,512,1152]{1,2,0:T(8,128)(2,1)} %bitcast.52) | data formatting | bytes 2359296
  178.4 3.0 %norm_back.1 = bf16[4,128,1152]{2,1,0:T(8,128)(2,1)} custom-call(s32[4]{0:T(128)S(1)} %copy-done.6, bf16[4,128,1152]{2,1,0:T(8,128)(2,1)S(1)} %bitcast.49, bf16[4,128,1152]{2,1,0:T(8,128)(2,1)S(1)} %bitcast.48, f32[1152]{0:T(1024)S(1)} %copy-done.1), custom_call_target="tpu_custom_call" | custom-call | flops 4718592 | bytes 4718592 | tf_op jit(solution)/shard_map/norm_back/pallas_call | solution.py:272
  181.4 9.6 %all-to-all-done.4 = bf16[16,72,432]{2,1,0:T(8,128)(2,1)} async-done(((bf16[16,72,432]{2,1,0:T(8,128)(2,1)}), bf16[16,72,432]{2,1,0:T(8,128)(2,1)}, u32[]{:S(2)}, u32[]{:S(2)}) %all-to-all-start.4) | async-done | bytes 995360 | tf_op jit(solution)/shard_map/all_to_all | solution.py:394
  191.1 1.5 reduce_sum.28
  192.5 16.6 %all-gather = bf16[576,432]{1,0:T(8,128)(2,1)S(1)} all-gather(bf16[72,432]{1,0:T(8,128)(2,1)S(1)} %reduce_sum.28), channel_id=2, replica_groups=mesh['y'=4,'core'=2,'z'=4,'x'=4] {'y','core'}, dimensions={0}, use_global_device_ids=true | all-gather | bytes 559872 | tf_op jit(solution)/shard_map/all_gather | solution.py:396
  209.2 1.6 assemble.1
  210.8 0.6 reduce.2
  (29 shorter events, 0.1 us)
Async XLA Ops:
  13.1 8.6 %copy-start.7 = (bf16[1,512,1152]{2,1,0:T(8,128)(2,1)S(1)}, bf16[1,512,1152]{2,1,0:T(8,128)(2,1)}, u32[]{:S(2)}) copy-start(bf16[1,512,1152]{2,1,0:T(8,128)(2,1)} %param.11) | copy-start | bytes 3538948
  13.1 26.1 %all-to-all-start = ((bf16[16,32,1152]{2,1,0:T(8,128)(2,1)}), bf16[16,32,1152]{2,1,0:T(8,128)(2,1)S(1)}, u32[]{:S(2)}, u32[]{:S(2)}) async-start(bf16[16,32,1152]{2,1,0:T(8,128)(2,1)} %bitcast.53), calls=%async_computation | async-start | bytes 2359296 | tf_op jit(solution)/shard_map/all_to_all | solution.py:345
  21.7 17.5 %copy-start.5 = (s32[16]{0:T(128)S(1)}, s32[16]{0:T(128)}, u32[]{:S(2)}) copy-start(s32[16]{0:T(128)} %get-tuple-element.16.index_ref) | copy-start | bytes 196
  40.8 26.3 %all-to-all-start.1 = ((bf16[16,32,1152]{2,1,0:T(8,128)(2,1)}), bf16[16,32,1152]{2,1,0:T(8,128)(2,1)S(1)}, u32[]{:S(2)}, u32[]{:S(2)}) async-start(bf16[16,32,1152]{2,1,0:T(8,128)(2,1)} %pick_blocks.4), calls=%async_computation.1 | async-start | bytes 2359296 | tf_op jit(solution)/shard_map/all_to_all | solution.py:345
  45.8 5.5 %copy-start.9 = (s32[1,128]{1,0:T(1,128)S(1)}, s32[1,128]{1,0:T(1,128)}, u32[]{:S(2)}) copy-start(s32[1,128]{1,0:T(1,128)} %param.7) | copy-start | bytes 1540
  45.8 119.5 %reduce-scatter.2.cloned.1.call-start = ((), (), s32[]{:S(2)}) async-start(), calls=%async_computation.6 | async-start | bytes 8957952 | tf_op jit(solution)/shard_map/reduce_scatter | solution.py:379
  46.6 20.5 %copy-start.4 = (s32[4]{0:T(128)S(1)}, s32[4]{0:T(128)}, u32[]{:S(2)}) copy-start(s32[4]{0:T(128)} %get-tuple-element.15.index_ref) | copy-start | bytes 52
  46.6 17.3 %collective-permute-start.2 = (bf16[128,1152]{0,1:T(8,128)(2,1)}, bf16[128,1152]{0,1:T(8,128)(2,1)S(1)}, u32[]{:S(2)}, u32[]{:S(2)}) collective-permute-start(bf16[128,1152]{0,1:T(8,128)(2,1)} %get-tuple-element.38), channel_id=1, source_target_pairs={{0,1},{1,2},{2,3},{3,4},{4,5},{5,6},{6,7},{7,8},{8,9},{9,10},{10,1... | collective-permute-start | bytes 884744 | tf_op jit(solution)/shard_map/ppermute | solution.py:351
  50.0 16.0 %collective-permute-start.3 = (bf16[128,1152]{0,1:T(8,128)(2,1)S(1)}, bf16[128,1152]{0,1:T(8,128)(2,1)}, u32[]{:S(2)}, u32[]{:S(2)}) collective-permute-start(bf16[128,1152]{0,1:T(8,128)(2,1)S(1)} %get-tuple-element.39), channel_id=1, source_target_pairs={{1,0},{2,1},{3,2},{4,3},{5,4},{6,5},{7,6},{8,7},{9,8},{10,9},{11,1... | collective-permute-start | bytes 884744 | tf_op jit(solution)/shard_map/ppermute | solution.py:352
  63.9 0.7 copy-start.8
  67.8 16.6 %slice-start = ((s8[7962624]{0:T(1024)(128)(4,1)}), s8[4194304]{0:T(1024)(128)(4,1)S(1)}, s32[]{:S(2)}) async-start(s8[7962624]{0:T(1024)(128)(4,1)} %bitcast.56), calls=%async_computation.7 | async-start | bytes 8388608
  67.9 16.5 %collective-permute-start = (bf16[128,1152]{1,0:T(8,128)(2,1)S(1)}, bf16[128,1152]{1,0:T(8,128)(2,1)S(1)}, u32[]{:S(2)}, u32[]{:S(2)}) collective-permute-start(bf16[128,1152]{1,0:T(8,128)(2,1)S(1)} %get-tuple-element.40), channel_id=1, source_target_pairs={{0,1},{1,2},{2,3},{3,4},{4,5},{5,6},{6,7},{7,8},{8,9},{9,10},{10,1... | collective-permute-start | bytes 884744 | tf_op jit(solution)/shard_map/ppermute | solution.py:351
  72.6 11.7 %collective-permute-start.1 = (bf16[128,1152]{1,0:T(8,128)(2,1)S(1)}, bf16[128,1152]{1,0:T(8,128)(2,1)S(1)}, u32[]{:S(2)}, u32[]{:S(2)}) collective-permute-start(bf16[128,1152]{1,0:T(8,128)(2,1)S(1)} %get-tuple-element.41), channel_id=1, source_target_pairs={{1,0},{2,1},{3,2},{4,3},{5,4},{6,5},{7,6},{8,7},{9,8},{10,9},{11,1... | collective-permute-start | bytes 884744 | tf_op jit(solution)/shard_map/ppermute | solution.py:352
  74.1 10.3 %slice-start.1 = ((s8[7962624]{0:T(1024)(128)(4,1)}), s8[3768320]{0:T(1024)(128)(4,1)S(1)}, s32[]{:S(2)}) async-start(s8[7962624]{0:T(1024)(128)(4,1)} %bitcast.56), calls=%async_computation.8 | async-start | bytes 7536640
  110.9 2.0 copy-start.10
  112.9 7.5 %copy-start.3 = (s32[4]{0:T(128)S(1)}, s32[4]{0:T(128)}, u32[]{:S(2)}) copy-start(s32[4]{0:T(128)} %get-tuple-element.21.index_ref) | copy-start | bytes 52
  121.0 25.9 %copy-start.2 = (s32[16]{0:T(128)S(1)}, s32[16]{0:T(128)}, u32[]{:S(2)}) copy-start(s32[16]{0:T(128)} %get-tuple-element.20.index_ref) | copy-start | bytes 196
  148.6 19.8 %all-to-all-start.3 = ((bf16[16,32,1152]{2,1,0:T(8,128)(2,1)}), bf16[16,32,1152]{2,1,0:T(8,128)(2,1)S(1)}, u32[]{:S(2)}, u32[]{:S(2)}) async-start(bf16[16,32,1152]{2,1,0:T(8,128)(2,1)} %pick_blocks.7), calls=%async_computation.3 | async-start | bytes 2359296 | tf_op jit(solution)/shard_map/all_to_all | solution.py:345
  168.4 6.2 %copy-start.1 = (f32[1152]{0:T(1024)S(1)}, f32[1152]{0:T(1024)}, u32[]{:S(2)}) copy-start(f32[1152]{0:T(1024)} %gain_ref.3) | copy-start | bytes 13828
  168.4 22.7 %all-to-all-start.4 = ((bf16[16,72,432]{2,1,0:T(8,128)(2,1)}), bf16[16,72,432]{2,1,0:T(8,128)(2,1)}, u32[]{:S(2)}, u32[]{:S(2)}) async-start(bf16[16,72,432]{2,1,0:T(8,128)(2,1)} %bitcast.24), calls=%async_computation.5 | async-start | bytes 2359296 | tf_op jit(solution)/shard_map/all_to_all | solution.py:394
  175.9 2.5 %copy-start = (bf16[1,512,1152]{2,1,0:T(8,128)(2,1)S(1)}, bf16[1,512,1152]{2,1,0:T(8,128)(2,1)}, u32[]{:S(2)}) copy-start(bf16[1,512,1152]{2,1,0:T(8,128)(2,1)} %param.6) | copy-start | bytes 3538948
  175.9 2.5 %copy-start.6 = (s32[4]{0:T(128)S(1)}, s32[4]{0:T(128)}, u32[]{:S(2)}) copy-start(s32[4]{0:T(128)} %get-tuple-element.19.index_ref) | copy-start | bytes 52
Sparse Core Ops, SparseCore 0:
  111.1 54.2 reduce-scatter.1
